TPU v7x, 256 devices: a whole 4x4x8 slice. The times are simulated.
256 devices in a mesh: outer: 8 (over z), inner: 32 (over y, x, core).
Axes of the slice: x: 4, y: 4, z: 8, core: 2. Of those that a mesh axis runs over, the one named last changes fastest.
Arguments:
- context: bfloat16 [32768, 4096], P(('outer', 'inner')), may hold values from -5 to 5
- query_acts: bfloat16 [64, 4096], replicated, may hold values from -5 to 5
- norm_gain: float32 [4096], replicated, may hold values from 0.25 to 1.75
- w_query: bfloat16 [4096, 2048], P('inner'), may hold values from -0.078125 to 0.078125
- w_key: bfloat16 [4096, 512], P('inner'), may hold values from -0.453125 to 0.453125
- value_weight: bfloat16 [4096, 512], P('inner'), may hold values from -0.09375 to 0.09375
- lengths: int32 [256], replicated, may hold values from 64 to 128, as said below
Outputs:
- block_out: bfloat16 [32768, 2048], P(('outer', 'inner'))
- query_out: bfloat16 [64, 2048], replicated
Inputs may be any that keep to these rules, and one draw needn't show every extreme that they name: `lengths`: valid tokens of a block are its first ones; the rest of it is padding.
All inputs are finite; a program needn't handle non-finite values.
Results may differ from a plain program's by a relative error of at most 0.004.
The roundings to bfloat16 on the way count: a program that leaves them out, or rounds other values in their place, can miss the bound.
Values may be sent and summed in bfloat16 or wider, within the bound.
No kernel may reach another device: no remote copies, remote signals or barrier semaphores. Data moves between devices by JAX's collectives and lax.ppermute only.
A program may use at most 320 MiB of HBM per device.

v0:
```python
import jax
import jax.numpy as jnp
from jax import lax
from jax.sharding import PartitionSpec as P

QUERY_HEADS = 16
KEY_VALUE_HEADS = 4
HEAD_SIZE = 128


epsilon = 1e-05


def broadcast(block, axis, owner):
    block = jnp.where(lax.axis_index(axis) == owner, block, jnp.zeros_like(block))
    return lax.psum(block, axis)


def normalize(matrix, norm_gain):
    widened = matrix.astype(jnp.float32)
    factor = lax.rsqrt(jnp.mean(widened * widened, axis=-1, keepdims=True) + epsilon)
    return (widened * factor * norm_gain).astype(jnp.bfloat16)


def attend_part(query_rows, key_row_block, value_matrix, allowed):
    count_of_rows = query_rows.shape[0]
    head_groups = query_rows.reshape(
        count_of_rows, KEY_VALUE_HEADS, QUERY_HEADS // KEY_VALUE_HEADS, HEAD_SIZE
    )
    per_head_keys = key_row_block.reshape(key_row_block.shape[0], KEY_VALUE_HEADS, HEAD_SIZE)
    per_head_values = value_matrix.reshape(value_matrix.shape[0], KEY_VALUE_HEADS, HEAD_SIZE)
    scores = jnp.einsum(
        "rhgd,khd->hgrk", head_groups, per_head_keys, preferred_element_type=jnp.float32
    ) * HEAD_SIZE ** (-0.5)
    scores = jnp.where(allowed, scores, -jnp.inf)
    maxima = jnp.max(scores, axis=-1)
    weights = jnp.exp(scores - maxima[..., None])
    sum_exp = jnp.sum(weights, axis=-1)
    numerator = jnp.einsum(
        "hgrk,khd->rhgd",
        weights.astype(jnp.bfloat16),
        per_head_values,
        preferred_element_type=jnp.float32,
    )
    return (
        maxima.reshape(QUERY_HEADS, count_of_rows),
        sum_exp.reshape(QUERY_HEADS, count_of_rows),
        numerator.reshape(count_of_rows, QUERY_HEADS * HEAD_SIZE),
    )


def spread(factor):
    return jnp.repeat(factor.T, HEAD_SIZE, axis=1)


def combine(former, latter):
    maxima = jnp.maximum(former[0], latter[0])
    scale_one = jnp.exp(former[0] - maxima)
    scale_two = jnp.exp(latter[0] - maxima)
    return (
        maxima,
        former[1] * scale_one + latter[1] * scale_two,
        former[2] * spread(scale_one) + latter[2] * spread(scale_two),
    )


def finish(pieces):
    return (pieces[2] / spread(pieces[1])).astype(jnp.bfloat16)


def share_anchor(stacked):
    return broadcast(stacked, ("outer", "inner"), 0)


def per_device(context, query_acts, norm_gain, w_query, w_key, value_weight, lengths):
    block_rows = context.shape[0]
    normed = jnp.concatenate(
        [normalize(context, norm_gain), normalize(query_acts, norm_gain)], axis=0
    )

    def apply_weight(whole_weight):
        return jnp.dot(normed, whole_weight, preferred_element_type=jnp.float32).astype(
            jnp.bfloat16
        )

    whole_q, whole_k, whole_v = (
        lax.all_gather(w_query, "inner", axis=0, tiled=True),
        lax.all_gather(w_key, "inner", axis=0, tiled=True),
        lax.all_gather(value_weight, "inner", axis=0, tiled=True),
    )
    projected_k = apply_weight(whole_k)
    projected_v = apply_weight(whole_v)
    anchor = share_anchor(jnp.stack([projected_k[:block_rows], projected_v[:block_rows]]))
    projected_q = apply_weight(whole_q)
    position = lax.axis_index(("outer", "inner"))
    own_length = lengths[position]
    anchor_length = lengths[0]
    places = jnp.arange(block_rows, dtype=jnp.int32)
    causal = places[:, None] >= places[None, :]
    block_q = projected_q[:block_rows]
    block_k = projected_k[:block_rows]
    block_v = projected_v[:block_rows]
    query_q = projected_q[block_rows:]
    query_k = projected_k[block_rows:]
    query_v = projected_v[block_rows:]
    query_count = query_q.shape[0]
    own_allowed = causal & (places[None, :] < own_length)
    anchor_allowed = jnp.broadcast_to(
        (places[None, :] < anchor_length) & (position > 0), (block_rows, block_rows)
    )
    allowed = jnp.concatenate([anchor_allowed, own_allowed], axis=1)
    key_row_block = jnp.concatenate([anchor[0], block_k], axis=0)
    value_rows = jnp.concatenate([anchor[1], block_v], axis=0)
    block_out = finish(attend_part(block_q, key_row_block, value_rows, allowed))
    reached = jnp.broadcast_to(places[None, :] < own_length, (query_count, block_rows))
    block_part = attend_part(query_q, block_k, block_v, reached)
    highest = lax.pmax(block_part[0], ("outer", "inner"))
    rescale = jnp.exp(block_part[0] - highest)
    summed_parts = lax.psum(
        (block_part[1] * rescale, block_part[2] * spread(rescale)), ("outer", "inner")
    )
    merged = (highest, summed_parts[0], summed_parts[1])
    query_places = jnp.arange(query_count, dtype=jnp.int32)
    self_part = attend_part(
        query_q, query_k, query_v, query_places[:, None] >= query_places[None, :]
    )
    return (block_out, finish(combine(merged, self_part)))


def solution(mesh):
    in_specs = (
        P(("outer", "inner"), None),
        P(),
        P(),
        P("inner", None),
        P("inner", None),
        P("inner", None),
        P(),
    )
    out_specs = (P(("outer", "inner"), None), P())
    return jax.shard_map(
        per_device, mesh=mesh, in_specs=in_specs, out_specs=out_specs, check_vma=False
    )
```

profile of v0, /device:TPU:1, one launch (start us, length us, event | category | flops | bytes accessed | tf_op | source)
XLA Modules:
  0.0 875.3 jit_solution(4082930749184454192)
XLA Ops:
  7.2 0.7 all-gather.4.cloned.1.call-update
  8.0 0.7 all-gather.6.cloned.1.call-update
  8.7 1.2 fusion.9
  10.0 1.5 fusion
  11.5 0.9 fusion.11
  12.8 53.1 %all-gather.4.cloned.1.call-done = bf16[4096,512]{1,0:T(8,128)(2,1)} async-done(((bf16[128,512]{1,0:T(8,128)(2,1)}), bf16[4096,512]{1,0:T(8,128)(2,1)}) %all-gather.4.cloned.1.call-update) | async-done | bytes 4194320 | tf_op jit(solution)/shard_map/all_gather | solution.py:88
  65.9 3.2 convolution_convert_fusion.2
  69.2 49.9 %all-gather.6.cloned.1.call-done = bf16[4096,512]{1,0:T(8,128)(2,1)} async-done(((bf16[128,512]{1,0:T(8,128)(2,1)}), bf16[4096,512]{1,0:T(8,128)(2,1)}) %all-gather.6.cloned.1.call-update) | async-done | bytes 4194320 | tf_op jit(solution)/shard_map/all_gather | solution.py:89
  119.0 3.2 convolution_convert_fusion.1
  122.2 0.7 maximum_select_fusion
  123.1 0.5 all-gather.8.cloned.1.call-update
  123.6 0.6 fusion.52
  124.2 0.6 compare_and_fusion
  124.8 0.6 iota_compare_fusion.2
  125.7 0.8 copy.28
  126.5 0.7 concatenate.28
  127.2 0.6 reshape.106
  127.8 0.6 reshape.109
  128.5 244.5 %all-reduce.3.cloned.1.call-done = bf16[2,128,512]{2,1,0:T(8,128)(2,1)} async-done(((bf16[2,128,512]{2,1,0:T(8,128)(2,1)}), bf16[2,128,512]{2,1,0:T(8,128)(2,1)}) %all-reduce.3.cloned.1.call-update) | async-done | bytes 262160 | tf_op jit(solution)/shard_map/psum | solution.py:16
  373.0 1.0 fusion.49
  374.0 0.8 copy.56
  374.8 78.6 %all-gather.8.cloned.1.call-done = bf16[4096,2048]{1,0:T(8,128)(2,1)} async-done(((bf16[128,2048]{1,0:T(8,128)(2,1)}), bf16[4096,2048]{1,0:T(8,128)(2,1)}) %all-gather.8.cloned.1.call-update) | async-done | bytes 16777232 | tf_op jit(solution)/shard_map/all_gather | solution.py:87
  453.4 7.7 convolution_convert_fusion
  461.6 0.5 fusion.53
  462.5 0.5 fusion.12
  464.3 75.8 %pmax.7 = f32[16,64]{1,0:T(8,128)S(1)} all-reduce(f32[16,64]{1,0:T(8,128)S(1)} %bitcast.97), channel_id=1, replica_groups=mesh['outer'=8,'inner'=32] {'outer','inner'}, use_global_device_ids=true, to_apply=%region_6.7 | all-reduce | flops 1024 | bytes 8192 | tf_op jit(solution)/shard_map/pmax | solution.py:117
  540.2 0.4 fusion.19
  540.6 74.6 %psum.23 = f32[16,64]{1,0:T(8,128)S(1)} all-reduce(f32[16,64]{1,0:T(8,128)S(1)} %get-tuple-element.13), channel_id=1, replica_groups=mesh['outer'=8,'inner'=32] {'outer','inner'}, use_global_device_ids=true, to_apply=%region_10.11 | all-reduce | flops 1024 | bytes 8192 | tf_op jit(solution)/shard_map/psum | solution.py:119
  617.9 1.0 bitcast_multiply_fusion.2
  619.3 1.2 fusion.14
  620.5 245.4 %all-reduce.5.cloned.1.call-done = f32[64,2048]{1,0:T(8,128)} async-done(((f32[64,2048]{1,0:T(8,128)}), f32[64,2048]{1,0:T(8,128)}) %all-reduce.5.cloned.1.call-update) | async-done | bytes 524304 | tf_op jit(solution)/shard_map/psum | solution.py:119
  866.5 2.2 fusion.16
  (74 shorter events, 6.8 us)
Async XLA Ops:
  7.2 4.4 copy-start.1
  7.2 5.3 copy-start
  7.2 5.3 copy-start.10
  7.2 58.7 %all-gather.4.cloned.1.call-start = ((), (), s32[]{:S(2)}) async-start(), calls=%async_computation | async-start | bytes 4325376 | tf_op jit(solution)/shard_map/all_gather | solution.py:88
  7.9 111.1 %all-gather.6.cloned.1.call-start = ((), (), s32[]{:S(2)}) async-start(), calls=%async_computation.1 | async-start | bytes 4325376 | tf_op jit(solution)/shard_map/all_gather | solution.py:89
  8.7 364.3 %all-reduce.3.cloned.1.call-start = ((), (), s32[]{:S(2)}) async-start(), calls=%async_computation.2 | async-start | bytes 524288 | tf_op jit(solution)/shard_map/psum | solution.py:16
  12.5 106.6 %copy-start.3 = (bf16[64,4096]{1,0:T(8,128)(2,1)}, bf16[64,4096]{1,0:T(8,128)(2,1)S(1)}, u32[]{:S(2)}) copy-start(bf16[64,4096]{1,0:T(8,128)(2,1)S(1)} %fusion.11) | copy-start | bytes 1572868
  69.1 54.5 %copy-start.11 = (s32[256]{0:T(256)S(1)}, s32[256]{0:T(256)}, u32[]{:S(2)}) copy-start(s32[256]{0:T(256)} %param.13) | copy-start | bytes 3076
  122.2 331.2 %copy-start.4 = (bf16[64,4096]{1,0:T(8,128)(2,1)S(1)}, bf16[64,4096]{1,0:T(8,128)(2,1)}, u32[]{:S(2)}) copy-start(bf16[64,4096]{1,0:T(8,128)(2,1)} %copy-done.3) | copy-start | bytes 1572868
  123.0 330.4 %all-gather.8.cloned.1.call-start = ((), (), s32[]{:S(2)}) async-start(), calls=%async_computation.3 | async-start | bytes 17301504 | tf_op jit(solution)/shard_map/all_gather | solution.py:87
  123.6 742.3 %all-reduce.5.cloned.1.call-start = ((), (), s32[]{:S(2)}) async-start(), calls=%async_computation.4 | async-start | bytes 1048576 | tf_op jit(solution)/shard_map/psum | solution.py:119
  461.1 0.9 copy-start.2
  461.6 0.9 copy-start.5
  461.6 1.0 copy-start.6
  462.5 1.0 slice-start
  463.0 0.9 copy-start.9
  463.0 152.1 %copy-start.8 = (bf16[64,4,128]{2,1,0:T(4,128)(2,1)S(1)}, bf16[64,4,128]{2,1,0:T(4,128)(2,1)}, u32[]{:S(2)}) copy-start(bf16[64,4,128]{2,1,0:T(4,128)(2,1)} %reshape.106) | copy-start | bytes 196612
  463.4 152.4 %copy-start.7 = (bf16[64,4,128]{2,1,0:T(4,128)(2,1)S(1)}, bf16[64,4,128]{2,1,0:T(4,128)(2,1)}, u32[]{:S(2)}) copy-start(bf16[64,4,128]{2,1,0:T(4,128)(2,1)} %reshape.109) | copy-start | bytes 196612
Sparse Core Ops, SparseCore 0:
  10.6 55.2 all-gather.3
  68.5 50.5 all-gather.5
  125.1 247.8 all-reduce.2
  375.4 77.9 all-gather.7
  619.0 246.8 all-reduce.4
where the time goes:
time: 876 us; the launch traced here: 875 us
  waiting for transfers between devices  673 us (77%)
  blocking collectives  150 us (17%)
  matrix products  16.3 us (2%)
  between operations  14.2 us (2%)
  other arithmetic  11.4 us (1%)
  local copies, waits for them, and re-layouts  9.33 us (1%)
    psum x1, waiting for transfers between devices, per_device(): lax.psum((block_part[1] * rescale, block_part[2] * spread(rescale)), ('ou...  245 us
    psum x1, waiting for transfers between devices, broadcast(): return lax.psum(block, axis)  245 us
    all_gather x1, waiting for transfers between devices, per_device(): lax.all_gather(w_query, 'inner', axis=0, tiled=True)  78.6 us
    pmax x1, blocking collectives, per_device(): highest = lax.pmax(block_part[0], ('outer', 'inner'))  75.8 us
    psum x1, blocking collectives, per_device(): lax.psum((block_part[1] * rescale, block_part[2] * spread(rescale)), ('ou...  74.6 us
    all_gather x1, waiting for transfers between devices, per_device(): lax.all_gather(w_key, 'inner', axis=0, tiled=True)  53.1 us
    all_gather x1, waiting for transfers between devices, per_device(): lax.all_gather(value_weight, 'inner', axis=0, tiled=True)  49.9 us
  transfers between devices with their start and end apart: 5, of which 5 were waited for; matrix products, arithmetic and copies ran while one was open for 2% of the time, Pallas kernels for 0%

commit v1 on v0

v1 whole, which is shorter than its diff:
```python
import functools

import jax
import jax.numpy as jnp
from jax import lax
from jax.experimental import pallas as pl
from jax.experimental.pallas import tpu as pltpu
from jax.sharding import Mesh
from jax.sharding import PartitionSpec as P

HEAD_SIZE = 128
GROUP_HEADS = 4
BLK = 128
QTOK = 64
PAIRS = GROUP_HEADS * QTOK
CHIPS = 16
SHARE = PAIRS // CHIPS
ANCHOR_SHARE = BLK // CHIPS
SCALE = HEAD_SIZE ** (-0.5)
EPSILON = 1e-05
AXES = ("zg", "zi", "y", "x", "core")
PLANE = ("y", "x")
YXC = ("y", "x", "core")
OFFSETS = (0, -1, 1, 2)
bf16 = jnp.bfloat16
f32 = jnp.float32
VMEM = pl.BlockSpec(memory_space=pltpu.VMEM)
SMEM = pl.BlockSpec(memory_space=pltpu.SMEM)
SWAP = [(0, 1), (1, 0)]


def device_index(y, x, core):
    return (y * 4 + x) * 2 + core


def torus_pairs(step, first):
    pairs = []
    for y in range(4):
        for x in range(4):
            for core in range(2):
                along_x = (core == 0) == first
                to = (y, (x + step) % 4) if along_x else ((y + step) % 4, x)
                pairs.append((device_index(y, x, core), device_index(*to, core)))
    return pairs


def ring(piece, first):
    half = piece.shape[0] // 2
    send = lambda rows, step: lax.ppermute(rows, YXC, torus_pairs(step, first))
    before, after = send(piece, 1), send(piece, -1)
    return before, after, send(before[:half], 1), send(after[half:], -1)


def prepare_kernel(place, own, core_mate, z_mate, zc_mate, query, gain, *outs):
    y, x, core = place[0], place[1], place[2]
    step = 64
    for number, ref in enumerate((own, core_mate, z_mate, zc_mate, query)):
        for start in range(0, ref.shape[0], step):
            widened = ref[start : start + step, :].astype(f32)
            factor = lax.rsqrt(jnp.mean(widened * widened, axis=-1, keepdims=True) + EPSILON)
            rows = slice(number * BLK + start, number * BLK + start + step)
            for b in range(4):
                for a in range(4):
                    dx = jnp.where(core == 0, OFFSETS[a], OFFSETS[b])
                    dy = jnp.where(core == 0, OFFSETS[b], OFFSETS[a])
                    chip = ((y + dy) & 3) * 4 + ((x + dx) & 3)
                    cols = pl.ds(pl.multiple_of(chip * 256, 256), 256)
                    part = ref[start : start + step, cols].astype(f32) * factor * gain[:, cols]
                    outs[b][rows, a * 256 : (a + 1) * 256] = part.astype(bf16)


def query_kernel(place, lengths, proj, packed, anchor):
    position, origin = place[3], place[4]
    q = jnp.concatenate(
        [proj[4 * BLK :, HEAD_SIZE * g : HEAD_SIZE * (g + 1)] for g in range(GROUP_HEADS)], axis=0
    )
    k = proj[:, 512:640]
    v = proj[:, 640:768]
    scores = lax.dot_general(q, k, (((1,), (1,)), ((), ())), preferred_element_type=f32) * SCALE
    keys = 4 * BLK + QTOK
    col = lax.broadcasted_iota(jnp.int32, (PAIRS, keys), 1)
    row = lax.broadcasted_iota(jnp.int32, (PAIRS, keys), 0) & (QTOK - 1)
    allowed = (col >= 4 * BLK) & (col - 4 * BLK <= row) & (origin == 1)
    for j in range(4):
        length = lengths[position ^ ((j & 1) | ((j >> 1) << 5))]
        allowed = allowed | ((col >= j * BLK) & (col < j * BLK + length))
    scores = jnp.where(allowed, scores, -jnp.inf)
    peak = jnp.max(scores, axis=-1, keepdims=True)
    weights = jnp.exp(scores - peak)
    total = jnp.sum(weights, axis=-1, keepdims=True)
    numerator = jnp.dot(weights.astype(bf16), v, preferred_element_type=f32)
    lane = lax.broadcasted_iota(jnp.int32, (PAIRS, HEAD_SIZE), 1)
    stats = jnp.where(lane < 64, peak, total)
    head = place[5]
    start = pl.multiple_of(head * BLK, BLK)
    anchor_rows = proj[pl.ds(start, BLK), 512:768].astype(f32)
    for t in range(CHIPS):
        packed[t, :SHARE, :HEAD_SIZE] = numerator[t * SHARE : (t + 1) * SHARE]
        packed[t, :SHARE, HEAD_SIZE:] = stats[t * SHARE : (t + 1) * SHARE]
        packed[t, SHARE:, :] = anchor_rows[t * ANCHOR_SHARE : (t + 1) * ANCHOR_SHARE]


def merge(parts):
    peaks = [s[:, :1] for _, s in parts]
    top = functools.reduce(jnp.maximum, peaks)
    scales = [jnp.exp(p - top) for p in peaks]
    total = sum(s[:, 127:] * w for (_, s), w in zip(parts, scales))
    numerator = sum(n * w for (n, _), w in zip(parts, scales))
    return top, total, numerator


def merge_plane_kernel(parts, out):
    top, total, numerator = merge(
        [(parts[t, :SHARE, :HEAD_SIZE], parts[t, :SHARE, HEAD_SIZE:]) for t in range(CHIPS)]
    )
    lane = lax.broadcasted_iota(jnp.int32, (SHARE, HEAD_SIZE), 1)
    out[:SHARE, :HEAD_SIZE] = numerator
    out[:SHARE, HEAD_SIZE:] = jnp.where(lane < 64, top, total)
    out[SHARE:, :] = parts[0, SHARE:, :]


def merge_deep_kernel(place, own, before, after, across, out):
    refs = (own, before, after, across)
    _, total, numerator = merge([(r[:SHARE, :HEAD_SIZE], r[:SHARE, HEAD_SIZE:]) for r in refs])
    out[:SHARE, :] = numerator / total
    zg = place[6]
    anchor = own[SHARE:, :]
    for source, ref in ((1, before), (3, after), (2, across)):
        anchor = jnp.where(zg == source, ref[SHARE:, :], anchor)
    out[SHARE : SHARE + ANCHOR_SHARE, :] = anchor[:, :HEAD_SIZE]
    out[SHARE + ANCHOR_SHARE :, :] = anchor[:, HEAD_SIZE:]


def block_kernel(place, lengths, proj, shared, *outs):
    position = place[3]
    anchor_k = shared[:, SHARE : SHARE + ANCHOR_SHARE, :].reshape(BLK, HEAD_SIZE).astype(bf16)
    anchor_v = shared[:, SHARE + ANCHOR_SHARE :, :].reshape(BLK, HEAD_SIZE).astype(bf16)
    query_out = shared[:, :SHARE, :].reshape(PAIRS, HEAD_SIZE).astype(bf16)
    rows = GROUP_HEADS * BLK
    col = lax.broadcasted_iota(jnp.int32, (rows, 2 * BLK), 1)
    row = lax.broadcasted_iota(jnp.int32, (rows, 2 * BLK), 0) & (BLK - 1)
    for j in range(4):
        block = position ^ ((j & 1) | ((j >> 1) << 5))
        anchor_length = jnp.where(block > 0, lengths[0], 0)
        allowed = (col < anchor_length) | (
            (col >= BLK) & (col - BLK <= row) & (col - BLK < lengths[block])
        )
        here = slice(j * BLK, (j + 1) * BLK)
        q = jnp.concatenate(
            [proj[here, HEAD_SIZE * g : HEAD_SIZE * (g + 1)] for g in range(GROUP_HEADS)], axis=0
        )
        k = jnp.concatenate([anchor_k, proj[here, 512:640]], axis=0)
        v = jnp.concatenate([anchor_v, proj[here, 640:768]], axis=0)
        scores = lax.dot_general(q, k, (((1,), (1,)), ((), ())), preferred_element_type=f32) * SCALE
        scores = jnp.where(allowed, scores, -jnp.inf)
        peak = jnp.max(scores, axis=-1, keepdims=True)
        weights = jnp.exp(scores - peak)
        total = jnp.sum(weights, axis=-1, keepdims=True)
        numerator = jnp.dot(weights.astype(bf16), v, preferred_element_type=f32)
        result = (numerator / total).astype(bf16)
        for g in range(GROUP_HEADS):
            cols = slice(HEAD_SIZE * g, HEAD_SIZE * (g + 1))
            outs[j][:BLK, cols] = result[g * BLK : (g + 1) * BLK]
            outs[j][BLK:, cols] = query_out[g * QTOK : (g + 1) * QTOK]


def assemble_kernel(place, *refs):
    parts, block_out, query_out = refs[:4], refs[4], refs[5]
    for j in range(4):
        cols = pl.ds(pl.multiple_of((place[5] ^ j) * 512, 512), 512)
        block_out[:, cols] = parts[j][:BLK, :]
        query_out[:, cols] = parts[j][BLK:, :]


def shapes(*items):
    return tuple(jax.ShapeDtypeStruct(s, d) for s, d in items)


def call(kernel, out_shape, n_smem, n_vmem, flops=0, size=0):
    return pl.pallas_call(
        kernel,
        out_shape=out_shape,
        in_specs=[SMEM] * n_smem + [VMEM] * n_vmem,
        out_specs=jax.tree.map(lambda _: VMEM, out_shape),
        compiler_params=pltpu.CompilerParams(vmem_limit_bytes=40 << 20),
        cost_estimate=pl.CostEstimate(flops=flops, bytes_accessed=size, transcendentals=0),
    )


def per_device(context, query_acts, norm_gain, w_query, w_key, value_weight, lengths):
    zg, zi, y, x, core = (lax.axis_index(a).astype(jnp.int32) for a in AXES)
    head = zi * 2 + core
    position = ((zg * 2 + zi) * 16 + y * 4 + x) * 2 + core
    origin = ((zg == 0) & (y == 0) & (x == 0)).astype(jnp.int32)
    place = jnp.stack([y, x, core, position, origin, head, zg, zi])

    def columns(h):
        cut = lambda w, width: lax.dynamic_slice(w, (0, h * width), (w.shape[0], width))
        return jnp.concatenate([cut(w_query, 512), cut(w_key, 128), cut(value_weight, 128)], axis=1)

    mine = columns(head)
    theirs = lax.ppermute(columns(zi * 2 + 1 - core), "core", SWAP)
    flip = core == 1
    chip_rows = jnp.concatenate(
        [jnp.where(flip, theirs, mine), jnp.where(flip, mine, theirs)], axis=0
    )
    line = jnp.concatenate([chip_rows, *ring(chip_rows, True)], axis=0)
    w_before, w_after, w_top, w_bottom = ring(line, False)

    z_mate = lax.ppermute(context, "zi", SWAP)
    core_mate = lax.ppermute(context, "core", SWAP)
    zc_mate = lax.ppermute(z_mate, "core", SWAP)
    rows = 4 * BLK + QTOK
    x_own, x_before, x_after, x_across = call(
        prepare_kernel, shapes(*[((rows, 1024), bf16)] * 4), 1, 6, 1 << 24, 10 << 20
    )(place, context, core_mate, z_mate, zc_mate, query_acts, norm_gain[None])

    dot = functools.partial(jnp.dot, preferred_element_type=f32)
    total = dot(x_own, line) + dot(x_before, w_before) + dot(x_after, w_after)
    total = total + dot(x_across[:, :512], w_top) + dot(x_across[:, 512:], w_bottom)
    proj = total.astype(bf16)

    packed = call(
        lambda p, l, r, o: query_kernel(p, l, r, o, None),
        jax.ShapeDtypeStruct((CHIPS, SHARE + ANCHOR_SHARE, 256), f32), 2, 1, 1 << 27, 2 << 20,
    )(place, lengths, proj)
    gathered = lax.all_to_all(packed, PLANE, 0, 0, tiled=True)
    merged = call(
        merge_plane_kernel, jax.ShapeDtypeStruct((SHARE + ANCHOR_SHARE, 256), f32), 0, 1, 1 << 20, 1 << 19
    )(gathered)
    deep = lambda k: lax.ppermute(merged, "zg", [(i, (i + k) % 4) for i in range(4)])
    final = call(
        merge_deep_kernel,
        jax.ShapeDtypeStruct((SHARE + 2 * ANCHOR_SHARE, HEAD_SIZE), f32), 1, 4, 1 << 20, 1 << 17,
    )(place, merged, deep(1), deep(-1), deep(2)).astype(bf16)
    shared = lax.all_to_all(
        jnp.broadcast_to(final[None], (CHIPS, *final.shape)), PLANE, 0, 0, tiled=True
    )
    pieces = call(
        block_kernel, shapes(*[((BLK + QTOK, 512), bf16)] * 4), 2, 2, 1 << 29, 3 << 20
    )(place, lengths, proj, shared)
    received = (
        pieces[0],
        lax.ppermute(pieces[1], "core", SWAP),
        lax.ppermute(pieces[2], "zi", SWAP),
        lax.ppermute(pieces[3], ("zi", "core"), [(i, 3 - i) for i in range(4)]),
    )
    return call(
        assemble_kernel, shapes(((BLK, 2048), bf16), ((QTOK, 2048), bf16)), 1, 4, 0, 2 << 20
    )(place, *received)


def solution(mesh):
    grid = Mesh(mesh.devices.reshape(4, 2, 4, 4, 2), AXES)
    own_rows, width = P(AXES, None), P(YXC, None)
    return jax.shard_map(
        per_device,
        mesh=grid,
        in_specs=(own_rows, P(), P(), width, width, width, P()),
        out_specs=(own_rows, P()),
        check_vma=False,
    )
```

time: 876 us -> 123 us (0.14)
  waiting for transfers between devices: 673 us -> 34.3 us
  blocking collectives: 150 us -> 22 us
  starting transfers between devices: 0.19 us -> 38.3 us
  between operations: 14.2 us -> 0.82 us
  other arithmetic: 11.4 us -> 1.48 us
    psum x2 -> x0, waiting for transfers between devices: 490 us -> none  [the longest x1 245 us: per_device(): lax.psum((block_part[1] * rescale, block_part[2] * spread(rescale)), ('ou...]
    all_gather x3 -> x0, waiting for transfers between devices: 182 us -> none  [the longest x1 78.6 us: per_device(): lax.all_gather(w_query, 'inner', axis=0, tiled=True)]
    pmax x1 -> x0, blocking collectives: 75.8 us -> none  [per_device(): highest = lax.pmax(block_part[0], ('outer', 'inner'))]
    psum x1 -> x0, blocking collectives: 74.6 us -> none  [per_device(): lax.psum((block_part[1] * rescale, block_part[2] * spread(rescale)), ('ou...]
    ppermute x0 -> x18, starting transfers between devices: none -> 38.3 us  [the longest x8 9.59 us: ring(): send = lambda rows, step: lax.ppermute(rows, YXC, torus_pairs(step, first))]
    ppermute x0 -> x18, waiting for transfers between devices: none -> 34.3 us  [the longest x8 16.1 us: ring(): send = lambda rows, step: lax.ppermute(rows, YXC, torus_pairs(step, first))]
    all_to_all x0 -> x2, blocking collectives: none -> 22 us  [the longest x1 12.5 us: per_device(): gathered = lax.all_to_all(packed, PLANE, 0, 0, tiled=True)]
  transfers between devices with their start and end apart: 5 -> 18, of which waited for: 5 -> 12; matrix products, arithmetic and copies ran while one was open for 2% -> 11% of each run, Pallas kernels for 0% -> 3%
where the time goes in v1:
time: 123 us
  starting transfers between devices  38.3 us (31%)
  waiting for transfers between devices  34.3 us (28%)
  blocking collectives  22 us (18%)
  matrix products  8.88 us (7%)
  local copies, waits for them, and re-layouts  8.42 us (7%)
  Pallas kernels  8.31 us (7%)
  other arithmetic  1.48 us (1%)
    ppermute x8, waiting for transfers between devices, ring(): send = lambda rows, step: lax.ppermute(rows, YXC, torus_pairs(step, first))  16.1 us
    all_to_all x1, blocking collectives, per_device(): gathered = lax.all_to_all(packed, PLANE, 0, 0, tiled=True)  12.5 us
    ppermute x8, starting transfers between devices, ring(): send = lambda rows, step: lax.ppermute(rows, YXC, torus_pairs(step, first))  9.59 us
    all_to_all x1, blocking collectives, per_device(): lax.all_to_all(jnp.broadcast_to(final[None], (CHIPS, *final.shape)), PLAN...  9.47 us
    ppermute x3, starting transfers between devices, per_device(): lax.ppermute(merged, 'zg', [(i, (i + k) % 4) for i in range(4)])  9.33 us
    ppermute x1, starting transfers between devices, per_device(): lax.ppermute(pieces[1], 'core', SWAP)  8.7 us
    dot_general x3, matrix products, per_device(): total = dot(x_own, line) + dot(x_before, w_before) + dot(x_after, w_after)  7.48 us
    ppermute x1, waiting for transfers between devices, per_device(): lax.ppermute(pieces[2], 'zi', SWAP)  4.73 us
  transfers between devices with their start and end apart: 18, of which 12 were waited for; matrix products, arithmetic and copies ran while one was open for 11% of the time, Pallas kernels for 3%

profile of v1, /device:TPU:1, one launch (start us, length us, event | category | flops | bytes accessed | tf_op | source)
XLA Modules:
  0.0 122.5 jit_solution(4420630341204892618)
XLA Ops:
  2.6 3.3 %collective-permute-start.3 = (bf16[128,768]{1,0:T(8,128)(2,1)S(1)}, bf16[128,768]{1,0:T(8,128)(2,1)S(1)}, u32[]{:S(2)}, u32[]{:S(2)}) collective-permute-start(bf16[128,768]{1,0:T(8,128)(2,1)S(1)} %pad_maximum_fusion.1), channel_id=1, source_target_pairs={{0,1},{1,0},{2,3},{3,2},{4,5},{5,4},{6,7},{7,6},{8,9},{9,8},{10,11... | collective-permute-start | bytes 589832 | tf_op jit(solution)/shard_map/ppermute | solution.py:202
  10.0 1.2 collective-permute-start.1
  11.2 4.3 %collective-permute-done.5 = bf16[256,768]{1,0:T(8,128)(2,1)S(1)} collective-permute-done((bf16[256,768]{1,0:T(8,128)(2,1)S(1)}, bf16[256,768]{1,0:T(8,128)(2,1)S(1)}, u32[]{:S(2)}, u32[]{:S(2)}) %collective-permute-start.5) | collective-permute-done | bytes 393248 | tf_op jit(solution)/shard_map/ppermute | solution.py:49
  15.5 2.3 %collective-permute-start.7 = (bf16[128,768]{1,0:T(8,128)(2,1)S(1)}, bf16[128,768]{1,0:T(8,128)(2,1)S(1)}, u32[]{:S(2)}, u32[]{:S(2)}) collective-permute-start(bf16[128,768]{1,0:T(8,128)(2,1)S(1)} %slice.25), channel_id=1, source_target_pairs={{0,6},{1,25},{2,0},{3,27},{4,2},{5,29},{6,4},{7,31},{8,14},{9,1},{... | collective-permute-start | bytes 589832 | tf_op jit(solution)/shard_map/ppermute | solution.py:49
  19.5 4.4 %collective-permute-done.6 = bf16[128,768]{1,0:T(8,128)(2,1)S(1)} collective-permute-done((bf16[128,768]{1,0:T(8,128)(2,1)S(1)}, bf16[128,768]{1,0:T(8,128)(2,1)S(1)}, u32[]{:S(2)}, u32[]{:S(2)}) %collective-permute-start.6) | collective-permute-done | bytes 196640 | tf_op jit(solution)/shard_map/ppermute | solution.py:49
  25.9 2.1 %collective-permute-start.9 = (bf16[1024,768]{1,0:T(8,128)(2,1)}, bf16[1024,768]{1,0:T(8,128)(2,1)}, u32[]{:S(2)}, u32[]{:S(2)}) collective-permute-start(bf16[1024,768]{1,0:T(8,128)(2,1)} %constant_dynamic-update-slice_fusion), channel_id=1, source_target_pairs={{0,24},{1,7},{2,26},{3,1},{4,28},{5,3},{6,30},{7,5},{8,0},{9,15},{... | collective-permute-start | bytes 4718600 | tf_op jit(solution)/shard_map/ppermute | solution.py:49
  28.0 2.7 %collective-permute-start = (bf16[128,4096]{1,0:T(8,128)(2,1)S(1)}, bf16[128,4096]{1,0:T(8,128)(2,1)S(1)}, u32[]{:S(2)}, u32[]{:S(2)}) collective-permute-start(bf16[128,4096]{1,0:T(8,128)(2,1)S(1)} %copy-done), channel_id=1, source_target_pairs={{0,1},{1,0},{2,3},{3,2},{4,5},{5,4},{6,7},{7,6},{8,9},{9,8},{10,11... | collective-permute-start | bytes 3145736 | tf_op jit(solution)/shard_map/ppermute | solution.py:211
  30.6 3.2 %collective-permute-done.1.z_mate = bf16[128,4096]{1,0:T(8,128)(2,1)S(1)} collective-permute-done((bf16[128,4096]{1,0:T(8,128)(2,1)S(1)}, bf16[128,4096]{1,0:T(8,128)(2,1)S(1)}, u32[]{:S(2)}, u32[]{:S(2)}) %collective-permute-start.1) | collective-permute-done | bytes 1048608 | tf_op jit(solution)/shard_map/ppermute | solution.py:210
  33.8 1.7 %collective-permute-start.2 = (bf16[128,4096]{1,0:T(8,128)(2,1)S(1)}, bf16[128,4096]{1,0:T(8,128)(2,1)}, u32[]{:S(2)}, u32[]{:S(2)}) collective-permute-start(bf16[128,4096]{1,0:T(8,128)(2,1)S(1)} %collective-permute-done.1.z_mate), channel_id=1, source_target_pairs={{0,1},{1,0},{2,3},{3,2},{4,5},{5,4},{6,7},{7,6},{8,9},{9,8},{10,11... | collective-permute-start | bytes 3145736 | tf_op jit(solution)/shard_map/ppermute | solution.py:212
  35.7 2.3 %collective-permute-done.2.zc_mate = bf16[128,4096]{1,0:T(8,128)(2,1)} collective-permute-done((bf16[128,4096]{1,0:T(8,128)(2,1)S(1)}, bf16[128,4096]{1,0:T(8,128)(2,1)}, u32[]{:S(2)}, u32[]{:S(2)}) %collective-permute-start.2) | collective-permute-done | bytes 1048608 | tf_op jit(solution)/shard_map/ppermute | solution.py:212
  39.1 3.3 %shard_map.86 = (bf16[576,1024]{1,0:T(8,128)(2,1)S(1)}, bf16[576,1024]{1,0:T(8,128)(2,1)S(1)}, bf16[576,1024]{1,0:T(8,128)(2,1)S(1)}, bf16[576,1024]{1,0:T(8,128)(2,1)S(1)}) custom-call(s32[8]{0:T(128)S(1)} %stack.39.place.p, bf16[128,4096]{1,0:T(8,128)(2,1)S(1)} %copy-done, bf16[128,4096]{1,0:T(8,128)(2,1)S(1)} %collective-permute-done.core_mate, ...), custom_call_target="tpu_custom_call" | custom-call | flops 16777216 | bytes 10485760 | tf_op jit(solution)/shard_map/pallas_call | solution.py:214
  42.3 4.1 %collective-permute-done.8 = bf16[1024,768]{1,0:T(8,128)(2,1)} collective-permute-done((bf16[1024,768]{1,0:T(8,128)(2,1)}, bf16[1024,768]{1,0:T(8,128)(2,1)}, u32[]{:S(2)}, u32[]{:S(2)}) %collective-permute-start.8) | collective-permute-done | bytes 1572896 | tf_op jit(solution)/shard_map/ppermute | solution.py:49
  46.4 1.2 slice.26
  47.7 2.5 %fusion.6 = f32[576,768]{1,0:T(8,128)S(1)} fusion(bf16[576,1024]{1,0:T(8,128)(2,1)S(1)} %get-tuple-element.10, bf16[1024,768]{1,0:T(8,128)(2,1)} %constant_dynamic-update-slice_fusion), kind=kOutput, calls=%fused_computation.22 | convolution fusion | flops 905969664 | bytes 4521984 | tf_op jit(solution)/shard_map/dot_general | solution.py:219
  50.2 1.2 slice.27
  51.4 2.9 %collective-permute-start.11 = (bf16[512,768]{1,0:T(8,128)(2,1)S(1)}, bf16[512,768]{1,0:T(8,128)(2,1)S(1)}, u32[]{:S(2)}, u32[]{:S(2)}) collective-permute-start(bf16[512,768]{1,0:T(8,128)(2,1)S(1)} %slice.27), channel_id=1, source_target_pairs={{0,24},{1,7},{2,26},{3,1},{4,28},{5,3},{6,30},{7,5},{8,0},{9,15},{... | collective-permute-start | bytes 2359304 | tf_op jit(solution)/shard_map/ppermute | solution.py:49
  54.3 2.5 %fusion.8 = f32[576,768]{1,0:T(8,128)S(1)} fusion(bf16[576,1024]{1,0:T(8,128)(2,1)S(1)} %get-tuple-element.12, bf16[1024,768]{1,0:T(8,128)(2,1)} %collective-permute-done.9), kind=kOutput, calls=%fused_computation.24 | convolution fusion | flops 905969664 | bytes 4521984 | tf_op jit(solution)/shard_map/dot_general | solution.py:219
  56.8 2.5 %fusion.7 = f32[576,768]{1,0:T(8,128)S(1)} fusion(bf16[576,1024]{1,0:T(8,128)(2,1)S(1)} %get-tuple-element.11, bf16[1024,768]{1,0:T(8,128)(2,1)} %collective-permute-done.8), kind=kOutput, calls=%fused_computation.23 | convolution fusion | flops 905969664 | bytes 4521984 | tf_op jit(solution)/shard_map/dot_general | solution.py:219
  60.6 2.6 %collective-permute-done.11 = bf16[512,768]{1,0:T(8,128)(2,1)S(1)} collective-permute-done((bf16[512,768]{1,0:T(8,128)(2,1)S(1)}, bf16[512,768]{1,0:T(8,128)(2,1)S(1)}, u32[]{:S(2)}, u32[]{:S(2)}) %collective-permute-start.11) | collective-permute-done | bytes 786464 | tf_op jit(solution)/shard_map/ppermute | solution.py:49
  64.0 1.2 shard_map.87
  65.2 12.5 %all_to_all.10.parts = f32[16,24,256]{2,1,0:T(8,128)S(1)} all-to-all(f32[16,24,256]{2,1,0:T(8,128)S(1)} %shard_map.87), channel_id=1, replica_groups=mesh['zg'=4,'zi'=2,'y'=4,'x'=4,'core'=2] {'y','x'}, dimensions={0} | all-to-all | bytes 786432 | tf_op jit(solution)/shard_map/all_to_all | solution.py:227
  77.9 7.0 %collective-permute-start.14 = (f32[24,256]{1,0:T(8,128)S(1)}, f32[24,256]{1,0:T(8,128)S(1)}, u32[]{:S(2)}, u32[]{:S(2)}) collective-permute-start(f32[24,256]{1,0:T(8,128)S(1)} %shard_map.88.own), channel_id=1, source_target_pairs={{0,128},{64,192},{128,0},{192,64},{1,129},{65,193},{129,1},{193,65... | collective-permute-start | bytes 73736 | tf_op jit(solution)/shard_map/ppermute | solution.py:231
  84.9 2.4 %collective-permute-start.12 = (f32[24,256]{1,0:T(8,128)S(1)}, f32[24,256]{1,0:T(8,128)S(1)}, u32[]{:S(2)}, u32[]{:S(2)}) collective-permute-start(f32[24,256]{1,0:T(8,128)S(1)} %shard_map.88.own), channel_id=1, source_target_pairs={{0,64},{64,128},{128,192},{192,0},{1,65},{65,129},{129,193},{193,1... | collective-permute-start | bytes 73736 | tf_op jit(solution)/shard_map/ppermute | solution.py:231
  87.3 1.2 collective-permute-done.13.after
  88.5 1.3 %collective-permute-done.12.before = f32[24,256]{1,0:T(8,128)S(1)} collective-permute-done((f32[24,256]{1,0:T(8,128)S(1)}, f32[24,256]{1,0:T(8,128)S(1)}, u32[]{:S(2)}, u32[]{:S(2)}) %collective-permute-start.12) | collective-permute-done | bytes 24608 | tf_op jit(solution)/shard_map/ppermute | solution.py:231
  90.5 9.5 %all_to_all.11.shared = bf16[16,32,128]{2,1,0:T(8,128)(2,1)S(1)} all-to-all(bf16[16,32,128]{2,1,0:T(8,128)(2,1)S(1)} %broadcast_in_dim.10), channel_id=1, replica_groups=mesh['zg'=4,'zi'=2,'y'=4,'x'=4,'core'=2] {'y','x'}, dimensions={0} | all-to-all | bytes 262144 | tf_op jit(solution)/shard_map/all_to_all | solution.py:236
  100.0 1.5 %shard_map.90 = (bf16[192,512]{1,0:T(8,128)(2,1)S(1)}, bf16[192,512]{1,0:T(8,128)(2,1)S(1)}, bf16[192,512]{1,0:T(8,128)(2,1)S(1)}, bf16[192,512]{1,0:T(8,128)(2,1)S(1)}) custom-call(s32[8]{0:T(128)S(1)} %stack.39.place.p, s32[256]{0:T(256)S(1)} %copy-done.3, bf16[576,768]{1,0:T(8,128)(2,1)S(1)} %add_convert_fusion.r.proj, ...), custom_call_target="tpu_custom_call" | custom-call | flops 536870912 | bytes 3145728 | tf_op jit(solution)/shard_map/pallas_call | solution.py:239
  101.5 8.7 %collective-permute-start.15 = (bf16[192,512]{1,0:T(8,128)(2,1)S(1)}, bf16[192,512]{1,0:T(8,128)(2,1)S(1)}, u32[]{:S(2)}, u32[]{:S(2)}) collective-permute-start(bf16[192,512]{1,0:T(8,128)(2,1)S(1)} %get-tuple-element.15), channel_id=1, source_target_pairs={{0,1},{1,0},{2,3},{3,2},{4,5},{5,4},{6,7},{7,6},{8,9},{9,8},{10,11... | collective-permute-start | bytes 589832 | tf_op jit(solution)/shard_map/ppermute | solution.py:244
  110.2 1.4 %collective-permute-start.16 = (bf16[192,512]{1,0:T(8,128)(2,1)S(1)}, bf16[192,512]{1,0:T(8,128)(2,1)S(1)}, u32[]{:S(2)}, u32[]{:S(2)}) collective-permute-start(bf16[192,512]{1,0:T(8,128)(2,1)S(1)} %get-tuple-element.16), channel_id=1, source_target_pairs={{0,32},{32,0},{1,33},{33,1},{2,34},{34,2},{3,35},{35,3},{4,36},{36... | collective-permute-start | bytes 589832 | tf_op jit(solution)/shard_map/ppermute | solution.py:245
  111.9 4.7 %collective-permute-done.16.refs_2_ = bf16[192,512]{1,0:T(8,128)(2,1)S(1)} collective-permute-done((bf16[192,512]{1,0:T(8,128)(2,1)S(1)}, bf16[192,512]{1,0:T(8,128)(2,1)S(1)}, u32[]{:S(2)}, u32[]{:S(2)}) %collective-permute-start.16) | collective-permute-done | bytes 196640 | tf_op jit(solution)/shard_map/ppermute | solution.py:245
  116.7 4.4 %collective-permute-done.17.refs_3_ = bf16[192,512]{1,0:T(8,128)(2,1)S(1)} collective-permute-done((bf16[192,512]{1,0:T(8,128)(2,1)S(1)}, bf16[192,512]{1,0:T(8,128)(2,1)S(1)}, u32[]{:S(2)}, u32[]{:S(2)}) %collective-permute-start.17) | collective-permute-done | bytes 196640 | tf_op jit(solution)/shard_map/ppermute | solution.py:246
  121.1 1.5 %shard_map.91 = (bf16[128,2048]{1,0:T(8,128)(2,1)}, bf16[64,2048]{1,0:T(8,128)(2,1)}) custom-call(s32[8]{0:T(128)S(1)} %stack.39.place.p, bf16[192,512]{1,0:T(8,128)(2,1)S(1)} %get-tuple-element.14.refs_0_, bf16[192,512]{1,0:T(8,128)(2,1)S(1)} %collective-permute-done.15.refs_1_, bf16[192,512]{1,0:T(8,128)(2,1)S(1)} %collective-permute-done.16.refs_2_, ...), custom_call_target="tpu_custom_call" | custom-call | bytes 2097152 | tf_op jit(solution)/shard_map/pallas_call | solution.py:248
  (42 shorter events, 14.2 us)
Async XLA Ops:
  1.6 8.4 %copy-start = (bf16[128,4096]{1,0:T(8,128)(2,1)S(1)}, bf16[128,4096]{1,0:T(8,128)(2,1)}, u32[]{:S(2)}) copy-start(bf16[128,4096]{1,0:T(8,128)(2,1)} %own.1) | copy-start | bytes 3145732
  2.6 4.4 %collective-permute-start.3 = (bf16[128,768]{1,0:T(8,128)(2,1)S(1)}, bf16[128,768]{1,0:T(8,128)(2,1)S(1)}, u32[]{:S(2)}, u32[]{:S(2)}) collective-permute-start(bf16[128,768]{1,0:T(8,128)(2,1)S(1)} %pad_maximum_fusion.1), channel_id=1, source_target_pairs={{0,1},{1,0},{2,3},{3,2},{4,5},{5,4},{6,7},{7,6},{8,9},{9,8},{10,11... | collective-permute-start | bytes 589832 | tf_op jit(solution)/shard_map/ppermute | solution.py:202
  8.5 29.6 %copy-start.2 = (f32[4096]{0:T(1024)S(1)}, f32[4096]{0:T(1024)}, u32[]{:S(2)}) copy-start(f32[4096]{0:T(1024)} %param.9) | copy-start | bytes 49156
  8.5 7.0 %collective-permute-start.5 = (bf16[256,768]{1,0:T(8,128)(2,1)S(1)}, bf16[256,768]{1,0:T(8,128)(2,1)S(1)}, u32[]{:S(2)}, u32[]{:S(2)}) collective-permute-start(bf16[256,768]{1,0:T(8,128)(2,1)S(1)} %pad_maximum_fusion), channel_id=1, source_target_pairs={{0,6},{1,25},{2,0},{3,27},{4,2},{5,29},{6,4},{7,31},{8,14},{9,1},{... | collective-permute-start | bytes 1179656 | tf_op jit(solution)/shard_map/ppermute | solution.py:49
  9.5 8.2 %collective-permute-start.4 = (bf16[256,768]{1,0:T(8,128)(2,1)S(1)}, bf16[256,768]{1,0:T(8,128)(2,1)S(1)}, u32[]{:S(2)}, u32[]{:S(2)}) collective-permute-start(bf16[256,768]{1,0:T(8,128)(2,1)S(1)} %pad_maximum_fusion), channel_id=1, source_target_pairs={{0,2},{1,9},{2,4},{3,11},{4,6},{5,13},{6,0},{7,15},{8,10},{9,17},{... | collective-permute-start | bytes 1179656 | tf_op jit(solution)/shard_map/ppermute | solution.py:49
  10.0 23.8 %collective-permute-start.1 = (bf16[128,4096]{1,0:T(8,128)(2,1)S(1)}, bf16[128,4096]{1,0:T(8,128)(2,1)S(1)}, u32[]{:S(2)}, u32[]{:S(2)}) collective-permute-start(bf16[128,4096]{1,0:T(8,128)(2,1)S(1)} %copy-done), channel_id=1, source_target_pairs={{0,32},{32,0},{1,33},{33,1},{2,34},{34,2},{3,35},{35,3},{4,36},{36... | collective-permute-start | bytes 3145736 | tf_op jit(solution)/shard_map/ppermute | solution.py:210
  15.5 9.1 %collective-permute-start.7 = (bf16[128,768]{1,0:T(8,128)(2,1)S(1)}, bf16[128,768]{1,0:T(8,128)(2,1)S(1)}, u32[]{:S(2)}, u32[]{:S(2)}) collective-permute-start(bf16[128,768]{1,0:T(8,128)(2,1)S(1)} %slice.25), channel_id=1, source_target_pairs={{0,6},{1,25},{2,0},{3,27},{4,2},{5,29},{6,4},{7,31},{8,14},{9,1},{... | collective-permute-start | bytes 589832 | tf_op jit(solution)/shard_map/ppermute | solution.py:49
  17.8 6.1 %collective-permute-start.6 = (bf16[128,768]{1,0:T(8,128)(2,1)S(1)}, bf16[128,768]{1,0:T(8,128)(2,1)S(1)}, u32[]{:S(2)}, u32[]{:S(2)}) collective-permute-start(bf16[128,768]{1,0:T(8,128)(2,1)S(1)} %slice.24), channel_id=1, source_target_pairs={{0,2},{1,9},{2,4},{3,11},{4,6},{5,13},{6,0},{7,15},{8,10},{9,17},{... | collective-permute-start | bytes 589832 | tf_op jit(solution)/shard_map/ppermute | solution.py:49
  25.3 21.1 %collective-permute-start.8 = (bf16[1024,768]{1,0:T(8,128)(2,1)}, bf16[1024,768]{1,0:T(8,128)(2,1)}, u32[]{:S(2)}, u32[]{:S(2)}) collective-permute-start(bf16[1024,768]{1,0:T(8,128)(2,1)} %constant_dynamic-update-slice_fusion), channel_id=1, source_target_pairs={{0,8},{1,3},{2,10},{3,5},{4,12},{5,7},{6,14},{7,1},{8,16},{9,11},{... | collective-permute-start | bytes 4718600 | tf_op jit(solution)/shard_map/ppermute | solution.py:49
  25.9 24.2 %collective-permute-start.9 = (bf16[1024,768]{1,0:T(8,128)(2,1)}, bf16[1024,768]{1,0:T(8,128)(2,1)}, u32[]{:S(2)}, u32[]{:S(2)}) collective-permute-start(bf16[1024,768]{1,0:T(8,128)(2,1)} %constant_dynamic-update-slice_fusion), channel_id=1, source_target_pairs={{0,24},{1,7},{2,26},{3,1},{4,28},{5,3},{6,30},{7,5},{8,0},{9,15},{... | collective-permute-start | bytes 4718600 | tf_op jit(solution)/shard_map/ppermute | solution.py:49
  28.0 7.7 %collective-permute-start = (bf16[128,4096]{1,0:T(8,128)(2,1)S(1)}, bf16[128,4096]{1,0:T(8,128)(2,1)S(1)}, u32[]{:S(2)}, u32[]{:S(2)}) collective-permute-start(bf16[128,4096]{1,0:T(8,128)(2,1)S(1)} %copy-done), channel_id=1, source_target_pairs={{0,1},{1,0},{2,3},{3,2},{4,5},{5,4},{6,7},{7,6},{8,9},{9,8},{10,11... | collective-permute-start | bytes 3145736 | tf_op jit(solution)/shard_map/ppermute | solution.py:211
  33.8 4.2 %collective-permute-start.2 = (bf16[128,4096]{1,0:T(8,128)(2,1)S(1)}, bf16[128,4096]{1,0:T(8,128)(2,1)}, u32[]{:S(2)}, u32[]{:S(2)}) collective-permute-start(bf16[128,4096]{1,0:T(8,128)(2,1)S(1)} %collective-permute-done.1.z_mate), channel_id=1, source_target_pairs={{0,1},{1,0},{2,3},{3,2},{4,5},{5,4},{6,7},{7,6},{8,9},{9,8},{10,11... | collective-permute-start | bytes 3145736 | tf_op jit(solution)/shard_map/ppermute | solution.py:212
  38.0 1.0 copy-start.1
  47.6 12.4 %collective-permute-start.10 = (bf16[512,768]{1,0:T(8,128)(2,1)S(1)}, bf16[512,768]{1,0:T(8,128)(2,1)S(1)}, u32[]{:S(2)}, u32[]{:S(2)}) collective-permute-start(bf16[512,768]{1,0:T(8,128)(2,1)S(1)} %slice.26), channel_id=1, source_target_pairs={{0,8},{1,3},{2,10},{3,5},{4,12},{5,7},{6,14},{7,1},{8,16},{9,11},{... | collective-permute-start | bytes 2359304 | tf_op jit(solution)/shard_map/ppermute | solution.py:49
  51.4 11.9 %collective-permute-start.11 = (bf16[512,768]{1,0:T(8,128)(2,1)S(1)}, bf16[512,768]{1,0:T(8,128)(2,1)S(1)}, u32[]{:S(2)}, u32[]{:S(2)}) collective-permute-start(bf16[512,768]{1,0:T(8,128)(2,1)S(1)} %slice.27), channel_id=1, source_target_pairs={{0,24},{1,7},{2,26},{3,1},{4,28},{5,3},{6,30},{7,5},{8,0},{9,15},{... | collective-permute-start | bytes 2359304 | tf_op jit(solution)/shard_map/ppermute | solution.py:49
  60.6 3.4 %copy-start.3 = (s32[256]{0:T(256)S(1)}, s32[256]{0:T(256)}, u32[]{:S(2)}) copy-start(s32[256]{0:T(256)} %lengths.1) | copy-start | bytes 3076
  77.9 9.3 %collective-permute-start.14 = (f32[24,256]{1,0:T(8,128)S(1)}, f32[24,256]{1,0:T(8,128)S(1)}, u32[]{:S(2)}, u32[]{:S(2)}) collective-permute-start(f32[24,256]{1,0:T(8,128)S(1)} %shard_map.88.own), channel_id=1, source_target_pairs={{0,128},{64,192},{128,0},{192,64},{1,129},{65,193},{129,1},{193,65... | collective-permute-start | bytes 73736 | tf_op jit(solution)/shard_map/ppermute | solution.py:231
  84.9 3.6 %collective-permute-start.13 = (f32[24,256]{1,0:T(8,128)S(1)}, f32[24,256]{1,0:T(8,128)S(1)}, u32[]{:S(2)}, u32[]{:S(2)}) collective-permute-start(f32[24,256]{1,0:T(8,128)S(1)} %shard_map.88.own), channel_id=1, source_target_pairs={{0,192},{64,0},{128,64},{192,128},{1,193},{65,1},{129,65},{193,129... | collective-permute-start | bytes 73736 | tf_op jit(solution)/shard_map/ppermute | solution.py:231
  84.9 4.9 %collective-permute-start.12 = (f32[24,256]{1,0:T(8,128)S(1)}, f32[24,256]{1,0:T(8,128)S(1)}, u32[]{:S(2)}, u32[]{:S(2)}) collective-permute-start(f32[24,256]{1,0:T(8,128)S(1)} %shard_map.88.own), channel_id=1, source_target_pairs={{0,64},{64,128},{128,192},{192,0},{1,65},{65,129},{129,193},{193,1... | collective-permute-start | bytes 73736 | tf_op jit(solution)/shard_map/ppermute | solution.py:231
  101.5 10.4 %collective-permute-start.15 = (bf16[192,512]{1,0:T(8,128)(2,1)S(1)}, bf16[192,512]{1,0:T(8,128)(2,1)S(1)}, u32[]{:S(2)}, u32[]{:S(2)}) collective-permute-start(bf16[192,512]{1,0:T(8,128)(2,1)S(1)} %get-tuple-element.15), channel_id=1, source_target_pairs={{0,1},{1,0},{2,3},{3,2},{4,5},{5,4},{6,7},{7,6},{8,9},{9,8},{10,11... | collective-permute-start | bytes 589832 | tf_op jit(solution)/shard_map/ppermute | solution.py:244
  110.2 6.5 %collective-permute-start.16 = (bf16[192,512]{1,0:T(8,128)(2,1)S(1)}, bf16[192,512]{1,0:T(8,128)(2,1)S(1)}, u32[]{:S(2)}, u32[]{:S(2)}) collective-permute-start(bf16[192,512]{1,0:T(8,128)(2,1)S(1)} %get-tuple-element.16), channel_id=1, source_target_pairs={{0,32},{32,0},{1,33},{33,1},{2,34},{34,2},{3,35},{35,3},{4,36},{36... | collective-permute-start | bytes 589832 | tf_op jit(solution)/shard_map/ppermute | solution.py:245
  111.6 9.4 %collective-permute-start.17 = (bf16[192,512]{1,0:T(8,128)(2,1)S(1)}, bf16[192,512]{1,0:T(8,128)(2,1)S(1)}, u32[]{:S(2)}, u32[]{:S(2)}) collective-permute-start(bf16[192,512]{1,0:T(8,128)(2,1)S(1)} %get-tuple-element.17), channel_id=1, source_target_pairs={{0,33},{1,32},{32,1},{33,0},{2,35},{3,34},{34,3},{35,2},{4,37},{5,... | collective-permute-start | bytes 589832 | tf_op jit(solution)/shard_map/ppermute | solution.py:246

commit v2 on v1

--- a/solution.py
+++ b/solution.py
@@ -44,11 +44,24 @@
     return pairs
 
 
-def ring(piece, first):
-    half = piece.shape[0] // 2
-    send = lambda rows, step: lax.ppermute(rows, YXC, torus_pairs(step, first))
-    before, after = send(piece, 1), send(piece, -1)
-    return before, after, send(before[:half], 1), send(after[half:], -1)
+def send(rows, step, first):
+    return lax.ppermute(rows, YXC, torus_pairs(step, first))
+
+
+def join(top, bottom):
+    return jnp.concatenate([top, bottom], axis=0)
+
+
+def gather_weights(mine, theirs):
+    mate = lax.ppermute(theirs, "core", SWAP)
+    own = join(mine, mate)
+    before, after = send(own, 1, True), send(own, -1, True)
+    across = join(send(mine, 2, True), send(mate, -2, True))
+    near, far = join(own, before), join(after, across)
+    near_before, far_after = send(near, 1, False), send(far, -1, False)
+    far_before, near_after = send(far, 1, False), send(near, -1, False)
+    near_across, far_across = send(near_before, 1, False), send(far_after, -1, False)
+    return (near, far), (near_before, far_before), (near_after, far_after), (near_across, far_across)
 
 
 def prepare_kernel(place, own, core_mate, z_mate, zc_mate, query, gain, *outs):
@@ -64,35 +77,63 @@
                     dx = jnp.where(core == 0, OFFSETS[a], OFFSETS[b])
                     dy = jnp.where(core == 0, OFFSETS[b], OFFSETS[a])
                     chip = ((y + dy) & 3) * 4 + ((x + dx) & 3)
-                    cols = pl.ds(pl.multiple_of(chip * 256, 256), 256)
-                    part = ref[start : start + step, cols].astype(f32) * factor * gain[:, cols]
-                    outs[b][rows, a * 256 : (a + 1) * 256] = part.astype(bf16)
-
-
-def query_kernel(place, lengths, proj, packed, anchor):
+                    for h in range(2):
+                        source = chip * 2 + (core ^ h)
+                        cols = pl.ds(pl.multiple_of(source * 128, 128), 128)
+                        part = ref[start : start + step, cols].astype(f32) * factor * gain[:, cols]
+                        place_in = a * 256 + h * 128
+                        outs[b][rows, place_in : place_in + 128] = part.astype(bf16)
+
+
+def multiply(rows, parts, cols):
+    weights = jnp.concatenate([p[:, cols] for p in parts], axis=0)
+    return jnp.dot(rows[...], weights, preferred_element_type=f32)
+
+
+COLUMNS = [slice(n, n + 256) for n in range(0, 768, 256)]
+
+
+def project_kernel(own, before, after, *refs):
+    out = refs[-1]
+    for cols in COLUMNS:
+        total = multiply(own, refs[:2], cols) + multiply(before, refs[2:4], cols)
+        out[:, cols] = total + multiply(after, refs[4:6], cols)
+
+
+def query_kernel(place, lengths, across, total, near, far, proj, packed):
+    for cols in COLUMNS:
+        proj[:, cols] = (total[:, cols] + multiply(across, (near, far), cols)).astype(bf16)
     position, origin = place[3], place[4]
     q = jnp.concatenate(
         [proj[4 * BLK :, HEAD_SIZE * g : HEAD_SIZE * (g + 1)] for g in range(GROUP_HEADS)], axis=0
     )
-    k = proj[:, 512:640]
-    v = proj[:, 640:768]
-    scores = lax.dot_general(q, k, (((1,), (1,)), ((), ())), preferred_element_type=f32) * SCALE
-    keys = 4 * BLK + QTOK
-    col = lax.broadcasted_iota(jnp.int32, (PAIRS, keys), 1)
-    row = lax.broadcasted_iota(jnp.int32, (PAIRS, keys), 0) & (QTOK - 1)
-    allowed = (col >= 4 * BLK) & (col - 4 * BLK <= row) & (origin == 1)
-    for j in range(4):
-        length = lengths[position ^ ((j & 1) | ((j >> 1) << 5))]
-        allowed = allowed | ((col >= j * BLK) & (col < j * BLK + length))
-    scores = jnp.where(allowed, scores, -jnp.inf)
-    peak = jnp.max(scores, axis=-1, keepdims=True)
-    weights = jnp.exp(scores - peak)
-    total = jnp.sum(weights, axis=-1, keepdims=True)
-    numerator = jnp.dot(weights.astype(bf16), v, preferred_element_type=f32)
+    sets = []
+    for j in range(5):
+        keys = BLK if j < 4 else QTOK
+        here = slice(j * BLK, j * BLK + keys)
+        scores = lax.dot_general(
+            q, proj[here, 512:640], (((1,), (1,)), ((), ())), preferred_element_type=f32
+        ) * SCALE
+        col = lax.broadcasted_iota(jnp.int32, (PAIRS, keys), 1)
+        if j < 4:
+            allowed = col < lengths[position ^ ((j & 1) | ((j >> 1) << 5))]
+        else:
+            allowed = col <= (lax.broadcasted_iota(jnp.int32, (PAIRS, keys), 0) & (QTOK - 1))
+        scores = jnp.where(allowed, scores, -jnp.inf)
+        peak = jnp.max(scores, axis=-1, keepdims=True)
+        weights = jnp.exp(scores - peak)
+        sum_exp = jnp.sum(weights, axis=-1, keepdims=True)
+        numerator = jnp.dot(weights.astype(bf16), proj[here, 640:768], preferred_element_type=f32)
+        if j == 4:
+            peak = jnp.where(origin == 1, peak, -jnp.inf)
+        sets.append((peak, sum_exp, numerator))
+    peak = functools.reduce(jnp.maximum, [s[0] for s in sets])
+    scales = [jnp.exp(s[0] - peak) for s in sets]
+    total_exp = sum(s[1] * w for s, w in zip(sets, scales))
+    numerator = sum(s[2] * w for s, w in zip(sets, scales))
     lane = lax.broadcasted_iota(jnp.int32, (PAIRS, HEAD_SIZE), 1)
-    stats = jnp.where(lane < 64, peak, total)
-    head = place[5]
-    start = pl.multiple_of(head * BLK, BLK)
+    stats = jnp.where(lane < 64, peak, total_exp)
+    start = pl.multiple_of(place[5] * BLK, BLK)
     anchor_rows = proj[pl.ds(start, BLK), 512:768].astype(f32)
     for t in range(CHIPS):
         packed[t, :SHARE, :HEAD_SIZE] = numerator[t * SHARE : (t + 1) * SHARE]
@@ -198,32 +239,25 @@
         cut = lambda w, width: lax.dynamic_slice(w, (0, h * width), (w.shape[0], width))
         return jnp.concatenate([cut(w_query, 512), cut(w_key, 128), cut(value_weight, 128)], axis=1)
 
-    mine = columns(head)
-    theirs = lax.ppermute(columns(zi * 2 + 1 - core), "core", SWAP)
-    flip = core == 1
-    chip_rows = jnp.concatenate(
-        [jnp.where(flip, theirs, mine), jnp.where(flip, mine, theirs)], axis=0
-    )
-    line = jnp.concatenate([chip_rows, *ring(chip_rows, True)], axis=0)
-    w_before, w_after, w_top, w_bottom = ring(line, False)
+    theirs = columns(zi * 2 + 1 - core)
+    w_own, w_before, w_after, w_across = gather_weights(columns(head), theirs)
 
     z_mate = lax.ppermute(context, "zi", SWAP)
     core_mate = lax.ppermute(context, "core", SWAP)
+    z_mate, _ = lax.optimization_barrier((z_mate, w_own[1]))
     zc_mate = lax.ppermute(z_mate, "core", SWAP)
     rows = 4 * BLK + QTOK
     x_own, x_before, x_after, x_across = call(
         prepare_kernel, shapes(*[((rows, 1024), bf16)] * 4), 1, 6, 1 << 24, 10 << 20
     )(place, context, core_mate, z_mate, zc_mate, query_acts, norm_gain[None])
 
-    dot = functools.partial(jnp.dot, preferred_element_type=f32)
-    total = dot(x_own, line) + dot(x_before, w_before) + dot(x_after, w_after)
-    total = total + dot(x_across[:, :512], w_top) + dot(x_across[:, 512:], w_bottom)
-    proj = total.astype(bf16)
-
-    packed = call(
-        lambda p, l, r, o: query_kernel(p, l, r, o, None),
-        jax.ShapeDtypeStruct((CHIPS, SHARE + ANCHOR_SHARE, 256), f32), 2, 1, 1 << 27, 2 << 20,
-    )(place, lengths, proj)
+    total = call(
+        project_kernel, jax.ShapeDtypeStruct((rows, 768), f32), 0, 9, 27 << 27, 12 << 20
+    )(x_own, x_before, x_after, *w_own, *w_before, *w_after)
+    proj, packed = call(
+        query_kernel,
+        shapes(((rows, 768), bf16), ((CHIPS, SHARE + ANCHOR_SHARE, 256), f32)), 2, 4, 9 << 27, 6 << 20,
+    )(place, lengths, x_across, total, *w_across)
     gathered = lax.all_to_all(packed, PLANE, 0, 0, tiled=True)
     merged = call(
         merge_plane_kernel, jax.ShapeDtypeStruct((SHARE + ANCHOR_SHARE, 256), f32), 0, 1, 1 << 20, 1 << 19

time: 123 us -> 115 us (0.935)
  matrix products: 8.88 us -> 0 us
  Pallas kernels: 8.31 us -> 16.7 us
  waiting for transfers between devices: 34.3 us -> 27.9 us
  local copies, waits for them, and re-layouts: 8.42 us -> 5.22 us
  blocking collectives: 22 us -> 24.6 us
    ppermute x9 -> x11, waiting for transfers between devices: 17.1 us -> 8.11 us  [the longest x10 7.04 us: send(): return lax.ppermute(rows, YXC, torus_pairs(step, first))]
    dot_general x5 -> x0, matrix products: 8.88 us -> none  [the longest x3 7.48 us: per_device(): total = dot(x_own, line) + dot(x_before, w_before) + dot(x_after, w_after)]
    pallas_call x1 -> x2, Pallas kernels: 1.19 us -> 9.24 us  [the longest x1 5.23 us: per_device(): call(project_kernel, jax.ShapeDtypeStruct((rows, 768), f32), 0, 9, 27 <<...]
    ppermute x9 -> x11, starting transfers between devices: 12.9 us -> 18.4 us  [the longest x10 15.1 us: send(): return lax.ppermute(rows, YXC, torus_pairs(step, first))]
    ppermute x1, waiting for transfers between devices: 3.22 us -> 8.26 us  [per_device(): z_mate = lax.ppermute(context, 'zi', SWAP)]
    ppermute x1, starting transfers between devices: 8.7 us -> 5.61 us  [per_device(): lax.ppermute(pieces[1], 'core', SWAP)]
    all_to_all x1, blocking collectives: 12.5 us -> 15 us  [per_device(): gathered = lax.all_to_all(packed, PLANE, 0, 0, tiled=True)]
    slice x4 -> x0, local copies, waits for them, and re-layouts: 2.4 us -> none  [ring(): return (before, after, send(before[:half], 1), send(after[half:], -1))]
  transfers between devices with their start and end apart: 18 -> 20, of which waited for: 12 -> 8; matrix products, arithmetic and copies ran while one was open for 11% -> 3% of each run, Pallas kernels for 3% -> 8%
where the time goes in v2:
time: 115 us; the launch traced here: 114 us
  starting transfers between devices  38.1 us (33%)
  waiting for transfers between devices  27.9 us (24%)
  blocking collectives  24.6 us (21%)
  Pallas kernels  16.7 us (15%)
  local copies, waits for them, and re-layouts  5.22 us (5%)
    ppermute x10, starting transfers between devices, send(): return lax.ppermute(rows, YXC, torus_pairs(step, first))  15.1 us
    all_to_all x1, blocking collectives, per_device(): gathered = lax.all_to_all(packed, PLANE, 0, 0, tiled=True)  15 us
    all_to_all x1, blocking collectives, per_device(): lax.all_to_all(jnp.broadcast_to(final[None], (CHIPS, *final.shape)), PLAN...  9.59 us
    ppermute x3, starting transfers between devices, per_device(): lax.ppermute(merged, 'zg', [(i, (i + k) % 4) for i in range(4)])  9.11 us
    ppermute x1, waiting for transfers between devices, per_device(): z_mate = lax.ppermute(context, 'zi', SWAP)  8.26 us
    ppermute x10, waiting for transfers between devices, send(): return lax.ppermute(rows, YXC, torus_pairs(step, first))  7.04 us
    ppermute x1, starting transfers between devices, per_device(): lax.ppermute(pieces[1], 'core', SWAP)  5.61 us
    pallas_call x1, Pallas kernels, per_device(): call(project_kernel, jax.ShapeDtypeStruct((rows, 768), f32), 0, 9, 27 <<...  5.23 us
  transfers between devices with their start and end apart: 20, of which 8 were waited for; matrix products, arithmetic and copies ran while one was open for 3% of the time, Pallas kernels for 8%

profile of v2, /device:TPU:1, one launch (start us, length us, event | category | flops | bytes accessed | tf_op | source)
XLA Modules:
  0.0 114.4 jit_solution(6309394157370999127)
XLA Ops:
  0.7 1.1 constant_dynamic-slice_fusion.5
  2.6 3.3 %collective-permute-start.2 = (bf16[128,768]{1,0:T(8,128)(2,1)S(1)}, bf16[128,768]{1,0:T(8,128)(2,1)S(1)}, u32[]{:S(2)}, u32[]{:S(2)}) collective-permute-start(bf16[128,768]{1,0:T(8,128)(2,1)S(1)} %pad_maximum_fusion.3), channel_id=1, source_target_pairs={{0,1},{1,0},{2,3},{3,2},{4,5},{5,4},{6,7},{7,6},{8,9},{9,8},{10,11... | collective-permute-start | bytes 589832 | tf_op jit(solution)/shard_map/ppermute | solution.py:56
  5.9 1.1 collective-permute-done.2
  7.1 1.2 %collective-permute-start.1 = (bf16[128,4096]{1,0:T(8,128)(2,1)S(1)}, bf16[128,4096]{1,0:T(8,128)(2,1)S(1)}, u32[]{:S(2)}, u32[]{:S(2)}) collective-permute-start(bf16[128,4096]{1,0:T(8,128)(2,1)S(1)} %copy-done), channel_id=1, source_target_pairs={{0,32},{32,0},{1,33},{33,1},{2,34},{34,2},{3,35},{35,3},{4,36},{36... | collective-permute-start | bytes 3145736 | tf_op jit(solution)/shard_map/ppermute | solution.py:245
  8.3 1.5 %collective-permute-start.3 = (bf16[256,768]{1,0:T(8,128)(2,1)S(1)}, bf16[256,768]{1,0:T(8,128)(2,1)S(1)}, u32[]{:S(2)}, u32[]{:S(2)}) collective-permute-start(bf16[256,768]{1,0:T(8,128)(2,1)S(1)} %pad_maximum_fusion.1), channel_id=1, source_target_pairs={{0,6},{1,25},{2,0},{3,27},{4,2},{5,29},{6,4},{7,31},{8,14},{9,1},{... | collective-permute-start | bytes 1179656 | tf_op jit(solution)/shard_map/ppermute | solution.py:48
  9.8 1.0 collective-permute-start
  10.9 3.0 %collective-permute-start.4 = (bf16[128,768]{1,0:T(8,128)(2,1)S(1)}, bf16[128,768]{1,0:T(8,128)(2,1)S(1)}, u32[]{:S(2)}, u32[]{:S(2)}) collective-permute-start(bf16[128,768]{1,0:T(8,128)(2,1)S(1)} %pad_maximum_fusion.2), channel_id=1, source_target_pairs={{0,4},{1,17},{2,6},{3,19},{4,0},{5,21},{6,2},{7,23},{8,12},{9,25},... | collective-permute-start | bytes 589832 | tf_op jit(solution)/shard_map/ppermute | solution.py:48
  13.9 1.3 %collective-permute-done.7 = bf16[256,768]{1,0:T(8,128)(2,1)S(1)} collective-permute-done((bf16[256,768]{1,0:T(8,128)(2,1)S(1)}, bf16[256,768]{1,0:T(8,128)(2,1)S(1)}, u32[]{:S(2)}, u32[]{:S(2)}) %collective-permute-start.7) | collective-permute-done | bytes 393248 | tf_op jit(solution)/shard_map/ppermute | solution.py:48
  16.2 3.8 %collective-permute-start.8 = (bf16[512,768]{1,0:T(8,128)(2,1)}, bf16[512,768]{1,0:T(8,128)(2,1)}, u32[]{:S(2)}, u32[]{:S(2)}) collective-permute-start(bf16[512,768]{1,0:T(8,128)(2,1)} %pad_maximum_fusion.refs_0_), channel_id=1, source_target_pairs={{0,8},{1,3},{2,10},{3,5},{4,12},{5,7},{6,14},{7,1},{8,16},{9,11},{... | collective-permute-start | bytes 2359304 | tf_op jit(solution)/shard_map/ppermute | solution.py:48
  22.2 1.3 %collective-permute-start.11 = (bf16[512,768]{1,0:T(8,128)(2,1)}, bf16[512,768]{1,0:T(8,128)(2,1)}, u32[]{:S(2)}, u32[]{:S(2)}) collective-permute-start(bf16[512,768]{1,0:T(8,128)(2,1)} %constant_dynamic-update-slice_fusion.refs_1_), channel_id=1, source_target_pairs={{0,24},{1,7},{2,26},{3,1},{4,28},{5,3},{6,30},{7,5},{8,0},{9,15},{... | collective-permute-start | bytes 2359304 | tf_op jit(solution)/shard_map/ppermute | solution.py:48
  23.4 8.3 %collective-permute-done.1.z_mate = bf16[128,4096]{1,0:T(8,128)(2,1)S(1)} collective-permute-done((bf16[128,4096]{1,0:T(8,128)(2,1)S(1)}, bf16[128,4096]{1,0:T(8,128)(2,1)S(1)}, u32[]{:S(2)}, u32[]{:S(2)}) %collective-permute-start.1) | collective-permute-done | bytes 1048608 | tf_op jit(solution)/shard_map/ppermute | solution.py:245
  31.7 1.1 collective-permute-start.6
  33.6 1.8 %collective-permute-start.10 = (bf16[512,768]{1,0:T(8,128)(2,1)}, bf16[512,768]{1,0:T(8,128)(2,1)}, u32[]{:S(2)}, u32[]{:S(2)}) collective-permute-start(bf16[512,768]{1,0:T(8,128)(2,1)} %pad_maximum_fusion.refs_0_), channel_id=1, source_target_pairs={{0,24},{1,7},{2,26},{3,1},{4,28},{5,3},{6,30},{7,5},{8,0},{9,15},{... | collective-permute-start | bytes 2359304 | tf_op jit(solution)/shard_map/ppermute | solution.py:48
  35.5 2.7 %collective-permute-start.13 = (bf16[512,768]{1,0:T(8,128)(2,1)}, bf16[512,768]{1,0:T(8,128)(2,1)}, u32[]{:S(2)}, u32[]{:S(2)}) collective-permute-start(bf16[512,768]{1,0:T(8,128)(2,1)} %collective-permute-done.11.refs_5_), channel_id=1, source_target_pairs={{0,24},{1,7},{2,26},{3,1},{4,28},{5,3},{6,30},{7,5},{8,0},{9,15},{... | collective-permute-start | bytes 2359304 | tf_op jit(solution)/shard_map/ppermute | solution.py:48
  38.3 1.0 copy-done.1
  39.3 3.6 %shard_map.86 = (bf16[576,1024]{1,0:T(8,128)(2,1)S(1)}, bf16[576,1024]{1,0:T(8,128)(2,1)S(1)}, bf16[576,1024]{1,0:T(8,128)(2,1)S(1)}, bf16[576,1024]{1,0:T(8,128)(2,1)S(1)}) custom-call(s32[8]{0:T(128)S(1)} %stack.39.place, bf16[128,4096]{1,0:T(8,128)(2,1)S(1)} %copy-done, bf16[128,4096]{1,0:T(8,128)(2,1)S(1)} %collective-permute-done.core_mate, ...), custom_call_target="tpu_custom_call" | custom-call | flops 16777216 | bytes 10485760 | tf_op jit(solution)/shard_map/pallas_call | solution.py:250
  42.9 2.5 %collective-permute-done.9.refs_3_ = bf16[512,768]{1,0:T(8,128)(2,1)} collective-permute-done((bf16[512,768]{1,0:T(8,128)(2,1)}, bf16[512,768]{1,0:T(8,128)(2,1)}, u32[]{:S(2)}, u32[]{:S(2)}) %collective-permute-start.9) | collective-permute-done | bytes 786464 | tf_op jit(solution)/shard_map/ppermute | solution.py:48
  45.5 5.2 %shard_map.87.total = f32[576,768]{1,0:T(8,128)S(1)} custom-call(bf16[576,1024]{1,0:T(8,128)(2,1)S(1)} %get-tuple-element.15.own, bf16[576,1024]{1,0:T(8,128)(2,1)S(1)} %get-tuple-element.16.before, bf16[576,1024]{1,0:T(8,128)(2,1)S(1)} %get-tuple-element.17.after, bf16[512,768]{1,0:T(8,128)(2,1)} %pad_maximum_fusion.refs_0_, ...), custom_call_target="tpu_custom_call" | custom-call | flops 3623878656 | bytes 12582912 | tf_op jit(solution)/shard_map/pallas_call | solution.py:254
  50.7 3.2 %collective-permute-done.12.near = bf16[512,768]{1,0:T(8,128)(2,1)} collective-permute-done((bf16[512,768]{1,0:T(8,128)(2,1)}, bf16[512,768]{1,0:T(8,128)(2,1)}, u32[]{:S(2)}, u32[]{:S(2)}) %collective-permute-start.12) | collective-permute-done | bytes 786464 | tf_op jit(solution)/shard_map/ppermute | solution.py:48
  53.9 4.0 %shard_map.88 = (bf16[576,768]{1,0:T(8,128)(2,1)S(1)}, f32[16,24,256]{2,1,0:T(8,128)S(1)}) custom-call(s32[8]{0:T(128)S(1)} %stack.39.place, s32[256]{0:T(256)S(1)} %copy-done.3, bf16[576,1024]{1,0:T(8,128)(2,1)S(1)} %get-tuple-element.14.across, f32[576,768]{1,0:T(8,128)S(1)} %shard_map.87.total, bf16[512,768]{1,0:T(8,128)(2,1)} %collective-permute-done.12.near, ...), custom_call_target="tpu_custom_call" | custom-call | flops 1207959552 | bytes 6291456 | tf_op jit(solution)/shard_map/pallas_call | solution.py:257
  57.9 15.0 %all_to_all.10.parts = f32[16,24,256]{2,1,0:T(8,128)S(1)} all-to-all(f32[16,24,256]{2,1,0:T(8,128)S(1)} %get-tuple-element.19), channel_id=1, replica_groups=mesh['zg'=4,'zi'=2,'y'=4,'x'=4,'core'=2] {'y','x'}, dimensions={0} | all-to-all | bytes 786432 | tf_op jit(solution)/shard_map/all_to_all | solution.py:261
  73.1 1.8 %collective-permute-start.14 = (f32[24,256]{1,0:T(8,128)S(1)}, f32[24,256]{1,0:T(8,128)S(1)}, u32[]{:S(2)}, u32[]{:S(2)}) collective-permute-start(f32[24,256]{1,0:T(8,128)S(1)} %shard_map.89.own), channel_id=1, source_target_pairs={{0,64},{64,128},{128,192},{192,0},{1,65},{65,129},{129,193},{193,1... | collective-permute-start | bytes 73736 | tf_op jit(solution)/shard_map/ppermute | solution.py:265
  74.9 3.0 %collective-permute-start.15 = (f32[24,256]{1,0:T(8,128)S(1)}, f32[24,256]{1,0:T(8,128)S(1)}, u32[]{:S(2)}, u32[]{:S(2)}) collective-permute-start(f32[24,256]{1,0:T(8,128)S(1)} %shard_map.89.own), channel_id=1, source_target_pairs={{0,192},{64,0},{128,64},{192,128},{1,193},{65,1},{129,65},{193,129... | collective-permute-start | bytes 73736 | tf_op jit(solution)/shard_map/ppermute | solution.py:265
  77.9 4.4 %collective-permute-start.16 = (f32[24,256]{1,0:T(8,128)S(1)}, f32[24,256]{1,0:T(8,128)S(1)}, u32[]{:S(2)}, u32[]{:S(2)}) collective-permute-start(f32[24,256]{1,0:T(8,128)S(1)} %shard_map.89.own), channel_id=1, source_target_pairs={{0,128},{64,192},{128,0},{192,64},{1,129},{65,193},{129,1},{193,65... | collective-permute-start | bytes 73736 | tf_op jit(solution)/shard_map/ppermute | solution.py:265
  82.2 2.4 %collective-permute-done.16.across = f32[24,256]{1,0:T(8,128)S(1)} collective-permute-done((f32[24,256]{1,0:T(8,128)S(1)}, f32[24,256]{1,0:T(8,128)S(1)}, u32[]{:S(2)}, u32[]{:S(2)}) %collective-permute-start.16) | collective-permute-done | bytes 24608 | tf_op jit(solution)/shard_map/ppermute | solution.py:265
  85.4 9.6 %all_to_all.11.shared = bf16[16,32,128]{2,1,0:T(8,128)(2,1)S(1)} all-to-all(bf16[16,32,128]{2,1,0:T(8,128)(2,1)S(1)} %broadcast_in_dim.10), channel_id=1, replica_groups=mesh['zg'=4,'zi'=2,'y'=4,'x'=4,'core'=2] {'y','x'}, dimensions={0} | all-to-all | bytes 262144 | tf_op jit(solution)/shard_map/all_to_all | solution.py:270
  95.0 1.5 %shard_map.91 = (bf16[192,512]{1,0:T(8,128)(2,1)S(1)}, bf16[192,512]{1,0:T(8,128)(2,1)S(1)}, bf16[192,512]{1,0:T(8,128)(2,1)S(1)}, bf16[192,512]{1,0:T(8,128)(2,1)S(1)}) custom-call(s32[8]{0:T(128)S(1)} %stack.39.place, s32[256]{0:T(256)S(1)} %copy-done.3, bf16[576,768]{1,0:T(8,128)(2,1)S(1)} %get-tuple-element.18.proj, ...), custom_call_target="tpu_custom_call" | custom-call | flops 536870912 | bytes 3145728 | tf_op jit(solution)/shard_map/pallas_call | solution.py:273
  96.5 5.6 %collective-permute-start.17 = (bf16[192,512]{1,0:T(8,128)(2,1)S(1)}, bf16[192,512]{1,0:T(8,128)(2,1)S(1)}, u32[]{:S(2)}, u32[]{:S(2)}) collective-permute-start(bf16[192,512]{1,0:T(8,128)(2,1)S(1)} %get-tuple-element.21), channel_id=1, source_target_pairs={{0,1},{1,0},{2,3},{3,2},{4,5},{5,4},{6,7},{7,6},{8,9},{9,8},{10,11... | collective-permute-start | bytes 589832 | tf_op jit(solution)/shard_map/ppermute | solution.py:278
  102.8 1.0 collective-permute-start.19
  103.8 4.7 %collective-permute-done.18.refs_2_ = bf16[192,512]{1,0:T(8,128)(2,1)S(1)} collective-permute-done((bf16[192,512]{1,0:T(8,128)(2,1)S(1)}, bf16[192,512]{1,0:T(8,128)(2,1)S(1)}, u32[]{:S(2)}, u32[]{:S(2)}) %collective-permute-start.18) | collective-permute-done | bytes 196640 | tf_op jit(solution)/shard_map/ppermute | solution.py:279
  108.6 4.4 %collective-permute-done.19.refs_3_ = bf16[192,512]{1,0:T(8,128)(2,1)S(1)} collective-permute-done((bf16[192,512]{1,0:T(8,128)(2,1)S(1)}, bf16[192,512]{1,0:T(8,128)(2,1)S(1)}, u32[]{:S(2)}, u32[]{:S(2)}) %collective-permute-start.19) | collective-permute-done | bytes 196640 | tf_op jit(solution)/shard_map/ppermute | solution.py:280
  113.0 1.5 %shard_map.92 = (bf16[128,2048]{1,0:T(8,128)(2,1)}, bf16[64,2048]{1,0:T(8,128)(2,1)}) custom-call(s32[8]{0:T(128)S(1)} %stack.39.place, bf16[192,512]{1,0:T(8,128)(2,1)S(1)} %get-tuple-element.20.refs_0_, bf16[192,512]{1,0:T(8,128)(2,1)S(1)} %collective-permute-done.17.refs_1_, bf16[192,512]{1,0:T(8,128)(2,1)S(1)} %collective-permute-done.18.refs_2_, ...), custom_call_target="tpu_custom_call" | custom-call | bytes 2097152 | tf_op jit(solution)/shard_map/pallas_call | solution.py:282
  (37 shorter events, 6.7 us)
Async XLA Ops:
  0.6 6.5 %copy-start = (bf16[128,4096]{1,0:T(8,128)(2,1)S(1)}, bf16[128,4096]{1,0:T(8,128)(2,1)}, u32[]{:S(2)}) copy-start(bf16[128,4096]{1,0:T(8,128)(2,1)} %own.1) | copy-start | bytes 3145732
  2.6 4.4 %collective-permute-start.2 = (bf16[128,768]{1,0:T(8,128)(2,1)S(1)}, bf16[128,768]{1,0:T(8,128)(2,1)S(1)}, u32[]{:S(2)}, u32[]{:S(2)}) collective-permute-start(bf16[128,768]{1,0:T(8,128)(2,1)S(1)} %pad_maximum_fusion.3), channel_id=1, source_target_pairs={{0,1},{1,0},{2,3},{3,2},{4,5},{5,4},{6,7},{7,6},{8,9},{9,8},{10,11... | collective-permute-start | bytes 589832 | tf_op jit(solution)/shard_map/ppermute | solution.py:56
  7.0 8.2 %collective-permute-start.7 = (bf16[256,768]{1,0:T(8,128)(2,1)S(1)}, bf16[256,768]{1,0:T(8,128)(2,1)S(1)}, u32[]{:S(2)}, u32[]{:S(2)}) collective-permute-start(bf16[256,768]{1,0:T(8,128)(2,1)S(1)} %pad_maximum_fusion.1), channel_id=1, source_target_pairs={{0,2},{1,9},{2,4},{3,11},{4,6},{5,13},{6,0},{7,15},{8,10},{9,17},{... | collective-permute-start | bytes 1179656 | tf_op jit(solution)/shard_map/ppermute | solution.py:48
  7.1 24.6 %collective-permute-start.1 = (bf16[128,4096]{1,0:T(8,128)(2,1)S(1)}, bf16[128,4096]{1,0:T(8,128)(2,1)S(1)}, u32[]{:S(2)}, u32[]{:S(2)}) collective-permute-start(bf16[128,4096]{1,0:T(8,128)(2,1)S(1)} %copy-done), channel_id=1, source_target_pairs={{0,32},{32,0},{1,33},{33,1},{2,34},{34,2},{3,35},{35,3},{4,36},{36... | collective-permute-start | bytes 3145736 | tf_op jit(solution)/shard_map/ppermute | solution.py:245
  8.3 7.9 %collective-permute-start.3 = (bf16[256,768]{1,0:T(8,128)(2,1)S(1)}, bf16[256,768]{1,0:T(8,128)(2,1)S(1)}, u32[]{:S(2)}, u32[]{:S(2)}) collective-permute-start(bf16[256,768]{1,0:T(8,128)(2,1)S(1)} %pad_maximum_fusion.1), channel_id=1, source_target_pairs={{0,6},{1,25},{2,0},{3,27},{4,2},{5,29},{6,4},{7,31},{8,14},{9,1},{... | collective-permute-start | bytes 1179656 | tf_op jit(solution)/shard_map/ppermute | solution.py:48
  9.8 23.8 %collective-permute-start = (bf16[128,4096]{1,0:T(8,128)(2,1)S(1)}, bf16[128,4096]{1,0:T(8,128)(2,1)S(1)}, u32[]{:S(2)}, u32[]{:S(2)}) collective-permute-start(bf16[128,4096]{1,0:T(8,128)(2,1)S(1)} %copy-done), channel_id=1, source_target_pairs={{0,1},{1,0},{2,3},{3,2},{4,5},{5,4},{6,7},{7,6},{8,9},{9,8},{10,11... | collective-permute-start | bytes 3145736 | tf_op jit(solution)/shard_map/ppermute | solution.py:246
  10.9 27.3 %copy-start.2 = (f32[4096]{0:T(1024)S(1)}, f32[4096]{0:T(1024)}, u32[]{:S(2)}) copy-start(f32[4096]{0:T(1024)} %param.9) | copy-start | bytes 49156
  10.9 9.9 %collective-permute-start.4 = (bf16[128,768]{1,0:T(8,128)(2,1)S(1)}, bf16[128,768]{1,0:T(8,128)(2,1)S(1)}, u32[]{:S(2)}, u32[]{:S(2)}) collective-permute-start(bf16[128,768]{1,0:T(8,128)(2,1)S(1)} %pad_maximum_fusion.2), channel_id=1, source_target_pairs={{0,4},{1,17},{2,6},{3,19},{4,0},{5,21},{6,2},{7,23},{8,12},{9,25},... | collective-permute-start | bytes 589832 | tf_op jit(solution)/shard_map/ppermute | solution.py:48
  15.2 6.2 %collective-permute-start.5 = (bf16[128,768]{1,0:T(8,128)(2,1)S(1)}, bf16[128,768]{1,0:T(8,128)(2,1)S(1)}, u32[]{:S(2)}, u32[]{:S(2)}) collective-permute-start(bf16[128,768]{1,0:T(8,128)(2,1)S(1)} %collective-permute-done.2), channel_id=1, source_target_pairs={{0,4},{1,17},{2,6},{3,19},{4,0},{5,21},{6,2},{7,23},{8,12},{9,25},... | collective-permute-start | bytes 589832 | tf_op jit(solution)/shard_map/ppermute | solution.py:48
  16.2 19.3 %collective-permute-start.8 = (bf16[512,768]{1,0:T(8,128)(2,1)}, bf16[512,768]{1,0:T(8,128)(2,1)}, u32[]{:S(2)}, u32[]{:S(2)}) collective-permute-start(bf16[512,768]{1,0:T(8,128)(2,1)} %pad_maximum_fusion.refs_0_), channel_id=1, source_target_pairs={{0,8},{1,3},{2,10},{3,5},{4,12},{5,7},{6,14},{7,1},{8,16},{9,11},{... | collective-permute-start | bytes 2359304 | tf_op jit(solution)/shard_map/ppermute | solution.py:48
  22.2 13.3 %collective-permute-start.11 = (bf16[512,768]{1,0:T(8,128)(2,1)}, bf16[512,768]{1,0:T(8,128)(2,1)}, u32[]{:S(2)}, u32[]{:S(2)}) collective-permute-start(bf16[512,768]{1,0:T(8,128)(2,1)} %constant_dynamic-update-slice_fusion.refs_1_), channel_id=1, source_target_pairs={{0,24},{1,7},{2,26},{3,1},{4,28},{5,3},{6,30},{7,5},{8,0},{9,15},{... | collective-permute-start | bytes 2359304 | tf_op jit(solution)/shard_map/ppermute | solution.py:48
  31.7 6.5 %collective-permute-start.6 = (bf16[128,4096]{1,0:T(8,128)(2,1)S(1)}, bf16[128,4096]{1,0:T(8,128)(2,1)}, u32[]{:S(2)}, u32[]{:S(2)}) collective-permute-start(bf16[128,4096]{1,0:T(8,128)(2,1)S(1)} %collective-permute-done.1.z_mate), channel_id=1, source_target_pairs={{0,1},{1,0},{2,3},{3,2},{4,5},{5,4},{6,7},{7,6},{8,9},{9,8},{10,11... | collective-permute-start | bytes 3145736 | tf_op jit(solution)/shard_map/ppermute | solution.py:248
  32.8 12.7 %collective-permute-start.9 = (bf16[512,768]{1,0:T(8,128)(2,1)}, bf16[512,768]{1,0:T(8,128)(2,1)}, u32[]{:S(2)}, u32[]{:S(2)}) collective-permute-start(bf16[512,768]{1,0:T(8,128)(2,1)} %constant_dynamic-update-slice_fusion.refs_1_), channel_id=1, source_target_pairs={{0,8},{1,3},{2,10},{3,5},{4,12},{5,7},{6,14},{7,1},{8,16},{9,11},{... | collective-permute-start | bytes 2359304 | tf_op jit(solution)/shard_map/ppermute | solution.py:48
  33.6 11.8 %collective-permute-start.10 = (bf16[512,768]{1,0:T(8,128)(2,1)}, bf16[512,768]{1,0:T(8,128)(2,1)}, u32[]{:S(2)}, u32[]{:S(2)}) collective-permute-start(bf16[512,768]{1,0:T(8,128)(2,1)} %pad_maximum_fusion.refs_0_), channel_id=1, source_target_pairs={{0,24},{1,7},{2,26},{3,1},{4,28},{5,3},{6,30},{7,5},{8,0},{9,15},{... | collective-permute-start | bytes 2359304 | tf_op jit(solution)/shard_map/ppermute | solution.py:48
  35.5 18.4 %collective-permute-start.12 = (bf16[512,768]{1,0:T(8,128)(2,1)}, bf16[512,768]{1,0:T(8,128)(2,1)}, u32[]{:S(2)}, u32[]{:S(2)}) collective-permute-start(bf16[512,768]{1,0:T(8,128)(2,1)} %collective-permute-done.8.refs_2_), channel_id=1, source_target_pairs={{0,8},{1,3},{2,10},{3,5},{4,12},{5,7},{6,14},{7,1},{8,16},{9,11},{... | collective-permute-start | bytes 2359304 | tf_op jit(solution)/shard_map/ppermute | solution.py:48
  35.5 18.4 %collective-permute-start.13 = (bf16[512,768]{1,0:T(8,128)(2,1)}, bf16[512,768]{1,0:T(8,128)(2,1)}, u32[]{:S(2)}, u32[]{:S(2)}) collective-permute-start(bf16[512,768]{1,0:T(8,128)(2,1)} %collective-permute-done.11.refs_5_), channel_id=1, source_target_pairs={{0,24},{1,7},{2,26},{3,1},{4,28},{5,3},{6,30},{7,5},{8,0},{9,15},{... | collective-permute-start | bytes 2359304 | tf_op jit(solution)/shard_map/ppermute | solution.py:48
  38.2 1.0 copy-start.1
  45.5 8.4 %copy-start.3 = (s32[256]{0:T(256)S(1)}, s32[256]{0:T(256)}, u32[]{:S(2)}) copy-start(s32[256]{0:T(256)} %lengths.3) | copy-start | bytes 3076
  73.1 9.1 %collective-permute-start.14 = (f32[24,256]{1,0:T(8,128)S(1)}, f32[24,256]{1,0:T(8,128)S(1)}, u32[]{:S(2)}, u32[]{:S(2)}) collective-permute-start(f32[24,256]{1,0:T(8,128)S(1)} %shard_map.89.own), channel_id=1, source_target_pairs={{0,64},{64,128},{128,192},{192,0},{1,65},{65,129},{129,193},{193,1... | collective-permute-start | bytes 73736 | tf_op jit(solution)/shard_map/ppermute | solution.py:265
  74.9 7.3 %collective-permute-start.15 = (f32[24,256]{1,0:T(8,128)S(1)}, f32[24,256]{1,0:T(8,128)S(1)}, u32[]{:S(2)}, u32[]{:S(2)}) collective-permute-start(f32[24,256]{1,0:T(8,128)S(1)} %shard_map.89.own), channel_id=1, source_target_pairs={{0,192},{64,0},{128,64},{192,128},{1,193},{65,1},{129,65},{193,129... | collective-permute-start | bytes 73736 | tf_op jit(solution)/shard_map/ppermute | solution.py:265
  77.9 6.8 %collective-permute-start.16 = (f32[24,256]{1,0:T(8,128)S(1)}, f32[24,256]{1,0:T(8,128)S(1)}, u32[]{:S(2)}, u32[]{:S(2)}) collective-permute-start(f32[24,256]{1,0:T(8,128)S(1)} %shard_map.89.own), channel_id=1, source_target_pairs={{0,128},{64,192},{128,0},{192,64},{1,129},{65,193},{129,1},{193,65... | collective-permute-start | bytes 73736 | tf_op jit(solution)/shard_map/ppermute | solution.py:265
  96.5 7.3 %collective-permute-start.17 = (bf16[192,512]{1,0:T(8,128)(2,1)S(1)}, bf16[192,512]{1,0:T(8,128)(2,1)S(1)}, u32[]{:S(2)}, u32[]{:S(2)}) collective-permute-start(bf16[192,512]{1,0:T(8,128)(2,1)S(1)} %get-tuple-element.21), channel_id=1, source_target_pairs={{0,1},{1,0},{2,3},{3,2},{4,5},{5,4},{6,7},{7,6},{8,9},{9,8},{10,11... | collective-permute-start | bytes 589832 | tf_op jit(solution)/shard_map/ppermute | solution.py:278
  102.1 6.5 %collective-permute-start.18 = (bf16[192,512]{1,0:T(8,128)(2,1)S(1)}, bf16[192,512]{1,0:T(8,128)(2,1)S(1)}, u32[]{:S(2)}, u32[]{:S(2)}) collective-permute-start(bf16[192,512]{1,0:T(8,128)(2,1)S(1)} %get-tuple-element.22), channel_id=1, source_target_pairs={{0,32},{32,0},{1,33},{33,1},{2,34},{34,2},{3,35},{35,3},{4,36},{36... | collective-permute-start | bytes 589832 | tf_op jit(solution)/shard_map/ppermute | solution.py:279
  102.8 10.1 %collective-permute-start.19 = (bf16[192,512]{1,0:T(8,128)(2,1)S(1)}, bf16[192,512]{1,0:T(8,128)(2,1)S(1)}, u32[]{:S(2)}, u32[]{:S(2)}) collective-permute-start(bf16[192,512]{1,0:T(8,128)(2,1)S(1)} %get-tuple-element.23), channel_id=1, source_target_pairs={{0,33},{1,32},{32,1},{33,0},{2,35},{3,34},{34,3},{35,2},{4,37},{5,... | collective-permute-start | bytes 589832 | tf_op jit(solution)/shard_map/ppermute | solution.py:280

commit v3 on v2

--- a/solution.py
+++ b/solution.py
@@ -52,12 +52,22 @@
     return jnp.concatenate([top, bottom], axis=0)
 
 
+def join_kernel(own, before, after, across, near, far):
+    near[:256, :] = own[...]
+    near[256:, :] = before[...]
+    far[:256, :] = after[...]
+    far[256:, :] = across[...]
+
+
 def gather_weights(mine, theirs):
     mate = lax.ppermute(theirs, "core", SWAP)
     own = join(mine, mate)
     before, after = send(own, 1, True), send(own, -1, True)
-    across = join(send(mine, 2, True), send(mate, -2, True))
-    near, far = join(own, before), join(after, across)
+    firsts = before, after, send(own, 2, True)
+    before, after, across = lax.optimization_barrier(firsts)
+    near, far = call(join_kernel, shapes(*[((512, 768), bf16)] * 2), 0, 4, 0, 3 << 20)(
+        own, before, after, across
+    )
     near_before, far_after = send(near, 1, False), send(far, -1, False)
     far_before, near_after = send(far, 1, False), send(near, -1, False)
     near_across, far_across = send(near_before, 1, False), send(far_after, -1, False)

time: 115 us -> 112 us (0.974)
  waiting for transfers between devices: 27.9 us -> 30.8 us
  local copies, waits for them, and re-layouts: 5.22 us -> 2.97 us
  blocking collectives: 24.6 us -> 23 us
  starting transfers between devices: 38.1 us -> 36.5 us
  Pallas kernels: 16.7 us -> 18 us
    ppermute x10 -> x9, waiting for transfers between devices: 7.04 us -> 17.9 us  [send(): return lax.ppermute(rows, YXC, torus_pairs(step, first))]
    ppermute x1, waiting for transfers between devices: 8.26 us -> 0.55 us  [per_device(): z_mate = lax.ppermute(context, 'zi', SWAP)]
    ppermute x10 -> x9, starting transfers between devices: 15.1 us -> 12.5 us  [send(): return lax.ppermute(rows, YXC, torus_pairs(step, first))]
    ppermute x1, starting transfers between devices: 3.33 us -> 1.08 us  [gather_weights(): mate = lax.ppermute(theirs, 'core', SWAP)]
    all_to_all x1, blocking collectives: 15 us -> 13.4 us  [per_device(): gathered = lax.all_to_all(packed, PLANE, 0, 0, tiled=True)]
    unnamed x10 -> x8, local copies, waits for them, and re-layouts: 2.53 us -> 1.05 us
    ppermute x1, starting transfers between devices: 1.18 us -> 2.55 us  [per_device(): z_mate = lax.ppermute(context, 'zi', SWAP)]
    pallas_call x0 -> x1, Pallas kernels: none -> 1.26 us  [gather_weights(): call(join_kernel, shapes(*[((512, 768), bf16)] * 2), 0, 4, 0, 3 << 20)]
  transfers between devices with their start and end apart: 20 -> 19, of which waited for: 8 -> 11; matrix products, arithmetic and copies ran while one was open for 3% -> 2% of each run, Pallas kernels for 8% -> 9%
where the time goes in v3:
time: 112 us
  starting transfers between devices  36.5 us (33%)
  waiting for transfers between devices  30.8 us (28%)
  blocking collectives  23 us (21%)
  Pallas kernels  18 us (16%)
  local copies, waits for them, and re-layouts  2.97 us (3%)
    ppermute x9, waiting for transfers between devices, send(): return lax.ppermute(rows, YXC, torus_pairs(step, first))  17.9 us
    all_to_all x1, blocking collectives, per_device(): gathered = lax.all_to_all(packed, PLANE, 0, 0, tiled=True)  13.4 us
    ppermute x9, starting transfers between devices, send(): return lax.ppermute(rows, YXC, torus_pairs(step, first))  12.5 us
    ppermute x3, starting transfers between devices, per_device(): lax.ppermute(merged, 'zg', [(i, (i + k) % 4) for i in range(4)])  9.63 us
    all_to_all x1, blocking collectives, per_device(): lax.all_to_all(jnp.broadcast_to(final[None], (CHIPS, *final.shape)), PLAN...  9.58 us
    ppermute x1, starting transfers between devices, per_device(): lax.ppermute(pieces[1], 'core', SWAP)  6.79 us
    pallas_call x1, Pallas kernels, per_device(): call(project_kernel, jax.ShapeDtypeStruct((rows, 768), f32), 0, 9, 27 <<...  5.23 us
    ppermute x1, waiting for transfers between devices, per_device(): lax.ppermute(pieces[2], 'zi', SWAP)  4.73 us
  transfers between devices with their start and end apart: 19, of which 11 were waited for; matrix products, arithmetic and copies ran while one was open for 2% of the time, Pallas kernels for 9%

profile of v3, /device:TPU:1, one launch (start us, length us, event | category | flops | bytes accessed | tf_op | source)
XLA Modules:
  0.0 112.0 jit_solution(15527127076136023104)
XLA Ops:
  0.6 2.6 %collective-permute-start.1 = (bf16[128,4096]{1,0:T(8,128)(2,1)}, bf16[128,4096]{1,0:T(8,128)(2,1)S(1)}, u32[]{:S(2)}, u32[]{:S(2)}) collective-permute-start(bf16[128,4096]{1,0:T(8,128)(2,1)} %own.1), channel_id=1, source_target_pairs={{0,32},{32,0},{1,33},{33,1},{2,34},{34,2},{3,35},{35,3},{4,36},{36... | collective-permute-start | bytes 3145736 | tf_op jit(solution)/shard_map/ppermute | solution.py:255
  3.2 1.0 constant_dynamic-slice_fusion.5
  5.0 1.1 collective-permute-start.2
  7.2 1.3 %collective-permute-start.3 = (bf16[256,768]{1,0:T(8,128)(2,1)S(1)}, bf16[256,768]{1,0:T(8,128)(2,1)S(1)}, u32[]{:S(2)}, u32[]{:S(2)}) collective-permute-start(bf16[256,768]{1,0:T(8,128)(2,1)S(1)} %pad_maximum_fusion.own), channel_id=1, source_target_pairs={{0,2},{1,9},{2,4},{3,11},{4,6},{5,13},{6,0},{7,15},{8,10},{9,17},{... | collective-permute-start | bytes 1179656 | tf_op jit(solution)/shard_map/ppermute | solution.py:48
  8.6 1.5 %collective-permute-start.4 = (bf16[256,768]{1,0:T(8,128)(2,1)S(1)}, bf16[256,768]{1,0:T(8,128)(2,1)S(1)}, u32[]{:S(2)}, u32[]{:S(2)}) collective-permute-start(bf16[256,768]{1,0:T(8,128)(2,1)S(1)} %pad_maximum_fusion.own), channel_id=1, source_target_pairs={{0,6},{1,25},{2,0},{3,27},{4,2},{5,29},{6,4},{7,31},{8,14},{9,1},{... | collective-permute-start | bytes 1179656 | tf_op jit(solution)/shard_map/ppermute | solution.py:48
  10.1 1.6 %collective-permute-start.5 = (bf16[256,768]{1,0:T(8,128)(2,1)S(1)}, bf16[256,768]{1,0:T(8,128)(2,1)S(1)}, u32[]{:S(2)}, u32[]{:S(2)}) collective-permute-start(bf16[256,768]{1,0:T(8,128)(2,1)S(1)} %pad_maximum_fusion.own), channel_id=1, source_target_pairs={{0,4},{1,17},{2,6},{3,19},{4,0},{5,21},{6,2},{7,23},{8,12},{9,25},... | collective-permute-start | bytes 1179656 | tf_op jit(solution)/shard_map/ppermute | solution.py:48
  11.6 3.8 %collective-permute-done.3.before = bf16[256,768]{1,0:T(8,128)(2,1)S(1)} collective-permute-done((bf16[256,768]{1,0:T(8,128)(2,1)S(1)}, bf16[256,768]{1,0:T(8,128)(2,1)S(1)}, u32[]{:S(2)}, u32[]{:S(2)}) %collective-permute-start.3) | collective-permute-done | bytes 393248 | tf_op jit(solution)/shard_map/ppermute | solution.py:48
  15.5 3.6 %collective-permute-done.4.after = bf16[256,768]{1,0:T(8,128)(2,1)S(1)} collective-permute-done((bf16[256,768]{1,0:T(8,128)(2,1)S(1)}, bf16[256,768]{1,0:T(8,128)(2,1)S(1)}, u32[]{:S(2)}, u32[]{:S(2)}) %collective-permute-start.4) | collective-permute-done | bytes 393248 | tf_op jit(solution)/shard_map/ppermute | solution.py:48
  19.0 1.8 %collective-permute-done.5.across = bf16[256,768]{1,0:T(8,128)(2,1)S(1)} collective-permute-done((bf16[256,768]{1,0:T(8,128)(2,1)S(1)}, bf16[256,768]{1,0:T(8,128)(2,1)S(1)}, u32[]{:S(2)}, u32[]{:S(2)}) %collective-permute-start.5) | collective-permute-done | bytes 393248 | tf_op jit(solution)/shard_map/ppermute | solution.py:48
  20.9 1.3 %shard_map.86 = (bf16[512,768]{1,0:T(8,128)(2,1)}, bf16[512,768]{1,0:T(8,128)(2,1)}) custom-call(bf16[256,768]{1,0:T(8,128)(2,1)S(1)} %pad_maximum_fusion.own, bf16[256,768]{1,0:T(8,128)(2,1)S(1)} %collective-permute-done.3.before, bf16[256,768]{1,0:T(8,128)(2,1)S(1)} %collective-permute-done.4.after, bf16[256,768]{1,0:T(8,128)(2,1)S(1)} %collective-permute-done.5.across), custom_call_target="tpu_custom_call" | custom-call | bytes 3145728 | tf_op jit(solution)/shard_map/pallas_call | solution.py:68
  23.0 1.8 %collective-permute-start.10 = (bf16[512,768]{1,0:T(8,128)(2,1)}, bf16[512,768]{1,0:T(8,128)(2,1)}, u32[]{:S(2)}, u32[]{:S(2)}) collective-permute-start(bf16[512,768]{1,0:T(8,128)(2,1)} %get-tuple-element.21.refs_1_), channel_id=1, source_target_pairs={{0,24},{1,7},{2,26},{3,1},{4,28},{5,3},{6,30},{7,5},{8,0},{9,15},{... | collective-permute-start | bytes 2359304 | tf_op jit(solution)/shard_map/ppermute | solution.py:48
  25.3 2.2 %collective-permute-start.6 = (bf16[128,4096]{1,0:T(8,128)(2,1)S(1)}, bf16[128,4096]{1,0:T(8,128)(2,1)}, u32[]{:S(2)}, u32[]{:S(2)}) collective-permute-start(bf16[128,4096]{1,0:T(8,128)(2,1)S(1)} %collective-permute-done.1.z_mate), channel_id=1, source_target_pairs={{0,1},{1,0},{2,3},{3,2},{4,5},{5,4},{6,7},{7,6},{8,9},{9,8},{10,11... | collective-permute-start | bytes 3145736 | tf_op jit(solution)/shard_map/ppermute | solution.py:258
  27.5 1.2 %collective-permute-start.8 = (bf16[512,768]{1,0:T(8,128)(2,1)}, bf16[512,768]{1,0:T(8,128)(2,1)}, u32[]{:S(2)}, u32[]{:S(2)}) collective-permute-start(bf16[512,768]{1,0:T(8,128)(2,1)} %get-tuple-element.21.refs_1_), channel_id=1, source_target_pairs={{0,8},{1,3},{2,10},{3,5},{4,12},{5,7},{6,14},{7,1},{8,16},{9,11},{... | collective-permute-start | bytes 2359304 | tf_op jit(solution)/shard_map/ppermute | solution.py:48
  28.7 1.5 %collective-permute-start.9 = (bf16[512,768]{1,0:T(8,128)(2,1)}, bf16[512,768]{1,0:T(8,128)(2,1)}, u32[]{:S(2)}, u32[]{:S(2)}) collective-permute-start(bf16[512,768]{1,0:T(8,128)(2,1)} %get-tuple-element.27.refs_0_), channel_id=1, source_target_pairs={{0,24},{1,7},{2,26},{3,1},{4,28},{5,3},{6,30},{7,5},{8,0},{9,15},{... | collective-permute-start | bytes 2359304 | tf_op jit(solution)/shard_map/ppermute | solution.py:48
  30.2 4.6 %collective-permute-done.7.refs_2_ = bf16[512,768]{1,0:T(8,128)(2,1)} collective-permute-done((bf16[512,768]{1,0:T(8,128)(2,1)}, bf16[512,768]{1,0:T(8,128)(2,1)}, u32[]{:S(2)}, u32[]{:S(2)}) %collective-permute-start.7) | collective-permute-done | bytes 786464 | tf_op jit(solution)/shard_map/ppermute | solution.py:48
  34.8 2.7 %collective-permute-start.12 = (bf16[512,768]{1,0:T(8,128)(2,1)}, bf16[512,768]{1,0:T(8,128)(2,1)}, u32[]{:S(2)}, u32[]{:S(2)}) collective-permute-start(bf16[512,768]{1,0:T(8,128)(2,1)} %collective-permute-done.10.refs_5_), channel_id=1, source_target_pairs={{0,24},{1,7},{2,26},{3,1},{4,28},{5,3},{6,30},{7,5},{8,0},{9,15},{... | collective-permute-start | bytes 2359304 | tf_op jit(solution)/shard_map/ppermute | solution.py:48
  37.6 1.0 copy-done.1
  38.6 3.6 %shard_map.87 = (bf16[576,1024]{1,0:T(8,128)(2,1)S(1)}, bf16[576,1024]{1,0:T(8,128)(2,1)S(1)}, bf16[576,1024]{1,0:T(8,128)(2,1)S(1)}, bf16[576,1024]{1,0:T(8,128)(2,1)S(1)}) custom-call(s32[8]{0:T(128)S(1)} %stack.39.place, bf16[128,4096]{1,0:T(8,128)(2,1)S(1)} %copy-done, bf16[128,4096]{1,0:T(8,128)(2,1)S(1)} %collective-permute-done.core_mate, ...), custom_call_target="tpu_custom_call" | custom-call | flops 16777216 | bytes 10485760 | tf_op jit(solution)/shard_map/pallas_call | solution.py:260
  43.2 5.2 %shard_map.88.total = f32[576,768]{1,0:T(8,128)S(1)} custom-call(bf16[576,1024]{1,0:T(8,128)(2,1)S(1)} %get-tuple-element.24.own, bf16[576,1024]{1,0:T(8,128)(2,1)S(1)} %get-tuple-element.25.before, bf16[576,1024]{1,0:T(8,128)(2,1)S(1)} %get-tuple-element.26.after, bf16[512,768]{1,0:T(8,128)(2,1)} %get-tuple-element.27.refs_0_, ...), custom_call_target="tpu_custom_call" | custom-call | flops 3623878656 | bytes 12582912 | tf_op jit(solution)/shard_map/pallas_call | solution.py:264
  48.4 3.2 %collective-permute-done.11.near = bf16[512,768]{1,0:T(8,128)(2,1)} collective-permute-done((bf16[512,768]{1,0:T(8,128)(2,1)}, bf16[512,768]{1,0:T(8,128)(2,1)}, u32[]{:S(2)}, u32[]{:S(2)}) %collective-permute-start.11) | collective-permute-done | bytes 786464 | tf_op jit(solution)/shard_map/ppermute | solution.py:48
  51.6 4.0 %shard_map.89 = (bf16[576,768]{1,0:T(8,128)(2,1)S(1)}, f32[16,24,256]{2,1,0:T(8,128)S(1)}) custom-call(s32[8]{0:T(128)S(1)} %stack.39.place, s32[256]{0:T(256)S(1)} %copy-done.3, bf16[576,1024]{1,0:T(8,128)(2,1)S(1)} %get-tuple-element.23.across, f32[576,768]{1,0:T(8,128)S(1)} %shard_map.88.total, bf16[512,768]{1,0:T(8,128)(2,1)} %collective-permute-done.11.near, ...), custom_call_target="tpu_custom_call" | custom-call | flops 1207959552 | bytes 6291456 | tf_op jit(solution)/shard_map/pallas_call | solution.py:267
  55.6 13.4 %all_to_all.10.parts = f32[16,24,256]{2,1,0:T(8,128)S(1)} all-to-all(f32[16,24,256]{2,1,0:T(8,128)S(1)} %get-tuple-element.29), channel_id=1, replica_groups=mesh['zg'=4,'zi'=2,'y'=4,'x'=4,'core'=2] {'y','x'}, dimensions={0} | all-to-all | bytes 786432 | tf_op jit(solution)/shard_map/all_to_all | solution.py:271
  69.2 3.0 %collective-permute-start.13 = (f32[24,256]{1,0:T(8,128)S(1)}, f32[24,256]{1,0:T(8,128)S(1)}, u32[]{:S(2)}, u32[]{:S(2)}) collective-permute-start(f32[24,256]{1,0:T(8,128)S(1)} %shard_map.90.own), channel_id=1, source_target_pairs={{0,64},{64,128},{128,192},{192,0},{1,65},{65,129},{129,193},{193,1... | collective-permute-start | bytes 73736 | tf_op jit(solution)/shard_map/ppermute | solution.py:275
  72.3 2.2 %collective-permute-start.14 = (f32[24,256]{1,0:T(8,128)S(1)}, f32[24,256]{1,0:T(8,128)S(1)}, u32[]{:S(2)}, u32[]{:S(2)}) collective-permute-start(f32[24,256]{1,0:T(8,128)S(1)} %shard_map.90.own), channel_id=1, source_target_pairs={{0,192},{64,0},{128,64},{192,128},{1,193},{65,1},{129,65},{193,129... | collective-permute-start | bytes 73736 | tf_op jit(solution)/shard_map/ppermute | solution.py:275
  74.5 4.4 %collective-permute-start.15 = (f32[24,256]{1,0:T(8,128)S(1)}, f32[24,256]{1,0:T(8,128)S(1)}, u32[]{:S(2)}, u32[]{:S(2)}) collective-permute-start(f32[24,256]{1,0:T(8,128)S(1)} %shard_map.90.own), channel_id=1, source_target_pairs={{0,128},{64,192},{128,0},{192,64},{1,129},{65,193},{129,1},{193,65... | collective-permute-start | bytes 73736 | tf_op jit(solution)/shard_map/ppermute | solution.py:275
  78.9 2.2 %collective-permute-done.15.across = f32[24,256]{1,0:T(8,128)S(1)} collective-permute-done((f32[24,256]{1,0:T(8,128)S(1)}, f32[24,256]{1,0:T(8,128)S(1)}, u32[]{:S(2)}, u32[]{:S(2)}) %collective-permute-start.15) | collective-permute-done | bytes 24608 | tf_op jit(solution)/shard_map/ppermute | solution.py:275
  81.8 9.6 %all_to_all.11.shared = bf16[16,32,128]{2,1,0:T(8,128)(2,1)S(1)} all-to-all(bf16[16,32,128]{2,1,0:T(8,128)(2,1)S(1)} %broadcast_in_dim.10), channel_id=1, replica_groups=mesh['zg'=4,'zi'=2,'y'=4,'x'=4,'core'=2] {'y','x'}, dimensions={0} | all-to-all | bytes 262144 | tf_op jit(solution)/shard_map/all_to_all | solution.py:280
  91.4 1.5 %shard_map.92 = (bf16[192,512]{1,0:T(8,128)(2,1)S(1)}, bf16[192,512]{1,0:T(8,128)(2,1)S(1)}, bf16[192,512]{1,0:T(8,128)(2,1)S(1)}, bf16[192,512]{1,0:T(8,128)(2,1)S(1)}) custom-call(s32[8]{0:T(128)S(1)} %stack.39.place, s32[256]{0:T(256)S(1)} %copy-done.3, bf16[576,768]{1,0:T(8,128)(2,1)S(1)} %get-tuple-element.28.proj, ...), custom_call_target="tpu_custom_call" | custom-call | flops 536870912 | bytes 3145728 | tf_op jit(solution)/shard_map/pallas_call | solution.py:283
  92.9 6.8 %collective-permute-start.16 = (bf16[192,512]{1,0:T(8,128)(2,1)S(1)}, bf16[192,512]{1,0:T(8,128)(2,1)S(1)}, u32[]{:S(2)}, u32[]{:S(2)}) collective-permute-start(bf16[192,512]{1,0:T(8,128)(2,1)S(1)} %get-tuple-element.31), channel_id=1, source_target_pairs={{0,1},{1,0},{2,3},{3,2},{4,5},{5,4},{6,7},{7,6},{8,9},{9,8},{10,11... | collective-permute-start | bytes 589832 | tf_op jit(solution)/shard_map/ppermute | solution.py:288
  101.4 4.7 %collective-permute-done.17.refs_2_ = bf16[192,512]{1,0:T(8,128)(2,1)S(1)} collective-permute-done((bf16[192,512]{1,0:T(8,128)(2,1)S(1)}, bf16[192,512]{1,0:T(8,128)(2,1)S(1)}, u32[]{:S(2)}, u32[]{:S(2)}) %collective-permute-start.17) | collective-permute-done | bytes 196640 | tf_op jit(solution)/shard_map/ppermute | solution.py:289
  106.2 4.4 %collective-permute-done.18.refs_3_ = bf16[192,512]{1,0:T(8,128)(2,1)S(1)} collective-permute-done((bf16[192,512]{1,0:T(8,128)(2,1)S(1)}, bf16[192,512]{1,0:T(8,128)(2,1)S(1)}, u32[]{:S(2)}, u32[]{:S(2)}) %collective-permute-start.18) | collective-permute-done | bytes 196640 | tf_op jit(solution)/shard_map/ppermute | solution.py:290
  110.6 1.5 %shard_map.93 = (bf16[128,2048]{1,0:T(8,128)(2,1)}, bf16[64,2048]{1,0:T(8,128)(2,1)}) custom-call(s32[8]{0:T(128)S(1)} %stack.39.place, bf16[192,512]{1,0:T(8,128)(2,1)S(1)} %get-tuple-element.30.refs_0_, bf16[192,512]{1,0:T(8,128)(2,1)S(1)} %collective-permute-done.16.refs_1_, bf16[192,512]{1,0:T(8,128)(2,1)S(1)} %collective-permute-done.17.refs_2_, ...), custom_call_target="tpu_custom_call" | custom-call | bytes 2097152 | tf_op jit(solution)/shard_map/pallas_call | solution.py:292
  (31 shorter events, 7.1 us)
Async XLA Ops:
  0.6 5.5 %copy-start = (bf16[128,4096]{1,0:T(8,128)(2,1)S(1)}, bf16[128,4096]{1,0:T(8,128)(2,1)}, u32[]{:S(2)}) copy-start(bf16[128,4096]{1,0:T(8,128)(2,1)} %own.1) | copy-start | bytes 3145732
  0.6 24.7 %collective-permute-start.1 = (bf16[128,4096]{1,0:T(8,128)(2,1)}, bf16[128,4096]{1,0:T(8,128)(2,1)S(1)}, u32[]{:S(2)}, u32[]{:S(2)}) collective-permute-start(bf16[128,4096]{1,0:T(8,128)(2,1)} %own.1), channel_id=1, source_target_pairs={{0,32},{32,0},{1,33},{33,1},{2,34},{34,2},{3,35},{35,3},{4,36},{36... | collective-permute-start | bytes 3145736 | tf_op jit(solution)/shard_map/ppermute | solution.py:255
  5.0 2.1 %collective-permute-start.2 = (bf16[128,768]{1,0:T(8,128)(2,1)S(1)}, bf16[128,768]{1,0:T(8,128)(2,1)S(1)}, u32[]{:S(2)}, u32[]{:S(2)}) collective-permute-start(bf16[128,768]{1,0:T(8,128)(2,1)S(1)} %pad_maximum_fusion.1), channel_id=1, source_target_pairs={{0,1},{1,0},{2,3},{3,2},{4,5},{5,4},{6,7},{7,6},{8,9},{9,8},{10,11... | collective-permute-start | bytes 589832 | tf_op jit(solution)/shard_map/ppermute | solution.py:63
  6.1 22.6 %collective-permute-start = (bf16[128,4096]{1,0:T(8,128)(2,1)S(1)}, bf16[128,4096]{1,0:T(8,128)(2,1)S(1)}, u32[]{:S(2)}, u32[]{:S(2)}) collective-permute-start(bf16[128,4096]{1,0:T(8,128)(2,1)S(1)} %copy-done), channel_id=1, source_target_pairs={{0,1},{1,0},{2,3},{3,2},{4,5},{5,4},{6,7},{7,6},{8,9},{9,8},{10,11... | collective-permute-start | bytes 3145736 | tf_op jit(solution)/shard_map/ppermute | solution.py:256
  7.2 30.4 %copy-start.2 = (f32[4096]{0:T(1024)S(1)}, f32[4096]{0:T(1024)}, u32[]{:S(2)}) copy-start(f32[4096]{0:T(1024)} %param.9) | copy-start | bytes 49156
  7.2 8.2 %collective-permute-start.3 = (bf16[256,768]{1,0:T(8,128)(2,1)S(1)}, bf16[256,768]{1,0:T(8,128)(2,1)S(1)}, u32[]{:S(2)}, u32[]{:S(2)}) collective-permute-start(bf16[256,768]{1,0:T(8,128)(2,1)S(1)} %pad_maximum_fusion.own), channel_id=1, source_target_pairs={{0,2},{1,9},{2,4},{3,11},{4,6},{5,13},{6,0},{7,15},{8,10},{9,17},{... | collective-permute-start | bytes 1179656 | tf_op jit(solution)/shard_map/ppermute | solution.py:48
  8.6 10.5 %collective-permute-start.4 = (bf16[256,768]{1,0:T(8,128)(2,1)S(1)}, bf16[256,768]{1,0:T(8,128)(2,1)S(1)}, u32[]{:S(2)}, u32[]{:S(2)}) collective-permute-start(bf16[256,768]{1,0:T(8,128)(2,1)S(1)} %pad_maximum_fusion.own), channel_id=1, source_target_pairs={{0,6},{1,25},{2,0},{3,27},{4,2},{5,29},{6,4},{7,31},{8,14},{9,1},{... | collective-permute-start | bytes 1179656 | tf_op jit(solution)/shard_map/ppermute | solution.py:48
  10.1 10.8 %collective-permute-start.5 = (bf16[256,768]{1,0:T(8,128)(2,1)S(1)}, bf16[256,768]{1,0:T(8,128)(2,1)S(1)}, u32[]{:S(2)}, u32[]{:S(2)}) collective-permute-start(bf16[256,768]{1,0:T(8,128)(2,1)S(1)} %pad_maximum_fusion.own), channel_id=1, source_target_pairs={{0,4},{1,17},{2,6},{3,19},{4,0},{5,21},{6,2},{7,23},{8,12},{9,25},... | collective-permute-start | bytes 1179656 | tf_op jit(solution)/shard_map/ppermute | solution.py:48
  22.1 12.7 %collective-permute-start.7 = (bf16[512,768]{1,0:T(8,128)(2,1)}, bf16[512,768]{1,0:T(8,128)(2,1)}, u32[]{:S(2)}, u32[]{:S(2)}) collective-permute-start(bf16[512,768]{1,0:T(8,128)(2,1)} %get-tuple-element.27.refs_0_), channel_id=1, source_target_pairs={{0,8},{1,3},{2,10},{3,5},{4,12},{5,7},{6,14},{7,1},{8,16},{9,11},{... | collective-permute-start | bytes 2359304 | tf_op jit(solution)/shard_map/ppermute | solution.py:48
  23.0 11.8 %collective-permute-start.10 = (bf16[512,768]{1,0:T(8,128)(2,1)}, bf16[512,768]{1,0:T(8,128)(2,1)}, u32[]{:S(2)}, u32[]{:S(2)}) collective-permute-start(bf16[512,768]{1,0:T(8,128)(2,1)} %get-tuple-element.21.refs_1_), channel_id=1, source_target_pairs={{0,24},{1,7},{2,26},{3,1},{4,28},{5,3},{6,30},{7,5},{8,0},{9,15},{... | collective-permute-start | bytes 2359304 | tf_op jit(solution)/shard_map/ppermute | solution.py:48
  25.3 12.2 %collective-permute-start.6 = (bf16[128,4096]{1,0:T(8,128)(2,1)S(1)}, bf16[128,4096]{1,0:T(8,128)(2,1)}, u32[]{:S(2)}, u32[]{:S(2)}) collective-permute-start(bf16[128,4096]{1,0:T(8,128)(2,1)S(1)} %collective-permute-done.1.z_mate), channel_id=1, source_target_pairs={{0,1},{1,0},{2,3},{3,2},{4,5},{5,4},{6,7},{7,6},{8,9},{9,8},{10,11... | collective-permute-start | bytes 3145736 | tf_op jit(solution)/shard_map/ppermute | solution.py:258
  27.5 15.7 %collective-permute-start.8 = (bf16[512,768]{1,0:T(8,128)(2,1)}, bf16[512,768]{1,0:T(8,128)(2,1)}, u32[]{:S(2)}, u32[]{:S(2)}) collective-permute-start(bf16[512,768]{1,0:T(8,128)(2,1)} %get-tuple-element.21.refs_1_), channel_id=1, source_target_pairs={{0,8},{1,3},{2,10},{3,5},{4,12},{5,7},{6,14},{7,1},{8,16},{9,11},{... | collective-permute-start | bytes 2359304 | tf_op jit(solution)/shard_map/ppermute | solution.py:48
  28.7 14.5 %collective-permute-start.9 = (bf16[512,768]{1,0:T(8,128)(2,1)}, bf16[512,768]{1,0:T(8,128)(2,1)}, u32[]{:S(2)}, u32[]{:S(2)}) collective-permute-start(bf16[512,768]{1,0:T(8,128)(2,1)} %get-tuple-element.27.refs_0_), channel_id=1, source_target_pairs={{0,24},{1,7},{2,26},{3,1},{4,28},{5,3},{6,30},{7,5},{8,0},{9,15},{... | collective-permute-start | bytes 2359304 | tf_op jit(solution)/shard_map/ppermute | solution.py:48
  34.8 16.9 %collective-permute-start.11 = (bf16[512,768]{1,0:T(8,128)(2,1)}, bf16[512,768]{1,0:T(8,128)(2,1)}, u32[]{:S(2)}, u32[]{:S(2)}) collective-permute-start(bf16[512,768]{1,0:T(8,128)(2,1)} %collective-permute-done.7.refs_2_), channel_id=1, source_target_pairs={{0,8},{1,3},{2,10},{3,5},{4,12},{5,7},{6,14},{7,1},{8,16},{9,11},{... | collective-permute-start | bytes 2359304 | tf_op jit(solution)/shard_map/ppermute | solution.py:48
  34.8 16.8 %collective-permute-start.12 = (bf16[512,768]{1,0:T(8,128)(2,1)}, bf16[512,768]{1,0:T(8,128)(2,1)}, u32[]{:S(2)}, u32[]{:S(2)}) collective-permute-start(bf16[512,768]{1,0:T(8,128)(2,1)} %collective-permute-done.10.refs_5_), channel_id=1, source_target_pairs={{0,24},{1,7},{2,26},{3,1},{4,28},{5,3},{6,30},{7,5},{8,0},{9,15},{... | collective-permute-start | bytes 2359304 | tf_op jit(solution)/shard_map/ppermute | solution.py:48
  37.6 1.0 copy-start.1
  43.2 8.4 %copy-start.3 = (s32[256]{0:T(256)S(1)}, s32[256]{0:T(256)}, u32[]{:S(2)}) copy-start(s32[256]{0:T(256)} %lengths.3) | copy-start | bytes 3076
  69.2 9.6 %collective-permute-start.13 = (f32[24,256]{1,0:T(8,128)S(1)}, f32[24,256]{1,0:T(8,128)S(1)}, u32[]{:S(2)}, u32[]{:S(2)}) collective-permute-start(f32[24,256]{1,0:T(8,128)S(1)} %shard_map.90.own), channel_id=1, source_target_pairs={{0,64},{64,128},{128,192},{192,0},{1,65},{65,129},{129,193},{193,1... | collective-permute-start | bytes 73736 | tf_op jit(solution)/shard_map/ppermute | solution.py:275
  72.3 6.6 %collective-permute-start.14 = (f32[24,256]{1,0:T(8,128)S(1)}, f32[24,256]{1,0:T(8,128)S(1)}, u32[]{:S(2)}, u32[]{:S(2)}) collective-permute-start(f32[24,256]{1,0:T(8,128)S(1)} %shard_map.90.own), channel_id=1, source_target_pairs={{0,192},{64,0},{128,64},{192,128},{1,193},{65,1},{129,65},{193,129... | collective-permute-start | bytes 73736 | tf_op jit(solution)/shard_map/ppermute | solution.py:275
  74.5 6.6 %collective-permute-start.15 = (f32[24,256]{1,0:T(8,128)S(1)}, f32[24,256]{1,0:T(8,128)S(1)}, u32[]{:S(2)}, u32[]{:S(2)}) collective-permute-start(f32[24,256]{1,0:T(8,128)S(1)} %shard_map.90.own), channel_id=1, source_target_pairs={{0,128},{64,192},{128,0},{192,64},{1,129},{65,193},{129,1},{193,65... | collective-permute-start | bytes 73736 | tf_op jit(solution)/shard_map/ppermute | solution.py:275
  92.9 8.5 %collective-permute-start.16 = (bf16[192,512]{1,0:T(8,128)(2,1)S(1)}, bf16[192,512]{1,0:T(8,128)(2,1)S(1)}, u32[]{:S(2)}, u32[]{:S(2)}) collective-permute-start(bf16[192,512]{1,0:T(8,128)(2,1)S(1)} %get-tuple-element.31), channel_id=1, source_target_pairs={{0,1},{1,0},{2,3},{3,2},{4,5},{5,4},{6,7},{7,6},{8,9},{9,8},{10,11... | collective-permute-start | bytes 589832 | tf_op jit(solution)/shard_map/ppermute | solution.py:288
  99.7 6.5 %collective-permute-start.17 = (bf16[192,512]{1,0:T(8,128)(2,1)S(1)}, bf16[192,512]{1,0:T(8,128)(2,1)S(1)}, u32[]{:S(2)}, u32[]{:S(2)}) collective-permute-start(bf16[192,512]{1,0:T(8,128)(2,1)S(1)} %get-tuple-element.32), channel_id=1, source_target_pairs={{0,32},{32,0},{1,33},{33,1},{2,34},{34,2},{3,35},{35,3},{4,36},{36... | collective-permute-start | bytes 589832 | tf_op jit(solution)/shard_map/ppermute | solution.py:289
  100.5 10.1 %collective-permute-start.18 = (bf16[192,512]{1,0:T(8,128)(2,1)S(1)}, bf16[192,512]{1,0:T(8,128)(2,1)S(1)}, u32[]{:S(2)}, u32[]{:S(2)}) collective-permute-start(bf16[192,512]{1,0:T(8,128)(2,1)S(1)} %get-tuple-element.33), channel_id=1, source_target_pairs={{0,33},{1,32},{32,1},{33,0},{2,35},{3,34},{34,3},{35,2},{4,37},{5,... | collective-permute-start | bytes 589832 | tf_op jit(solution)/shard_map/ppermute | solution.py:290

commit v4 on v3

--- a/solution.py
+++ b/solution.py
@@ -283,12 +283,10 @@
     pieces = call(
         block_kernel, shapes(*[((BLK + QTOK, 512), bf16)] * 4), 2, 2, 1 << 29, 3 << 20
     )(place, lengths, proj, shared)
-    received = (
-        pieces[0],
-        lax.ppermute(pieces[1], "core", SWAP),
-        lax.ppermute(pieces[2], "zi", SWAP),
-        lax.ppermute(pieces[3], ("zi", "core"), [(i, 3 - i) for i in range(4)]),
-    )
+    from_z = lax.ppermute(pieces[2], "zi", SWAP)
+    from_zc = lax.ppermute(pieces[3], ("zi", "core"), [(i, 3 - i) for i in range(4)])
+    to_core, from_z = lax.optimization_barrier((pieces[1], from_z))
+    received = (pieces[0], lax.ppermute(to_core, "core", SWAP), from_z, from_zc)
     return call(
         assemble_kernel, shapes(((BLK, 2048), bf16), ((QTOK, 2048), bf16)), 1, 4, 0, 2 << 20
     )(place, *received)

time: 112 us -> 111 us (level)
  waiting for transfers between devices: 30.8 us -> 23.4 us
  starting transfers between devices: 36.5 us -> 42.2 us
    ppermute x1, starting transfers between devices: 0.98 us -> 7.58 us  [per_device(): lax.ppermute(pieces[3], ('zi', 'core'), [(i, 3 - i) for i in range(4)])]
    ppermute x2, waiting for transfers between devices: 4.73 us -> 0.01 us  [the longest x1 0.01 us: per_device(): from_z = lax.ppermute(pieces[2], 'zi', SWAP)]
    ppermute x1, waiting for transfers between devices: 4.4 us -> 1.77 us  [per_device(): lax.ppermute(pieces[3], ('zi', 'core'), [(i, 3 - i) for i in range(4)])]
  transfers between devices with their start and end apart: 19 -> 19, of which waited for: 11 -> 10; matrix products, arithmetic and copies ran while one was open for 2% -> 2% of each run, Pallas kernels for 9% -> 9%
where the time goes in v4:
time: 111 us; the launch traced here: 110 us
  starting transfers between devices  42.2 us (38%)
  waiting for transfers between devices  23.4 us (21%)
  blocking collectives  23 us (21%)
  Pallas kernels  18 us (16%)
  local copies, waits for them, and re-layouts  2.97 us (3%)
    ppermute x9, waiting for transfers between devices, send(): return lax.ppermute(rows, YXC, torus_pairs(step, first))  17.9 us
    all_to_all x1, blocking collectives, per_device(): gathered = lax.all_to_all(packed, PLANE, 0, 0, tiled=True)  13.4 us
    ppermute x9, starting transfers between devices, send(): return lax.ppermute(rows, YXC, torus_pairs(step, first))  12.5 us
    ppermute x3, starting transfers between devices, per_device(): lax.ppermute(merged, 'zg', [(i, (i + k) % 4) for i in range(4)])  9.63 us
    all_to_all x1, blocking collectives, per_device(): lax.all_to_all(jnp.broadcast_to(final[None], (CHIPS, *final.shape)), PLAN...  9.58 us
    ppermute x1, starting transfers between devices, per_device(): lax.ppermute(pieces[3], ('zi', 'core'), [(i, 3 - i) for i in range(4)])  7.58 us
    ppermute x1, starting transfers between devices, per_device(): received = (pieces[0], lax.ppermute(to_core, 'core', SWAP), from_z, from_zc)  5.79 us
    pallas_call x1, Pallas kernels, per_device(): call(project_kernel, jax.ShapeDtypeStruct((rows, 768), f32), 0, 9, 27 <<...  5.23 us
  transfers between devices with their start and end apart: 19, of which 10 were waited for; matrix products, arithmetic and copies ran while one was open for 2% of the time, Pallas kernels for 9%

profile of v4, /device:TPU:1, one launch (start us, length us, event | category | flops | bytes accessed | tf_op | source)
XLA Modules:
  0.0 110.4 jit_solution(16636582590123278684)
XLA Ops:
  0.6 2.6 %collective-permute-start.1 = (bf16[128,4096]{1,0:T(8,128)(2,1)}, bf16[128,4096]{1,0:T(8,128)(2,1)S(1)}, u32[]{:S(2)}, u32[]{:S(2)}) collective-permute-start(bf16[128,4096]{1,0:T(8,128)(2,1)} %own.1), channel_id=1, source_target_pairs={{0,32},{32,0},{1,33},{33,1},{2,34},{34,2},{3,35},{35,3},{4,36},{36... | collective-permute-start | bytes 3145736 | tf_op jit(solution)/shard_map/ppermute | solution.py:255
  3.2 1.0 constant_dynamic-slice_fusion.5
  5.0 1.1 collective-permute-start.2
  7.2 1.3 %collective-permute-start.3 = (bf16[256,768]{1,0:T(8,128)(2,1)S(1)}, bf16[256,768]{1,0:T(8,128)(2,1)S(1)}, u32[]{:S(2)}, u32[]{:S(2)}) collective-permute-start(bf16[256,768]{1,0:T(8,128)(2,1)S(1)} %pad_maximum_fusion.own), channel_id=1, source_target_pairs={{0,2},{1,9},{2,4},{3,11},{4,6},{5,13},{6,0},{7,15},{8,10},{9,17},{... | collective-permute-start | bytes 1179656 | tf_op jit(solution)/shard_map/ppermute | solution.py:48
  8.6 1.5 %collective-permute-start.4 = (bf16[256,768]{1,0:T(8,128)(2,1)S(1)}, bf16[256,768]{1,0:T(8,128)(2,1)S(1)}, u32[]{:S(2)}, u32[]{:S(2)}) collective-permute-start(bf16[256,768]{1,0:T(8,128)(2,1)S(1)} %pad_maximum_fusion.own), channel_id=1, source_target_pairs={{0,6},{1,25},{2,0},{3,27},{4,2},{5,29},{6,4},{7,31},{8,14},{9,1},{... | collective-permute-start | bytes 1179656 | tf_op jit(solution)/shard_map/ppermute | solution.py:48
  10.1 1.6 %collective-permute-start.5 = (bf16[256,768]{1,0:T(8,128)(2,1)S(1)}, bf16[256,768]{1,0:T(8,128)(2,1)S(1)}, u32[]{:S(2)}, u32[]{:S(2)}) collective-permute-start(bf16[256,768]{1,0:T(8,128)(2,1)S(1)} %pad_maximum_fusion.own), channel_id=1, source_target_pairs={{0,4},{1,17},{2,6},{3,19},{4,0},{5,21},{6,2},{7,23},{8,12},{9,25},... | collective-permute-start | bytes 1179656 | tf_op jit(solution)/shard_map/ppermute | solution.py:48
  11.6 3.8 %collective-permute-done.3.before = bf16[256,768]{1,0:T(8,128)(2,1)S(1)} collective-permute-done((bf16[256,768]{1,0:T(8,128)(2,1)S(1)}, bf16[256,768]{1,0:T(8,128)(2,1)S(1)}, u32[]{:S(2)}, u32[]{:S(2)}) %collective-permute-start.3) | collective-permute-done | bytes 393248 | tf_op jit(solution)/shard_map/ppermute | solution.py:48
  15.5 3.6 %collective-permute-done.4.after = bf16[256,768]{1,0:T(8,128)(2,1)S(1)} collective-permute-done((bf16[256,768]{1,0:T(8,128)(2,1)S(1)}, bf16[256,768]{1,0:T(8,128)(2,1)S(1)}, u32[]{:S(2)}, u32[]{:S(2)}) %collective-permute-start.4) | collective-permute-done | bytes 393248 | tf_op jit(solution)/shard_map/ppermute | solution.py:48
  19.0 1.8 %collective-permute-done.5.across = bf16[256,768]{1,0:T(8,128)(2,1)S(1)} collective-permute-done((bf16[256,768]{1,0:T(8,128)(2,1)S(1)}, bf16[256,768]{1,0:T(8,128)(2,1)S(1)}, u32[]{:S(2)}, u32[]{:S(2)}) %collective-permute-start.5) | collective-permute-done | bytes 393248 | tf_op jit(solution)/shard_map/ppermute | solution.py:48
  20.9 1.3 %shard_map.86 = (bf16[512,768]{1,0:T(8,128)(2,1)}, bf16[512,768]{1,0:T(8,128)(2,1)}) custom-call(bf16[256,768]{1,0:T(8,128)(2,1)S(1)} %pad_maximum_fusion.own, bf16[256,768]{1,0:T(8,128)(2,1)S(1)} %collective-permute-done.3.before, bf16[256,768]{1,0:T(8,128)(2,1)S(1)} %collective-permute-done.4.after, bf16[256,768]{1,0:T(8,128)(2,1)S(1)} %collective-permute-done.5.across), custom_call_target="tpu_custom_call" | custom-call | bytes 3145728 | tf_op jit(solution)/shard_map/pallas_call | solution.py:68
  23.0 1.8 %collective-permute-start.10 = (bf16[512,768]{1,0:T(8,128)(2,1)}, bf16[512,768]{1,0:T(8,128)(2,1)}, u32[]{:S(2)}, u32[]{:S(2)}) collective-permute-start(bf16[512,768]{1,0:T(8,128)(2,1)} %get-tuple-element.23.refs_1_), channel_id=1, source_target_pairs={{0,24},{1,7},{2,26},{3,1},{4,28},{5,3},{6,30},{7,5},{8,0},{9,15},{... | collective-permute-start | bytes 2359304 | tf_op jit(solution)/shard_map/ppermute | solution.py:48
  25.3 2.2 %collective-permute-start.6 = (bf16[128,4096]{1,0:T(8,128)(2,1)S(1)}, bf16[128,4096]{1,0:T(8,128)(2,1)}, u32[]{:S(2)}, u32[]{:S(2)}) collective-permute-start(bf16[128,4096]{1,0:T(8,128)(2,1)S(1)} %collective-permute-done.1.z_mate), channel_id=1, source_target_pairs={{0,1},{1,0},{2,3},{3,2},{4,5},{5,4},{6,7},{7,6},{8,9},{9,8},{10,11... | collective-permute-start | bytes 3145736 | tf_op jit(solution)/shard_map/ppermute | solution.py:258
  27.5 1.2 %collective-permute-start.8 = (bf16[512,768]{1,0:T(8,128)(2,1)}, bf16[512,768]{1,0:T(8,128)(2,1)}, u32[]{:S(2)}, u32[]{:S(2)}) collective-permute-start(bf16[512,768]{1,0:T(8,128)(2,1)} %get-tuple-element.23.refs_1_), channel_id=1, source_target_pairs={{0,8},{1,3},{2,10},{3,5},{4,12},{5,7},{6,14},{7,1},{8,16},{9,11},{... | collective-permute-start | bytes 2359304 | tf_op jit(solution)/shard_map/ppermute | solution.py:48
  28.7 1.5 %collective-permute-start.9 = (bf16[512,768]{1,0:T(8,128)(2,1)}, bf16[512,768]{1,0:T(8,128)(2,1)}, u32[]{:S(2)}, u32[]{:S(2)}) collective-permute-start(bf16[512,768]{1,0:T(8,128)(2,1)} %get-tuple-element.29.refs_0_), channel_id=1, source_target_pairs={{0,24},{1,7},{2,26},{3,1},{4,28},{5,3},{6,30},{7,5},{8,0},{9,15},{... | collective-permute-start | bytes 2359304 | tf_op jit(solution)/shard_map/ppermute | solution.py:48
  30.2 4.6 %collective-permute-done.7.refs_2_ = bf16[512,768]{1,0:T(8,128)(2,1)} collective-permute-done((bf16[512,768]{1,0:T(8,128)(2,1)}, bf16[512,768]{1,0:T(8,128)(2,1)}, u32[]{:S(2)}, u32[]{:S(2)}) %collective-permute-start.7) | collective-permute-done | bytes 786464 | tf_op jit(solution)/shard_map/ppermute | solution.py:48
  34.8 2.7 %collective-permute-start.12 = (bf16[512,768]{1,0:T(8,128)(2,1)}, bf16[512,768]{1,0:T(8,128)(2,1)}, u32[]{:S(2)}, u32[]{:S(2)}) collective-permute-start(bf16[512,768]{1,0:T(8,128)(2,1)} %collective-permute-done.10.refs_5_), channel_id=1, source_target_pairs={{0,24},{1,7},{2,26},{3,1},{4,28},{5,3},{6,30},{7,5},{8,0},{9,15},{... | collective-permute-start | bytes 2359304 | tf_op jit(solution)/shard_map/ppermute | solution.py:48
  37.6 1.0 copy-done.1
  38.6 3.6 %shard_map.87 = (bf16[576,1024]{1,0:T(8,128)(2,1)S(1)}, bf16[576,1024]{1,0:T(8,128)(2,1)S(1)}, bf16[576,1024]{1,0:T(8,128)(2,1)S(1)}, bf16[576,1024]{1,0:T(8,128)(2,1)S(1)}) custom-call(s32[8]{0:T(128)S(1)} %stack.39.place, bf16[128,4096]{1,0:T(8,128)(2,1)S(1)} %copy-done, bf16[128,4096]{1,0:T(8,128)(2,1)S(1)} %collective-permute-done.core_mate, ...), custom_call_target="tpu_custom_call" | custom-call | flops 16777216 | bytes 10485760 | tf_op jit(solution)/shard_map/pallas_call | solution.py:260
  43.2 5.2 %shard_map.88.total = f32[576,768]{1,0:T(8,128)S(1)} custom-call(bf16[576,1024]{1,0:T(8,128)(2,1)S(1)} %get-tuple-element.26.own, bf16[576,1024]{1,0:T(8,128)(2,1)S(1)} %get-tuple-element.27.before, bf16[576,1024]{1,0:T(8,128)(2,1)S(1)} %get-tuple-element.28.after, bf16[512,768]{1,0:T(8,128)(2,1)} %get-tuple-element.29.refs_0_, ...), custom_call_target="tpu_custom_call" | custom-call | flops 3623878656 | bytes 12582912 | tf_op jit(solution)/shard_map/pallas_call | solution.py:264
  48.4 3.2 %collective-permute-done.11.near = bf16[512,768]{1,0:T(8,128)(2,1)} collective-permute-done((bf16[512,768]{1,0:T(8,128)(2,1)}, bf16[512,768]{1,0:T(8,128)(2,1)}, u32[]{:S(2)}, u32[]{:S(2)}) %collective-permute-start.11) | collective-permute-done | bytes 786464 | tf_op jit(solution)/shard_map/ppermute | solution.py:48
  51.6 4.0 %shard_map.89 = (bf16[576,768]{1,0:T(8,128)(2,1)S(1)}, f32[16,24,256]{2,1,0:T(8,128)S(1)}) custom-call(s32[8]{0:T(128)S(1)} %stack.39.place, s32[256]{0:T(256)S(1)} %copy-done.3, bf16[576,1024]{1,0:T(8,128)(2,1)S(1)} %get-tuple-element.25.across, f32[576,768]{1,0:T(8,128)S(1)} %shard_map.88.total, bf16[512,768]{1,0:T(8,128)(2,1)} %collective-permute-done.11.near, ...), custom_call_target="tpu_custom_call" | custom-call | flops 1207959552 | bytes 6291456 | tf_op jit(solution)/shard_map/pallas_call | solution.py:267
  55.6 13.4 %all_to_all.10.parts = f32[16,24,256]{2,1,0:T(8,128)S(1)} all-to-all(f32[16,24,256]{2,1,0:T(8,128)S(1)} %get-tuple-element.31), channel_id=1, replica_groups=mesh['zg'=4,'zi'=2,'y'=4,'x'=4,'core'=2] {'y','x'}, dimensions={0} | all-to-all | bytes 786432 | tf_op jit(solution)/shard_map/all_to_all | solution.py:271
  69.2 3.0 %collective-permute-start.13 = (f32[24,256]{1,0:T(8,128)S(1)}, f32[24,256]{1,0:T(8,128)S(1)}, u32[]{:S(2)}, u32[]{:S(2)}) collective-permute-start(f32[24,256]{1,0:T(8,128)S(1)} %shard_map.90.own), channel_id=1, source_target_pairs={{0,64},{64,128},{128,192},{192,0},{1,65},{65,129},{129,193},{193,1... | collective-permute-start | bytes 73736 | tf_op jit(solution)/shard_map/ppermute | solution.py:275
  72.3 2.2 %collective-permute-start.14 = (f32[24,256]{1,0:T(8,128)S(1)}, f32[24,256]{1,0:T(8,128)S(1)}, u32[]{:S(2)}, u32[]{:S(2)}) collective-permute-start(f32[24,256]{1,0:T(8,128)S(1)} %shard_map.90.own), channel_id=1, source_target_pairs={{0,192},{64,0},{128,64},{192,128},{1,193},{65,1},{129,65},{193,129... | collective-permute-start | bytes 73736 | tf_op jit(solution)/shard_map/ppermute | solution.py:275
  74.5 4.4 %collective-permute-start.15 = (f32[24,256]{1,0:T(8,128)S(1)}, f32[24,256]{1,0:T(8,128)S(1)}, u32[]{:S(2)}, u32[]{:S(2)}) collective-permute-start(f32[24,256]{1,0:T(8,128)S(1)} %shard_map.90.own), channel_id=1, source_target_pairs={{0,128},{64,192},{128,0},{192,64},{1,129},{65,193},{129,1},{193,65... | collective-permute-start | bytes 73736 | tf_op jit(solution)/shard_map/ppermute | solution.py:275
  78.9 2.2 %collective-permute-done.15.across = f32[24,256]{1,0:T(8,128)S(1)} collective-permute-done((f32[24,256]{1,0:T(8,128)S(1)}, f32[24,256]{1,0:T(8,128)S(1)}, u32[]{:S(2)}, u32[]{:S(2)}) %collective-permute-start.15) | collective-permute-done | bytes 24608 | tf_op jit(solution)/shard_map/ppermute | solution.py:275
  81.8 9.6 %all_to_all.11.shared = bf16[16,32,128]{2,1,0:T(8,128)(2,1)S(1)} all-to-all(bf16[16,32,128]{2,1,0:T(8,128)(2,1)S(1)} %broadcast_in_dim.10), channel_id=1, replica_groups=mesh['zg'=4,'zi'=2,'y'=4,'x'=4,'core'=2] {'y','x'}, dimensions={0} | all-to-all | bytes 262144 | tf_op jit(solution)/shard_map/all_to_all | solution.py:280
  91.4 1.5 %shard_map.92 = (bf16[192,512]{1,0:T(8,128)(2,1)S(1)}, bf16[192,512]{1,0:T(8,128)(2,1)S(1)}, bf16[192,512]{1,0:T(8,128)(2,1)S(1)}, bf16[192,512]{1,0:T(8,128)(2,1)S(1)}) custom-call(s32[8]{0:T(128)S(1)} %stack.39.place, s32[256]{0:T(256)S(1)} %copy-done.3, bf16[576,768]{1,0:T(8,128)(2,1)S(1)} %get-tuple-element.30.proj, ...), custom_call_target="tpu_custom_call" | custom-call | flops 536870912 | bytes 3145728 | tf_op jit(solution)/shard_map/pallas_call | solution.py:283
  93.8 7.6 %collective-permute-start.18 = (bf16[192,512]{1,0:T(8,128)(2,1)S(1)}, bf16[192,512]{1,0:T(8,128)(2,1)S(1)}, u32[]{:S(2)}, u32[]{:S(2)}) collective-permute-start(bf16[192,512]{1,0:T(8,128)(2,1)S(1)} %get-tuple-element.37), channel_id=1, source_target_pairs={{0,33},{1,32},{32,1},{33,0},{2,35},{3,34},{34,3},{35,2},{4,37},{5,... | collective-permute-start | bytes 589832 | tf_op jit(solution)/shard_map/ppermute | solution.py:287
  101.3 5.8 %collective-permute-start.17 = (bf16[192,512]{1,0:T(8,128)(2,1)S(1)}, bf16[192,512]{1,0:T(8,128)(2,1)S(1)}, u32[]{:S(2)}, u32[]{:S(2)}) collective-permute-start(bf16[192,512]{1,0:T(8,128)(2,1)S(1)} %get-tuple-element.35), channel_id=1, source_target_pairs={{0,1},{1,0},{2,3},{3,2},{4,5},{5,4},{6,7},{7,6},{8,9},{9,8},{10,11... | collective-permute-start | bytes 589832 | tf_op jit(solution)/shard_map/ppermute | solution.py:289
  107.1 1.8 %collective-permute-done.18.refs_3_ = bf16[192,512]{1,0:T(8,128)(2,1)S(1)} collective-permute-done((bf16[192,512]{1,0:T(8,128)(2,1)S(1)}, bf16[192,512]{1,0:T(8,128)(2,1)S(1)}, u32[]{:S(2)}, u32[]{:S(2)}) %collective-permute-start.18) | collective-permute-done | bytes 196640 | tf_op jit(solution)/shard_map/ppermute | solution.py:287
  108.9 1.5 %shard_map.93 = (bf16[128,2048]{1,0:T(8,128)(2,1)}, bf16[64,2048]{1,0:T(8,128)(2,1)}) custom-call(s32[8]{0:T(128)S(1)} %stack.39.place, bf16[192,512]{1,0:T(8,128)(2,1)S(1)} %get-tuple-element.32.refs_0_, bf16[192,512]{1,0:T(8,128)(2,1)S(1)} %collective-permute-done.17.refs_1_, bf16[192,512]{1,0:T(8,128)(2,1)S(1)} %collective-permute-done.16.refs_2_, ...), custom_call_target="tpu_custom_call" | custom-call | bytes 2097152 | tf_op jit(solution)/shard_map/pallas_call | solution.py:290
  (31 shorter events, 6.3 us)
Async XLA Ops:
  0.6 5.5 %copy-start = (bf16[128,4096]{1,0:T(8,128)(2,1)S(1)}, bf16[128,4096]{1,0:T(8,128)(2,1)}, u32[]{:S(2)}) copy-start(bf16[128,4096]{1,0:T(8,128)(2,1)} %own.1) | copy-start | bytes 3145732
  0.6 24.7 %collective-permute-start.1 = (bf16[128,4096]{1,0:T(8,128)(2,1)}, bf16[128,4096]{1,0:T(8,128)(2,1)S(1)}, u32[]{:S(2)}, u32[]{:S(2)}) collective-permute-start(bf16[128,4096]{1,0:T(8,128)(2,1)} %own.1), channel_id=1, source_target_pairs={{0,32},{32,0},{1,33},{33,1},{2,34},{34,2},{3,35},{35,3},{4,36},{36... | collective-permute-start | bytes 3145736 | tf_op jit(solution)/shard_map/ppermute | solution.py:255
  5.0 2.1 %collective-permute-start.2 = (bf16[128,768]{1,0:T(8,128)(2,1)S(1)}, bf16[128,768]{1,0:T(8,128)(2,1)S(1)}, u32[]{:S(2)}, u32[]{:S(2)}) collective-permute-start(bf16[128,768]{1,0:T(8,128)(2,1)S(1)} %pad_maximum_fusion.1), channel_id=1, source_target_pairs={{0,1},{1,0},{2,3},{3,2},{4,5},{5,4},{6,7},{7,6},{8,9},{9,8},{10,11... | collective-permute-start | bytes 589832 | tf_op jit(solution)/shard_map/ppermute | solution.py:63
  6.1 22.6 %collective-permute-start = (bf16[128,4096]{1,0:T(8,128)(2,1)S(1)}, bf16[128,4096]{1,0:T(8,128)(2,1)S(1)}, u32[]{:S(2)}, u32[]{:S(2)}) collective-permute-start(bf16[128,4096]{1,0:T(8,128)(2,1)S(1)} %copy-done), channel_id=1, source_target_pairs={{0,1},{1,0},{2,3},{3,2},{4,5},{5,4},{6,7},{7,6},{8,9},{9,8},{10,11... | collective-permute-start | bytes 3145736 | tf_op jit(solution)/shard_map/ppermute | solution.py:256
  7.2 30.4 %copy-start.2 = (f32[4096]{0:T(1024)S(1)}, f32[4096]{0:T(1024)}, u32[]{:S(2)}) copy-start(f32[4096]{0:T(1024)} %param.9) | copy-start | bytes 49156
  7.2 8.2 %collective-permute-start.3 = (bf16[256,768]{1,0:T(8,128)(2,1)S(1)}, bf16[256,768]{1,0:T(8,128)(2,1)S(1)}, u32[]{:S(2)}, u32[]{:S(2)}) collective-permute-start(bf16[256,768]{1,0:T(8,128)(2,1)S(1)} %pad_maximum_fusion.own), channel_id=1, source_target_pairs={{0,2},{1,9},{2,4},{3,11},{4,6},{5,13},{6,0},{7,15},{8,10},{9,17},{... | collective-permute-start | bytes 1179656 | tf_op jit(solution)/shard_map/ppermute | solution.py:48
  8.6 10.5 %collective-permute-start.4 = (bf16[256,768]{1,0:T(8,128)(2,1)S(1)}, bf16[256,768]{1,0:T(8,128)(2,1)S(1)}, u32[]{:S(2)}, u32[]{:S(2)}) collective-permute-start(bf16[256,768]{1,0:T(8,128)(2,1)S(1)} %pad_maximum_fusion.own), channel_id=1, source_target_pairs={{0,6},{1,25},{2,0},{3,27},{4,2},{5,29},{6,4},{7,31},{8,14},{9,1},{... | collective-permute-start | bytes 1179656 | tf_op jit(solution)/shard_map/ppermute | solution.py:48
  10.1 10.8 %collective-permute-start.5 = (bf16[256,768]{1,0:T(8,128)(2,1)S(1)}, bf16[256,768]{1,0:T(8,128)(2,1)S(1)}, u32[]{:S(2)}, u32[]{:S(2)}) collective-permute-start(bf16[256,768]{1,0:T(8,128)(2,1)S(1)} %pad_maximum_fusion.own), channel_id=1, source_target_pairs={{0,4},{1,17},{2,6},{3,19},{4,0},{5,21},{6,2},{7,23},{8,12},{9,25},... | collective-permute-start | bytes 1179656 | tf_op jit(solution)/shard_map/ppermute | solution.py:48
  22.1 12.7 %collective-permute-start.7 = (bf16[512,768]{1,0:T(8,128)(2,1)}, bf16[512,768]{1,0:T(8,128)(2,1)}, u32[]{:S(2)}, u32[]{:S(2)}) collective-permute-start(bf16[512,768]{1,0:T(8,128)(2,1)} %get-tuple-element.29.refs_0_), channel_id=1, source_target_pairs={{0,8},{1,3},{2,10},{3,5},{4,12},{5,7},{6,14},{7,1},{8,16},{9,11},{... | collective-permute-start | bytes 2359304 | tf_op jit(solution)/shard_map/ppermute | solution.py:48
  23.0 11.8 %collective-permute-start.10 = (bf16[512,768]{1,0:T(8,128)(2,1)}, bf16[512,768]{1,0:T(8,128)(2,1)}, u32[]{:S(2)}, u32[]{:S(2)}) collective-permute-start(bf16[512,768]{1,0:T(8,128)(2,1)} %get-tuple-element.23.refs_1_), channel_id=1, source_target_pairs={{0,24},{1,7},{2,26},{3,1},{4,28},{5,3},{6,30},{7,5},{8,0},{9,15},{... | collective-permute-start | bytes 2359304 | tf_op jit(solution)/shard_map/ppermute | solution.py:48
  25.3 12.2 %collective-permute-start.6 = (bf16[128,4096]{1,0:T(8,128)(2,1)S(1)}, bf16[128,4096]{1,0:T(8,128)(2,1)}, u32[]{:S(2)}, u32[]{:S(2)}) collective-permute-start(bf16[128,4096]{1,0:T(8,128)(2,1)S(1)} %collective-permute-done.1.z_mate), channel_id=1, source_target_pairs={{0,1},{1,0},{2,3},{3,2},{4,5},{5,4},{6,7},{7,6},{8,9},{9,8},{10,11... | collective-permute-start | bytes 3145736 | tf_op jit(solution)/shard_map/ppermute | solution.py:258
  27.5 15.7 %collective-permute-start.8 = (bf16[512,768]{1,0:T(8,128)(2,1)}, bf16[512,768]{1,0:T(8,128)(2,1)}, u32[]{:S(2)}, u32[]{:S(2)}) collective-permute-start(bf16[512,768]{1,0:T(8,128)(2,1)} %get-tuple-element.23.refs_1_), channel_id=1, source_target_pairs={{0,8},{1,3},{2,10},{3,5},{4,12},{5,7},{6,14},{7,1},{8,16},{9,11},{... | collective-permute-start | bytes 2359304 | tf_op jit(solution)/shard_map/ppermute | solution.py:48
  28.7 14.5 %collective-permute-start.9 = (bf16[512,768]{1,0:T(8,128)(2,1)}, bf16[512,768]{1,0:T(8,128)(2,1)}, u32[]{:S(2)}, u32[]{:S(2)}) collective-permute-start(bf16[512,768]{1,0:T(8,128)(2,1)} %get-tuple-element.29.refs_0_), channel_id=1, source_target_pairs={{0,24},{1,7},{2,26},{3,1},{4,28},{5,3},{6,30},{7,5},{8,0},{9,15},{... | collective-permute-start | bytes 2359304 | tf_op jit(solution)/shard_map/ppermute | solution.py:48
  34.8 16.9 %collective-permute-start.11 = (bf16[512,768]{1,0:T(8,128)(2,1)}, bf16[512,768]{1,0:T(8,128)(2,1)}, u32[]{:S(2)}, u32[]{:S(2)}) collective-permute-start(bf16[512,768]{1,0:T(8,128)(2,1)} %collective-permute-done.7.refs_2_), channel_id=1, source_target_pairs={{0,8},{1,3},{2,10},{3,5},{4,12},{5,7},{6,14},{7,1},{8,16},{9,11},{... | collective-permute-start | bytes 2359304 | tf_op jit(solution)/shard_map/ppermute | solution.py:48
  34.8 16.8 %collective-permute-start.12 = (bf16[512,768]{1,0:T(8,128)(2,1)}, bf16[512,768]{1,0:T(8,128)(2,1)}, u32[]{:S(2)}, u32[]{:S(2)}) collective-permute-start(bf16[512,768]{1,0:T(8,128)(2,1)} %collective-permute-done.10.refs_5_), channel_id=1, source_target_pairs={{0,24},{1,7},{2,26},{3,1},{4,28},{5,3},{6,30},{7,5},{8,0},{9,15},{... | collective-permute-start | bytes 2359304 | tf_op jit(solution)/shard_map/ppermute | solution.py:48
  37.6 1.0 copy-start.1
  43.2 8.4 %copy-start.3 = (s32[256]{0:T(256)S(1)}, s32[256]{0:T(256)}, u32[]{:S(2)}) copy-start(s32[256]{0:T(256)} %lengths.3) | copy-start | bytes 3076
  69.2 9.6 %collective-permute-start.13 = (f32[24,256]{1,0:T(8,128)S(1)}, f32[24,256]{1,0:T(8,128)S(1)}, u32[]{:S(2)}, u32[]{:S(2)}) collective-permute-start(f32[24,256]{1,0:T(8,128)S(1)} %shard_map.90.own), channel_id=1, source_target_pairs={{0,64},{64,128},{128,192},{192,0},{1,65},{65,129},{129,193},{193,1... | collective-permute-start | bytes 73736 | tf_op jit(solution)/shard_map/ppermute | solution.py:275
  72.3 6.6 %collective-permute-start.14 = (f32[24,256]{1,0:T(8,128)S(1)}, f32[24,256]{1,0:T(8,128)S(1)}, u32[]{:S(2)}, u32[]{:S(2)}) collective-permute-start(f32[24,256]{1,0:T(8,128)S(1)} %shard_map.90.own), channel_id=1, source_target_pairs={{0,192},{64,0},{128,64},{192,128},{1,193},{65,1},{129,65},{193,129... | collective-permute-start | bytes 73736 | tf_op jit(solution)/shard_map/ppermute | solution.py:275
  74.5 6.6 %collective-permute-start.15 = (f32[24,256]{1,0:T(8,128)S(1)}, f32[24,256]{1,0:T(8,128)S(1)}, u32[]{:S(2)}, u32[]{:S(2)}) collective-permute-start(f32[24,256]{1,0:T(8,128)S(1)} %shard_map.90.own), channel_id=1, source_target_pairs={{0,128},{64,192},{128,0},{192,64},{1,129},{65,193},{129,1},{193,65... | collective-permute-start | bytes 73736 | tf_op jit(solution)/shard_map/ppermute | solution.py:275
  92.9 8.4 %collective-permute-start.16 = (bf16[192,512]{1,0:T(8,128)(2,1)S(1)}, bf16[192,512]{1,0:T(8,128)(2,1)S(1)}, u32[]{:S(2)}, u32[]{:S(2)}) collective-permute-start(bf16[192,512]{1,0:T(8,128)(2,1)S(1)} %get-tuple-element.34), channel_id=1, source_target_pairs={{0,32},{32,0},{1,33},{33,1},{2,34},{34,2},{3,35},{35,3},{4,36},{36... | collective-permute-start | bytes 589832 | tf_op jit(solution)/shard_map/ppermute | solution.py:286
  93.8 15.1 %collective-permute-start.18 = (bf16[192,512]{1,0:T(8,128)(2,1)S(1)}, bf16[192,512]{1,0:T(8,128)(2,1)S(1)}, u32[]{:S(2)}, u32[]{:S(2)}) collective-permute-start(bf16[192,512]{1,0:T(8,128)(2,1)S(1)} %get-tuple-element.37), channel_id=1, source_target_pairs={{0,33},{1,32},{32,1},{33,0},{2,35},{3,34},{34,3},{35,2},{4,37},{5,... | collective-permute-start | bytes 589832 | tf_op jit(solution)/shard_map/ppermute | solution.py:287
  101.3 7.6 %collective-permute-start.17 = (bf16[192,512]{1,0:T(8,128)(2,1)S(1)}, bf16[192,512]{1,0:T(8,128)(2,1)S(1)}, u32[]{:S(2)}, u32[]{:S(2)}) collective-permute-start(bf16[192,512]{1,0:T(8,128)(2,1)S(1)} %get-tuple-element.35), channel_id=1, source_target_pairs={{0,1},{1,0},{2,3},{3,2},{4,5},{5,4},{6,7},{7,6},{8,9},{9,8},{10,11... | collective-permute-start | bytes 589832 | tf_op jit(solution)/shard_map/ppermute | solution.py:289

commit v5 on v4

--- a/solution.py
+++ b/solution.py
@@ -52,22 +52,20 @@
     return jnp.concatenate([top, bottom], axis=0)
 
 
-def join_kernel(own, before, after, across, near, far):
-    near[:256, :] = own[...]
-    near[256:, :] = before[...]
-    far[:256, :] = after[...]
-    far[256:, :] = across[...]
+def join_kernel(top, bottom, out):
+    out[:256, :] = top[...]
+    out[256:, :] = bottom[...]
 
 
 def gather_weights(mine, theirs):
     mate = lax.ppermute(theirs, "core", SWAP)
     own = join(mine, mate)
     before, after = send(own, 1, True), send(own, -1, True)
-    firsts = before, after, send(own, 2, True)
-    before, after, across = lax.optimization_barrier(firsts)
-    near, far = call(join_kernel, shapes(*[((512, 768), bf16)] * 2), 0, 4, 0, 3 << 20)(
-        own, before, after, across
-    )
+    across = send(own, 2, True)
+    pair = lambda top, bottom: call(
+        join_kernel, jax.ShapeDtypeStruct((512, 768), bf16), 0, 2, 0, 3 << 19
+    )(top, bottom)
+    near, far = pair(own, before), pair(after, across)
     near_before, far_after = send(near, 1, False), send(far, -1, False)
     far_before, near_after = send(far, 1, False), send(near, -1, False)
     near_across, far_across = send(near_before, 1, False), send(far_after, -1, False)
@@ -254,7 +252,7 @@
 
     z_mate = lax.ppermute(context, "zi", SWAP)
     core_mate = lax.ppermute(context, "core", SWAP)
-    z_mate, _ = lax.optimization_barrier((z_mate, w_own[1]))
+    z_mate, _ = lax.optimization_barrier((z_mate, w_own[0]))
     zc_mate = lax.ppermute(z_mate, "core", SWAP)
     rows = 4 * BLK + QTOK
     x_own, x_before, x_after, x_across = call(

time: 111 us -> 110 us (level)
  waiting for transfers between devices: 23.4 us -> 20.1 us
  starting transfers between devices: 42.2 us -> 43.5 us
    ppermute x9, waiting for transfers between devices: 17.9 us -> 13.9 us  [send(): return lax.ppermute(rows, YXC, torus_pairs(step, first))]
    ppermute x9, starting transfers between devices: 12.5 us -> 13.7 us  [send(): return lax.ppermute(rows, YXC, torus_pairs(step, first))]
  transfers between devices with their start and end apart: 19 -> 19, of which waited for: 10 -> 11; matrix products, arithmetic and copies ran while one was open for 2% -> 2% of each run, Pallas kernels for 9% -> 10%
where the time goes in v5:
time: 110 us
  starting transfers between devices  43.5 us (40%)
  blocking collectives  23.9 us (22%)
  waiting for transfers between devices  20.1 us (18%)
  Pallas kernels  18.6 us (17%)
  local copies, waits for them, and re-layouts  2.97 us (3%)
    all_to_all x1, blocking collectives, per_device(): gathered = lax.all_to_all(packed, PLANE, 0, 0, tiled=True)  14.3 us
    ppermute x9, waiting for transfers between devices, send(): return lax.ppermute(rows, YXC, torus_pairs(step, first))  13.9 us
    ppermute x9, starting transfers between devices, send(): return lax.ppermute(rows, YXC, torus_pairs(step, first))  13.7 us
    ppermute x3, starting transfers between devices, per_device(): lax.ppermute(merged, 'zg', [(i, (i + k) % 4) for i in range(4)])  9.65 us
    all_to_all x1, blocking collectives, per_device(): lax.all_to_all(jnp.broadcast_to(final[None], (CHIPS, *final.shape)), PLAN...  9.58 us
    ppermute x1, starting transfers between devices, per_device(): lax.ppermute(pieces[3], ('zi', 'core'), [(i, 3 - i) for i in range(4)])  7.45 us
    ppermute x1, starting transfers between devices, per_device(): received = (pieces[0], lax.ppermute(to_core, 'core', SWAP), from_z, from_zc)  5.79 us
    pallas_call x1, Pallas kernels, per_device(): call(project_kernel, jax.ShapeDtypeStruct((rows, 768), f32), 0, 9, 27 <<...  5.23 us
  transfers between devices with their start and end apart: 19, of which 11 were waited for; matrix products, arithmetic and copies ran while one was open for 2% of the time, Pallas kernels for 10%

profile of v5, /device:TPU:1, one launch (start us, length us, event | category | flops | bytes accessed | tf_op | source)
XLA Modules:
  0.0 109.8 jit_solution(16036028637816648006)
XLA Ops:
  0.6 2.6 %collective-permute-start.1 = (bf16[128,4096]{1,0:T(8,128)(2,1)}, bf16[128,4096]{1,0:T(8,128)(2,1)S(1)}, u32[]{:S(2)}, u32[]{:S(2)}) collective-permute-start(bf16[128,4096]{1,0:T(8,128)(2,1)} %own.1), channel_id=1, source_target_pairs={{0,32},{32,0},{1,33},{33,1},{2,34},{34,2},{3,35},{35,3},{4,36},{36... | collective-permute-start | bytes 3145736 | tf_op jit(solution)/shard_map/ppermute | solution.py:253
  5.0 1.1 collective-permute-start.2
  7.2 1.3 %collective-permute-start.3 = (bf16[256,768]{1,0:T(8,128)(2,1)S(1)}, bf16[256,768]{1,0:T(8,128)(2,1)S(1)}, u32[]{:S(2)}, u32[]{:S(2)}) collective-permute-start(bf16[256,768]{1,0:T(8,128)(2,1)S(1)} %pad_maximum_fusion.top), channel_id=1, source_target_pairs={{0,2},{1,9},{2,4},{3,11},{4,6},{5,13},{6,0},{7,15},{8,10},{9,17},{... | collective-permute-start | bytes 1179656 | tf_op jit(solution)/shard_map/ppermute | solution.py:48
  8.6 1.5 %collective-permute-start.5 = (bf16[256,768]{1,0:T(8,128)(2,1)S(1)}, bf16[256,768]{1,0:T(8,128)(2,1)S(1)}, u32[]{:S(2)}, u32[]{:S(2)}) collective-permute-start(bf16[256,768]{1,0:T(8,128)(2,1)S(1)} %pad_maximum_fusion.top), channel_id=1, source_target_pairs={{0,6},{1,25},{2,0},{3,27},{4,2},{5,29},{6,4},{7,31},{8,14},{9,1},{... | collective-permute-start | bytes 1179656 | tf_op jit(solution)/shard_map/ppermute | solution.py:48
  10.1 1.6 %collective-permute-start.6 = (bf16[256,768]{1,0:T(8,128)(2,1)S(1)}, bf16[256,768]{1,0:T(8,128)(2,1)S(1)}, u32[]{:S(2)}, u32[]{:S(2)}) collective-permute-start(bf16[256,768]{1,0:T(8,128)(2,1)S(1)} %pad_maximum_fusion.top), channel_id=1, source_target_pairs={{0,4},{1,17},{2,6},{3,19},{4,0},{5,21},{6,2},{7,23},{8,12},{9,25},... | collective-permute-start | bytes 1179656 | tf_op jit(solution)/shard_map/ppermute | solution.py:48
  11.6 3.8 %collective-permute-done.3.bottom = bf16[256,768]{1,0:T(8,128)(2,1)S(1)} collective-permute-done((bf16[256,768]{1,0:T(8,128)(2,1)S(1)}, bf16[256,768]{1,0:T(8,128)(2,1)S(1)}, u32[]{:S(2)}, u32[]{:S(2)}) %collective-permute-start.3) | collective-permute-done | bytes 393248 | tf_op jit(solution)/shard_map/ppermute | solution.py:48
  17.3 1.7 %collective-permute-done.5.top = bf16[256,768]{1,0:T(8,128)(2,1)S(1)} collective-permute-done((bf16[256,768]{1,0:T(8,128)(2,1)S(1)}, bf16[256,768]{1,0:T(8,128)(2,1)S(1)}, u32[]{:S(2)}, u32[]{:S(2)}) %collective-permute-start.5) | collective-permute-done | bytes 393248 | tf_op jit(solution)/shard_map/ppermute | solution.py:48
  19.0 1.8 %collective-permute-done.6.bottom = bf16[256,768]{1,0:T(8,128)(2,1)S(1)} collective-permute-done((bf16[256,768]{1,0:T(8,128)(2,1)S(1)}, bf16[256,768]{1,0:T(8,128)(2,1)S(1)}, u32[]{:S(2)}, u32[]{:S(2)}) %collective-permute-start.6) | collective-permute-done | bytes 393248 | tf_op jit(solution)/shard_map/ppermute | solution.py:48
  21.8 2.3 %collective-permute-start.10 = (bf16[512,768]{1,0:T(8,128)(2,1)}, bf16[512,768]{1,0:T(8,128)(2,1)}, u32[]{:S(2)}, u32[]{:S(2)}) collective-permute-start(bf16[512,768]{1,0:T(8,128)(2,1)} %shard_map.88.refs_1_), channel_id=1, source_target_pairs={{0,24},{1,7},{2,26},{3,1},{4,28},{5,3},{6,30},{7,5},{8,0},{9,15},{... | collective-permute-start | bytes 2359304 | tf_op jit(solution)/shard_map/ppermute | solution.py:48
  24.1 1.3 %collective-permute-done.1.z_mate = bf16[128,4096]{1,0:T(8,128)(2,1)S(1)} collective-permute-done((bf16[128,4096]{1,0:T(8,128)(2,1)}, bf16[128,4096]{1,0:T(8,128)(2,1)S(1)}, u32[]{:S(2)}, u32[]{:S(2)}) %collective-permute-start.1) | collective-permute-done | bytes 1048608 | tf_op jit(solution)/shard_map/ppermute | solution.py:253
  25.3 2.2 %collective-permute-start.4 = (bf16[128,4096]{1,0:T(8,128)(2,1)S(1)}, bf16[128,4096]{1,0:T(8,128)(2,1)}, u32[]{:S(2)}, u32[]{:S(2)}) collective-permute-start(bf16[128,4096]{1,0:T(8,128)(2,1)S(1)} %collective-permute-done.1.z_mate), channel_id=1, source_target_pairs={{0,1},{1,0},{2,3},{3,2},{4,5},{5,4},{6,7},{7,6},{8,9},{9,8},{10,11... | collective-permute-start | bytes 3145736 | tf_op jit(solution)/shard_map/ppermute | solution.py:256
  27.5 1.2 %collective-permute-start.8 = (bf16[512,768]{1,0:T(8,128)(2,1)}, bf16[512,768]{1,0:T(8,128)(2,1)}, u32[]{:S(2)}, u32[]{:S(2)}) collective-permute-start(bf16[512,768]{1,0:T(8,128)(2,1)} %shard_map.88.refs_1_), channel_id=1, source_target_pairs={{0,8},{1,3},{2,10},{3,5},{4,12},{5,7},{6,14},{7,1},{8,16},{9,11},{... | collective-permute-start | bytes 2359304 | tf_op jit(solution)/shard_map/ppermute | solution.py:48
  28.7 1.5 %collective-permute-start.9 = (bf16[512,768]{1,0:T(8,128)(2,1)}, bf16[512,768]{1,0:T(8,128)(2,1)}, u32[]{:S(2)}, u32[]{:S(2)}) collective-permute-start(bf16[512,768]{1,0:T(8,128)(2,1)} %shard_map.86.refs_0_), channel_id=1, source_target_pairs={{0,24},{1,7},{2,26},{3,1},{4,28},{5,3},{6,30},{7,5},{8,0},{9,15},{... | collective-permute-start | bytes 2359304 | tf_op jit(solution)/shard_map/ppermute | solution.py:48
  30.2 3.1 %collective-permute-done.10.refs_5_ = bf16[512,768]{1,0:T(8,128)(2,1)} collective-permute-done((bf16[512,768]{1,0:T(8,128)(2,1)}, bf16[512,768]{1,0:T(8,128)(2,1)}, u32[]{:S(2)}, u32[]{:S(2)}) %collective-permute-start.10) | collective-permute-done | bytes 786464 | tf_op jit(solution)/shard_map/ppermute | solution.py:48
  33.3 3.4 %collective-permute-start.12 = (bf16[512,768]{1,0:T(8,128)(2,1)}, bf16[512,768]{1,0:T(8,128)(2,1)}, u32[]{:S(2)}, u32[]{:S(2)}) collective-permute-start(bf16[512,768]{1,0:T(8,128)(2,1)} %collective-permute-done.10.refs_5_), channel_id=1, source_target_pairs={{0,24},{1,7},{2,26},{3,1},{4,28},{5,3},{6,30},{7,5},{8,0},{9,15},{... | collective-permute-start | bytes 2359304 | tf_op jit(solution)/shard_map/ppermute | solution.py:48
  36.9 1.0 copy-done.1
  37.9 3.6 %shard_map.87 = (bf16[576,1024]{1,0:T(8,128)(2,1)S(1)}, bf16[576,1024]{1,0:T(8,128)(2,1)S(1)}, bf16[576,1024]{1,0:T(8,128)(2,1)S(1)}, bf16[576,1024]{1,0:T(8,128)(2,1)S(1)}) custom-call(s32[8]{0:T(128)S(1)} %stack.39.place, bf16[128,4096]{1,0:T(8,128)(2,1)S(1)} %copy-done, bf16[128,4096]{1,0:T(8,128)(2,1)S(1)} %collective-permute-done.core_mate, ...), custom_call_target="tpu_custom_call" | custom-call | flops 16777216 | bytes 10485760 | tf_op jit(solution)/shard_map/pallas_call | solution.py:258
  41.8 5.2 %shard_map.89.total = f32[576,768]{1,0:T(8,128)S(1)} custom-call(bf16[576,1024]{1,0:T(8,128)(2,1)S(1)} %get-tuple-element.17.own, bf16[576,1024]{1,0:T(8,128)(2,1)S(1)} %get-tuple-element.18.before, bf16[576,1024]{1,0:T(8,128)(2,1)S(1)} %get-tuple-element.19.after, bf16[512,768]{1,0:T(8,128)(2,1)} %shard_map.86.refs_0_, bf16[512,768]{1,0:T(8,128)(2,1)} %shard_map.88.refs_1_, ...), custom_call_target="tpu_custom_call" | custom-call | flops 3623878656 | bytes 12582912 | tf_op jit(solution)/shard_map/pallas_call | solution.py:262
  47.0 1.6 %collective-permute-done.11.near = bf16[512,768]{1,0:T(8,128)(2,1)} collective-permute-done((bf16[512,768]{1,0:T(8,128)(2,1)}, bf16[512,768]{1,0:T(8,128)(2,1)}, u32[]{:S(2)}, u32[]{:S(2)}) %collective-permute-start.11) | collective-permute-done | bytes 786464 | tf_op jit(solution)/shard_map/ppermute | solution.py:48
  48.6 1.6 %collective-permute-done.12.far = bf16[512,768]{1,0:T(8,128)(2,1)} collective-permute-done((bf16[512,768]{1,0:T(8,128)(2,1)}, bf16[512,768]{1,0:T(8,128)(2,1)}, u32[]{:S(2)}, u32[]{:S(2)}) %collective-permute-start.12) | collective-permute-done | bytes 786464 | tf_op jit(solution)/shard_map/ppermute | solution.py:48
  50.2 4.0 %shard_map.90 = (bf16[576,768]{1,0:T(8,128)(2,1)S(1)}, f32[16,24,256]{2,1,0:T(8,128)S(1)}) custom-call(s32[8]{0:T(128)S(1)} %stack.39.place, s32[256]{0:T(256)S(1)} %copy-done.3, bf16[576,1024]{1,0:T(8,128)(2,1)S(1)} %get-tuple-element.16.across, f32[576,768]{1,0:T(8,128)S(1)} %shard_map.89.total, bf16[512,768]{1,0:T(8,128)(2,1)} %collective-permute-done.11.near, ...), custom_call_target="tpu_custom_call" | custom-call | flops 1207959552 | bytes 6291456 | tf_op jit(solution)/shard_map/pallas_call | solution.py:265
  54.2 14.3 %all_to_all.10.parts = f32[16,24,256]{2,1,0:T(8,128)S(1)} all-to-all(f32[16,24,256]{2,1,0:T(8,128)S(1)} %get-tuple-element.21), channel_id=1, replica_groups=mesh['zg'=4,'zi'=2,'y'=4,'x'=4,'core'=2] {'y','x'}, dimensions={0} | all-to-all | bytes 786432 | tf_op jit(solution)/shard_map/all_to_all | solution.py:269
  68.7 3.0 %collective-permute-start.13 = (f32[24,256]{1,0:T(8,128)S(1)}, f32[24,256]{1,0:T(8,128)S(1)}, u32[]{:S(2)}, u32[]{:S(2)}) collective-permute-start(f32[24,256]{1,0:T(8,128)S(1)} %shard_map.91.own), channel_id=1, source_target_pairs={{0,64},{64,128},{128,192},{192,0},{1,65},{65,129},{129,193},{193,1... | collective-permute-start | bytes 73736 | tf_op jit(solution)/shard_map/ppermute | solution.py:273
  71.7 2.2 %collective-permute-start.14 = (f32[24,256]{1,0:T(8,128)S(1)}, f32[24,256]{1,0:T(8,128)S(1)}, u32[]{:S(2)}, u32[]{:S(2)}) collective-permute-start(f32[24,256]{1,0:T(8,128)S(1)} %shard_map.91.own), channel_id=1, source_target_pairs={{0,192},{64,0},{128,64},{192,128},{1,193},{65,1},{129,65},{193,129... | collective-permute-start | bytes 73736 | tf_op jit(solution)/shard_map/ppermute | solution.py:273
  74.0 4.4 %collective-permute-start.15 = (f32[24,256]{1,0:T(8,128)S(1)}, f32[24,256]{1,0:T(8,128)S(1)}, u32[]{:S(2)}, u32[]{:S(2)}) collective-permute-start(f32[24,256]{1,0:T(8,128)S(1)} %shard_map.91.own), channel_id=1, source_target_pairs={{0,128},{64,192},{128,0},{192,64},{1,129},{65,193},{129,1},{193,65... | collective-permute-start | bytes 73736 | tf_op jit(solution)/shard_map/ppermute | solution.py:273
  78.4 2.2 %collective-permute-done.15.across = f32[24,256]{1,0:T(8,128)S(1)} collective-permute-done((f32[24,256]{1,0:T(8,128)S(1)}, f32[24,256]{1,0:T(8,128)S(1)}, u32[]{:S(2)}, u32[]{:S(2)}) %collective-permute-start.15) | collective-permute-done | bytes 24608 | tf_op jit(solution)/shard_map/ppermute | solution.py:273
  81.3 9.6 %all_to_all.11.shared = bf16[16,32,128]{2,1,0:T(8,128)(2,1)S(1)} all-to-all(bf16[16,32,128]{2,1,0:T(8,128)(2,1)S(1)} %broadcast_in_dim.10), channel_id=1, replica_groups=mesh['zg'=4,'zi'=2,'y'=4,'x'=4,'core'=2] {'y','x'}, dimensions={0} | all-to-all | bytes 262144 | tf_op jit(solution)/shard_map/all_to_all | solution.py:278
  90.9 1.5 %shard_map.93 = (bf16[192,512]{1,0:T(8,128)(2,1)S(1)}, bf16[192,512]{1,0:T(8,128)(2,1)S(1)}, bf16[192,512]{1,0:T(8,128)(2,1)S(1)}, bf16[192,512]{1,0:T(8,128)(2,1)S(1)}) custom-call(s32[8]{0:T(128)S(1)} %stack.39.place, s32[256]{0:T(256)S(1)} %copy-done.3, bf16[576,768]{1,0:T(8,128)(2,1)S(1)} %get-tuple-element.20.proj, ...), custom_call_target="tpu_custom_call" | custom-call | flops 536870912 | bytes 3145728 | tf_op jit(solution)/shard_map/pallas_call | solution.py:281
  93.3 7.5 %collective-permute-start.18 = (bf16[192,512]{1,0:T(8,128)(2,1)S(1)}, bf16[192,512]{1,0:T(8,128)(2,1)S(1)}, u32[]{:S(2)}, u32[]{:S(2)}) collective-permute-start(bf16[192,512]{1,0:T(8,128)(2,1)S(1)} %get-tuple-element.27), channel_id=1, source_target_pairs={{0,33},{1,32},{32,1},{33,0},{2,35},{3,34},{34,3},{35,2},{4,37},{5,... | collective-permute-start | bytes 589832 | tf_op jit(solution)/shard_map/ppermute | solution.py:285
  100.7 5.8 %collective-permute-start.17 = (bf16[192,512]{1,0:T(8,128)(2,1)S(1)}, bf16[192,512]{1,0:T(8,128)(2,1)S(1)}, u32[]{:S(2)}, u32[]{:S(2)}) collective-permute-start(bf16[192,512]{1,0:T(8,128)(2,1)S(1)} %get-tuple-element.25), channel_id=1, source_target_pairs={{0,1},{1,0},{2,3},{3,2},{4,5},{5,4},{6,7},{7,6},{8,9},{9,8},{10,11... | collective-permute-start | bytes 589832 | tf_op jit(solution)/shard_map/ppermute | solution.py:287
  106.5 1.8 %collective-permute-done.18.refs_3_ = bf16[192,512]{1,0:T(8,128)(2,1)S(1)} collective-permute-done((bf16[192,512]{1,0:T(8,128)(2,1)S(1)}, bf16[192,512]{1,0:T(8,128)(2,1)S(1)}, u32[]{:S(2)}, u32[]{:S(2)}) %collective-permute-start.18) | collective-permute-done | bytes 196640 | tf_op jit(solution)/shard_map/ppermute | solution.py:285
  108.3 1.5 %shard_map.94 = (bf16[128,2048]{1,0:T(8,128)(2,1)}, bf16[64,2048]{1,0:T(8,128)(2,1)}) custom-call(s32[8]{0:T(128)S(1)} %stack.39.place, bf16[192,512]{1,0:T(8,128)(2,1)S(1)} %get-tuple-element.22.refs_0_, bf16[192,512]{1,0:T(8,128)(2,1)S(1)} %collective-permute-done.17.refs_1_, bf16[192,512]{1,0:T(8,128)(2,1)S(1)} %collective-permute-done.16.refs_2_, ...), custom_call_target="tpu_custom_call" | custom-call | bytes 2097152 | tf_op jit(solution)/shard_map/pallas_call | solution.py:288
  (32 shorter events, 7.9 us)
Async XLA Ops:
  0.6 5.5 %copy-start = (bf16[128,4096]{1,0:T(8,128)(2,1)S(1)}, bf16[128,4096]{1,0:T(8,128)(2,1)}, u32[]{:S(2)}) copy-start(bf16[128,4096]{1,0:T(8,128)(2,1)} %own.1) | copy-start | bytes 3145732
  0.6 24.7 %collective-permute-start.1 = (bf16[128,4096]{1,0:T(8,128)(2,1)}, bf16[128,4096]{1,0:T(8,128)(2,1)S(1)}, u32[]{:S(2)}, u32[]{:S(2)}) collective-permute-start(bf16[128,4096]{1,0:T(8,128)(2,1)} %own.1), channel_id=1, source_target_pairs={{0,32},{32,0},{1,33},{33,1},{2,34},{34,2},{3,35},{35,3},{4,36},{36... | collective-permute-start | bytes 3145736 | tf_op jit(solution)/shard_map/ppermute | solution.py:253
  5.0 2.1 %collective-permute-start.2 = (bf16[128,768]{1,0:T(8,128)(2,1)S(1)}, bf16[128,768]{1,0:T(8,128)(2,1)S(1)}, u32[]{:S(2)}, u32[]{:S(2)}) collective-permute-start(bf16[128,768]{1,0:T(8,128)(2,1)S(1)} %pad_maximum_fusion.1), channel_id=1, source_target_pairs={{0,1},{1,0},{2,3},{3,2},{4,5},{5,4},{6,7},{7,6},{8,9},{9,8},{10,11... | collective-permute-start | bytes 589832 | tf_op jit(solution)/shard_map/ppermute | solution.py:61
  6.1 22.6 %collective-permute-start = (bf16[128,4096]{1,0:T(8,128)(2,1)S(1)}, bf16[128,4096]{1,0:T(8,128)(2,1)S(1)}, u32[]{:S(2)}, u32[]{:S(2)}) collective-permute-start(bf16[128,4096]{1,0:T(8,128)(2,1)S(1)} %copy-done), channel_id=1, source_target_pairs={{0,1},{1,0},{2,3},{3,2},{4,5},{5,4},{6,7},{7,6},{8,9},{9,8},{10,11... | collective-permute-start | bytes 3145736 | tf_op jit(solution)/shard_map/ppermute | solution.py:254
  7.2 8.2 %collective-permute-start.3 = (bf16[256,768]{1,0:T(8,128)(2,1)S(1)}, bf16[256,768]{1,0:T(8,128)(2,1)S(1)}, u32[]{:S(2)}, u32[]{:S(2)}) collective-permute-start(bf16[256,768]{1,0:T(8,128)(2,1)S(1)} %pad_maximum_fusion.top), channel_id=1, source_target_pairs={{0,2},{1,9},{2,4},{3,11},{4,6},{5,13},{6,0},{7,15},{8,10},{9,17},{... | collective-permute-start | bytes 1179656 | tf_op jit(solution)/shard_map/ppermute | solution.py:48
  8.6 10.5 %collective-permute-start.5 = (bf16[256,768]{1,0:T(8,128)(2,1)S(1)}, bf16[256,768]{1,0:T(8,128)(2,1)S(1)}, u32[]{:S(2)}, u32[]{:S(2)}) collective-permute-start(bf16[256,768]{1,0:T(8,128)(2,1)S(1)} %pad_maximum_fusion.top), channel_id=1, source_target_pairs={{0,6},{1,25},{2,0},{3,27},{4,2},{5,29},{6,4},{7,31},{8,14},{9,1},{... | collective-permute-start | bytes 1179656 | tf_op jit(solution)/shard_map/ppermute | solution.py:48
  10.1 10.8 %collective-permute-start.6 = (bf16[256,768]{1,0:T(8,128)(2,1)S(1)}, bf16[256,768]{1,0:T(8,128)(2,1)S(1)}, u32[]{:S(2)}, u32[]{:S(2)}) collective-permute-start(bf16[256,768]{1,0:T(8,128)(2,1)S(1)} %pad_maximum_fusion.top), channel_id=1, source_target_pairs={{0,4},{1,17},{2,6},{3,19},{4,0},{5,21},{6,2},{7,23},{8,12},{9,25},... | collective-permute-start | bytes 1179656 | tf_op jit(solution)/shard_map/ppermute | solution.py:48
  16.4 20.4 %copy-start.2 = (f32[4096]{0:T(1024)S(1)}, f32[4096]{0:T(1024)}, u32[]{:S(2)}) copy-start(f32[4096]{0:T(1024)} %param.9) | copy-start | bytes 49156
  16.4 13.8 %collective-permute-start.7 = (bf16[512,768]{1,0:T(8,128)(2,1)}, bf16[512,768]{1,0:T(8,128)(2,1)}, u32[]{:S(2)}, u32[]{:S(2)}) collective-permute-start(bf16[512,768]{1,0:T(8,128)(2,1)} %shard_map.86.refs_0_), channel_id=1, source_target_pairs={{0,8},{1,3},{2,10},{3,5},{4,12},{5,7},{6,14},{7,1},{8,16},{9,11},{... | collective-permute-start | bytes 2359304 | tf_op jit(solution)/shard_map/ppermute | solution.py:48
  21.8 11.6 %collective-permute-start.10 = (bf16[512,768]{1,0:T(8,128)(2,1)}, bf16[512,768]{1,0:T(8,128)(2,1)}, u32[]{:S(2)}, u32[]{:S(2)}) collective-permute-start(bf16[512,768]{1,0:T(8,128)(2,1)} %shard_map.88.refs_1_), channel_id=1, source_target_pairs={{0,24},{1,7},{2,26},{3,1},{4,28},{5,3},{6,30},{7,5},{8,0},{9,15},{... | collective-permute-start | bytes 2359304 | tf_op jit(solution)/shard_map/ppermute | solution.py:48
  25.3 11.5 %collective-permute-start.4 = (bf16[128,4096]{1,0:T(8,128)(2,1)S(1)}, bf16[128,4096]{1,0:T(8,128)(2,1)}, u32[]{:S(2)}, u32[]{:S(2)}) collective-permute-start(bf16[128,4096]{1,0:T(8,128)(2,1)S(1)} %collective-permute-done.1.z_mate), channel_id=1, source_target_pairs={{0,1},{1,0},{2,3},{3,2},{4,5},{5,4},{6,7},{7,6},{8,9},{9,8},{10,11... | collective-permute-start | bytes 3145736 | tf_op jit(solution)/shard_map/ppermute | solution.py:256
  27.5 14.0 %collective-permute-start.8 = (bf16[512,768]{1,0:T(8,128)(2,1)}, bf16[512,768]{1,0:T(8,128)(2,1)}, u32[]{:S(2)}, u32[]{:S(2)}) collective-permute-start(bf16[512,768]{1,0:T(8,128)(2,1)} %shard_map.88.refs_1_), channel_id=1, source_target_pairs={{0,8},{1,3},{2,10},{3,5},{4,12},{5,7},{6,14},{7,1},{8,16},{9,11},{... | collective-permute-start | bytes 2359304 | tf_op jit(solution)/shard_map/ppermute | solution.py:48
  28.7 13.0 %collective-permute-start.9 = (bf16[512,768]{1,0:T(8,128)(2,1)}, bf16[512,768]{1,0:T(8,128)(2,1)}, u32[]{:S(2)}, u32[]{:S(2)}) collective-permute-start(bf16[512,768]{1,0:T(8,128)(2,1)} %shard_map.86.refs_0_), channel_id=1, source_target_pairs={{0,24},{1,7},{2,26},{3,1},{4,28},{5,3},{6,30},{7,5},{8,0},{9,15},{... | collective-permute-start | bytes 2359304 | tf_op jit(solution)/shard_map/ppermute | solution.py:48
  30.2 18.4 %collective-permute-start.11 = (bf16[512,768]{1,0:T(8,128)(2,1)}, bf16[512,768]{1,0:T(8,128)(2,1)}, u32[]{:S(2)}, u32[]{:S(2)}) collective-permute-start(bf16[512,768]{1,0:T(8,128)(2,1)} %collective-permute-done.7.refs_2_), channel_id=1, source_target_pairs={{0,8},{1,3},{2,10},{3,5},{4,12},{5,7},{6,14},{7,1},{8,16},{9,11},{... | collective-permute-start | bytes 2359304 | tf_op jit(solution)/shard_map/ppermute | solution.py:48
  33.3 16.9 %collective-permute-start.12 = (bf16[512,768]{1,0:T(8,128)(2,1)}, bf16[512,768]{1,0:T(8,128)(2,1)}, u32[]{:S(2)}, u32[]{:S(2)}) collective-permute-start(bf16[512,768]{1,0:T(8,128)(2,1)} %collective-permute-done.10.refs_5_), channel_id=1, source_target_pairs={{0,24},{1,7},{2,26},{3,1},{4,28},{5,3},{6,30},{7,5},{8,0},{9,15},{... | collective-permute-start | bytes 2359304 | tf_op jit(solution)/shard_map/ppermute | solution.py:48
  36.8 1.0 copy-start.1
  41.8 8.4 %copy-start.3 = (s32[256]{0:T(256)S(1)}, s32[256]{0:T(256)}, u32[]{:S(2)}) copy-start(s32[256]{0:T(256)} %lengths.3) | copy-start | bytes 3076
  68.7 9.7 %collective-permute-start.13 = (f32[24,256]{1,0:T(8,128)S(1)}, f32[24,256]{1,0:T(8,128)S(1)}, u32[]{:S(2)}, u32[]{:S(2)}) collective-permute-start(f32[24,256]{1,0:T(8,128)S(1)} %shard_map.91.own), channel_id=1, source_target_pairs={{0,64},{64,128},{128,192},{192,0},{1,65},{65,129},{129,193},{193,1... | collective-permute-start | bytes 73736 | tf_op jit(solution)/shard_map/ppermute | solution.py:273
  71.7 6.6 %collective-permute-start.14 = (f32[24,256]{1,0:T(8,128)S(1)}, f32[24,256]{1,0:T(8,128)S(1)}, u32[]{:S(2)}, u32[]{:S(2)}) collective-permute-start(f32[24,256]{1,0:T(8,128)S(1)} %shard_map.91.own), channel_id=1, source_target_pairs={{0,192},{64,0},{128,64},{192,128},{1,193},{65,1},{129,65},{193,129... | collective-permute-start | bytes 73736 | tf_op jit(solution)/shard_map/ppermute | solution.py:273
  74.0 6.6 %collective-permute-start.15 = (f32[24,256]{1,0:T(8,128)S(1)}, f32[24,256]{1,0:T(8,128)S(1)}, u32[]{:S(2)}, u32[]{:S(2)}) collective-permute-start(f32[24,256]{1,0:T(8,128)S(1)} %shard_map.91.own), channel_id=1, source_target_pairs={{0,128},{64,192},{128,0},{192,64},{1,129},{65,193},{129,1},{193,65... | collective-permute-start | bytes 73736 | tf_op jit(solution)/shard_map/ppermute | solution.py:273
  92.4 8.4 %collective-permute-start.16 = (bf16[192,512]{1,0:T(8,128)(2,1)S(1)}, bf16[192,512]{1,0:T(8,128)(2,1)S(1)}, u32[]{:S(2)}, u32[]{:S(2)}) collective-permute-start(bf16[192,512]{1,0:T(8,128)(2,1)S(1)} %get-tuple-element.24), channel_id=1, source_target_pairs={{0,32},{32,0},{1,33},{33,1},{2,34},{34,2},{3,35},{35,3},{4,36},{36... | collective-permute-start | bytes 589832 | tf_op jit(solution)/shard_map/ppermute | solution.py:284
  93.3 15.0 %collective-permute-start.18 = (bf16[192,512]{1,0:T(8,128)(2,1)S(1)}, bf16[192,512]{1,0:T(8,128)(2,1)S(1)}, u32[]{:S(2)}, u32[]{:S(2)}) collective-permute-start(bf16[192,512]{1,0:T(8,128)(2,1)S(1)} %get-tuple-element.27), channel_id=1, source_target_pairs={{0,33},{1,32},{32,1},{33,0},{2,35},{3,34},{34,3},{35,2},{4,37},{5,... | collective-permute-start | bytes 589832 | tf_op jit(solution)/shard_map/ppermute | solution.py:285
  100.7 7.6 %collective-permute-start.17 = (bf16[192,512]{1,0:T(8,128)(2,1)S(1)}, bf16[192,512]{1,0:T(8,128)(2,1)S(1)}, u32[]{:S(2)}, u32[]{:S(2)}) collective-permute-start(bf16[192,512]{1,0:T(8,128)(2,1)S(1)} %get-tuple-element.25), channel_id=1, source_target_pairs={{0,1},{1,0},{2,3},{3,2},{4,5},{5,4},{6,7},{7,6},{8,9},{9,8},{10,11... | collective-permute-start | bytes 589832 | tf_op jit(solution)/shard_map/ppermute | solution.py:287

commit v6 on v5

--- a/solution.py
+++ b/solution.py
@@ -171,13 +171,12 @@
 def merge_deep_kernel(place, own, before, after, across, out):
     refs = (own, before, after, across)
     _, total, numerator = merge([(r[:SHARE, :HEAD_SIZE], r[:SHARE, HEAD_SIZE:]) for r in refs])
-    out[:SHARE, :] = numerator / total
     zg = place[6]
     anchor = own[SHARE:, :]
     for source, ref in ((1, before), (3, after), (2, across)):
         anchor = jnp.where(zg == source, ref[SHARE:, :], anchor)
-    out[SHARE : SHARE + ANCHOR_SHARE, :] = anchor[:, :HEAD_SIZE]
-    out[SHARE + ANCHOR_SHARE :, :] = anchor[:, HEAD_SIZE:]
+    parts = [numerator / total, anchor[:, :HEAD_SIZE], anchor[:, HEAD_SIZE:]]
+    out[...] = jnp.concatenate(parts, axis=0).astype(bf16)
 
 
 def block_kernel(place, lengths, proj, shared, *outs):
@@ -273,8 +272,8 @@
     deep = lambda k: lax.ppermute(merged, "zg", [(i, (i + k) % 4) for i in range(4)])
     final = call(
         merge_deep_kernel,
-        jax.ShapeDtypeStruct((SHARE + 2 * ANCHOR_SHARE, HEAD_SIZE), f32), 1, 4, 1 << 20, 1 << 17,
-    )(place, merged, deep(1), deep(-1), deep(2)).astype(bf16)
+        jax.ShapeDtypeStruct((SHARE + 2 * ANCHOR_SHARE, HEAD_SIZE), bf16), 1, 4, 1 << 20, 1 << 17,
+    )(place, merged, deep(1), deep(-1), deep(2))
     shared = lax.all_to_all(
         jnp.broadcast_to(final[None], (CHIPS, *final.shape)), PLANE, 0, 0, tiled=True
     )

time: 110 us -> 110 us (level)
  no operation moved by 1% of the time
where the time goes in v6:
time: 110 us
  starting transfers between devices  43.5 us (40%)
  blocking collectives  23.9 us (22%)
  waiting for transfers between devices  20.1 us (18%)
  Pallas kernels  18.6 us (17%)
  local copies, waits for them, and re-layouts  2.97 us (3%)
    all_to_all x1, blocking collectives, per_device(): gathered = lax.all_to_all(packed, PLANE, 0, 0, tiled=True)  14.3 us
    ppermute x9, waiting for transfers between devices, send(): return lax.ppermute(rows, YXC, torus_pairs(step, first))  13.9 us
    ppermute x9, starting transfers between devices, send(): return lax.ppermute(rows, YXC, torus_pairs(step, first))  13.7 us
    ppermute x3, starting transfers between devices, per_device(): lax.ppermute(merged, 'zg', [(i, (i + k) % 4) for i in range(4)])  9.65 us
    all_to_all x1, blocking collectives, per_device(): lax.all_to_all(jnp.broadcast_to(final[None], (CHIPS, *final.shape)), PLAN...  9.58 us
    ppermute x1, starting transfers between devices, per_device(): lax.ppermute(pieces[3], ('zi', 'core'), [(i, 3 - i) for i in range(4)])  7.45 us
    ppermute x1, starting transfers between devices, per_device(): received = (pieces[0], lax.ppermute(to_core, 'core', SWAP), from_z, from_zc)  5.79 us
    pallas_call x1, Pallas kernels, per_device(): call(project_kernel, jax.ShapeDtypeStruct((rows, 768), f32), 0, 9, 27 <<...  5.23 us
  transfers between devices with their start and end apart: 19, of which 11 were waited for; matrix products, arithmetic and copies ran while one was open for 2% of the time, Pallas kernels for 10%

profile of v6, /device:TPU:1, one launch (start us, length us, event | category | flops | bytes accessed | tf_op | source)
XLA Modules:
  0.0 109.8 jit_solution(13112371644204791121)
XLA Ops:
  0.6 2.6 %collective-permute-start.1 = (bf16[128,4096]{1,0:T(8,128)(2,1)}, bf16[128,4096]{1,0:T(8,128)(2,1)S(1)}, u32[]{:S(2)}, u32[]{:S(2)}) collective-permute-start(bf16[128,4096]{1,0:T(8,128)(2,1)} %own.1), channel_id=1, source_target_pairs={{0,32},{32,0},{1,33},{33,1},{2,34},{34,2},{3,35},{35,3},{4,36},{36... | collective-permute-start | bytes 3145736 | tf_op jit(solution)/shard_map/ppermute | solution.py:252
  5.0 1.1 collective-permute-start.2
  7.2 1.3 %collective-permute-start.3 = (bf16[256,768]{1,0:T(8,128)(2,1)S(1)}, bf16[256,768]{1,0:T(8,128)(2,1)S(1)}, u32[]{:S(2)}, u32[]{:S(2)}) collective-permute-start(bf16[256,768]{1,0:T(8,128)(2,1)S(1)} %pad_maximum_fusion.top), channel_id=1, source_target_pairs={{0,2},{1,9},{2,4},{3,11},{4,6},{5,13},{6,0},{7,15},{8,10},{9,17},{... | collective-permute-start | bytes 1179656 | tf_op jit(solution)/shard_map/ppermute | solution.py:48
  8.6 1.5 %collective-permute-start.5 = (bf16[256,768]{1,0:T(8,128)(2,1)S(1)}, bf16[256,768]{1,0:T(8,128)(2,1)S(1)}, u32[]{:S(2)}, u32[]{:S(2)}) collective-permute-start(bf16[256,768]{1,0:T(8,128)(2,1)S(1)} %pad_maximum_fusion.top), channel_id=1, source_target_pairs={{0,6},{1,25},{2,0},{3,27},{4,2},{5,29},{6,4},{7,31},{8,14},{9,1},{... | collective-permute-start | bytes 1179656 | tf_op jit(solution)/shard_map/ppermute | solution.py:48
  10.1 1.6 %collective-permute-start.6 = (bf16[256,768]{1,0:T(8,128)(2,1)S(1)}, bf16[256,768]{1,0:T(8,128)(2,1)S(1)}, u32[]{:S(2)}, u32[]{:S(2)}) collective-permute-start(bf16[256,768]{1,0:T(8,128)(2,1)S(1)} %pad_maximum_fusion.top), channel_id=1, source_target_pairs={{0,4},{1,17},{2,6},{3,19},{4,0},{5,21},{6,2},{7,23},{8,12},{9,25},... | collective-permute-start | bytes 1179656 | tf_op jit(solution)/shard_map/ppermute | solution.py:48
  11.6 3.8 %collective-permute-done.3.bottom = bf16[256,768]{1,0:T(8,128)(2,1)S(1)} collective-permute-done((bf16[256,768]{1,0:T(8,128)(2,1)S(1)}, bf16[256,768]{1,0:T(8,128)(2,1)S(1)}, u32[]{:S(2)}, u32[]{:S(2)}) %collective-permute-start.3) | collective-permute-done | bytes 393248 | tf_op jit(solution)/shard_map/ppermute | solution.py:48
  17.3 1.7 %collective-permute-done.5.top = bf16[256,768]{1,0:T(8,128)(2,1)S(1)} collective-permute-done((bf16[256,768]{1,0:T(8,128)(2,1)S(1)}, bf16[256,768]{1,0:T(8,128)(2,1)S(1)}, u32[]{:S(2)}, u32[]{:S(2)}) %collective-permute-start.5) | collective-permute-done | bytes 393248 | tf_op jit(solution)/shard_map/ppermute | solution.py:48
  19.0 1.8 %collective-permute-done.6.bottom = bf16[256,768]{1,0:T(8,128)(2,1)S(1)} collective-permute-done((bf16[256,768]{1,0:T(8,128)(2,1)S(1)}, bf16[256,768]{1,0:T(8,128)(2,1)S(1)}, u32[]{:S(2)}, u32[]{:S(2)}) %collective-permute-start.6) | collective-permute-done | bytes 393248 | tf_op jit(solution)/shard_map/ppermute | solution.py:48
  21.8 2.3 %collective-permute-start.10 = (bf16[512,768]{1,0:T(8,128)(2,1)}, bf16[512,768]{1,0:T(8,128)(2,1)}, u32[]{:S(2)}, u32[]{:S(2)}) collective-permute-start(bf16[512,768]{1,0:T(8,128)(2,1)} %shard_map.88.refs_1_), channel_id=1, source_target_pairs={{0,24},{1,7},{2,26},{3,1},{4,28},{5,3},{6,30},{7,5},{8,0},{9,15},{... | collective-permute-start | bytes 2359304 | tf_op jit(solution)/shard_map/ppermute | solution.py:48
  24.1 1.3 %collective-permute-done.1.z_mate = bf16[128,4096]{1,0:T(8,128)(2,1)S(1)} collective-permute-done((bf16[128,4096]{1,0:T(8,128)(2,1)}, bf16[128,4096]{1,0:T(8,128)(2,1)S(1)}, u32[]{:S(2)}, u32[]{:S(2)}) %collective-permute-start.1) | collective-permute-done | bytes 1048608 | tf_op jit(solution)/shard_map/ppermute | solution.py:252
  25.3 2.2 %collective-permute-start.4 = (bf16[128,4096]{1,0:T(8,128)(2,1)S(1)}, bf16[128,4096]{1,0:T(8,128)(2,1)}, u32[]{:S(2)}, u32[]{:S(2)}) collective-permute-start(bf16[128,4096]{1,0:T(8,128)(2,1)S(1)} %collective-permute-done.1.z_mate), channel_id=1, source_target_pairs={{0,1},{1,0},{2,3},{3,2},{4,5},{5,4},{6,7},{7,6},{8,9},{9,8},{10,11... | collective-permute-start | bytes 3145736 | tf_op jit(solution)/shard_map/ppermute | solution.py:255
  27.5 1.2 %collective-permute-start.8 = (bf16[512,768]{1,0:T(8,128)(2,1)}, bf16[512,768]{1,0:T(8,128)(2,1)}, u32[]{:S(2)}, u32[]{:S(2)}) collective-permute-start(bf16[512,768]{1,0:T(8,128)(2,1)} %shard_map.88.refs_1_), channel_id=1, source_target_pairs={{0,8},{1,3},{2,10},{3,5},{4,12},{5,7},{6,14},{7,1},{8,16},{9,11},{... | collective-permute-start | bytes 2359304 | tf_op jit(solution)/shard_map/ppermute | solution.py:48
  28.7 1.5 %collective-permute-start.9 = (bf16[512,768]{1,0:T(8,128)(2,1)}, bf16[512,768]{1,0:T(8,128)(2,1)}, u32[]{:S(2)}, u32[]{:S(2)}) collective-permute-start(bf16[512,768]{1,0:T(8,128)(2,1)} %shard_map.86.refs_0_), channel_id=1, source_target_pairs={{0,24},{1,7},{2,26},{3,1},{4,28},{5,3},{6,30},{7,5},{8,0},{9,15},{... | collective-permute-start | bytes 2359304 | tf_op jit(solution)/shard_map/ppermute | solution.py:48
  30.2 3.1 %collective-permute-done.10.refs_5_ = bf16[512,768]{1,0:T(8,128)(2,1)} collective-permute-done((bf16[512,768]{1,0:T(8,128)(2,1)}, bf16[512,768]{1,0:T(8,128)(2,1)}, u32[]{:S(2)}, u32[]{:S(2)}) %collective-permute-start.10) | collective-permute-done | bytes 786464 | tf_op jit(solution)/shard_map/ppermute | solution.py:48
  33.3 3.4 %collective-permute-start.12 = (bf16[512,768]{1,0:T(8,128)(2,1)}, bf16[512,768]{1,0:T(8,128)(2,1)}, u32[]{:S(2)}, u32[]{:S(2)}) collective-permute-start(bf16[512,768]{1,0:T(8,128)(2,1)} %collective-permute-done.10.refs_5_), channel_id=1, source_target_pairs={{0,24},{1,7},{2,26},{3,1},{4,28},{5,3},{6,30},{7,5},{8,0},{9,15},{... | collective-permute-start | bytes 2359304 | tf_op jit(solution)/shard_map/ppermute | solution.py:48
  36.9 1.0 copy-done.1
  37.9 3.6 %shard_map.87 = (bf16[576,1024]{1,0:T(8,128)(2,1)S(1)}, bf16[576,1024]{1,0:T(8,128)(2,1)S(1)}, bf16[576,1024]{1,0:T(8,128)(2,1)S(1)}, bf16[576,1024]{1,0:T(8,128)(2,1)S(1)}) custom-call(s32[8]{0:T(128)S(1)} %stack.39.place, bf16[128,4096]{1,0:T(8,128)(2,1)S(1)} %copy-done, bf16[128,4096]{1,0:T(8,128)(2,1)S(1)} %collective-permute-done.core_mate, ...), custom_call_target="tpu_custom_call" | custom-call | flops 16777216 | bytes 10485760 | tf_op jit(solution)/shard_map/pallas_call | solution.py:257
  41.8 5.2 %shard_map.89.total = f32[576,768]{1,0:T(8,128)S(1)} custom-call(bf16[576,1024]{1,0:T(8,128)(2,1)S(1)} %get-tuple-element.17.own, bf16[576,1024]{1,0:T(8,128)(2,1)S(1)} %get-tuple-element.18.before, bf16[576,1024]{1,0:T(8,128)(2,1)S(1)} %get-tuple-element.19.after, bf16[512,768]{1,0:T(8,128)(2,1)} %shard_map.86.refs_0_, bf16[512,768]{1,0:T(8,128)(2,1)} %shard_map.88.refs_1_, ...), custom_call_target="tpu_custom_call" | custom-call | flops 3623878656 | bytes 12582912 | tf_op jit(solution)/shard_map/pallas_call | solution.py:261
  47.0 1.6 %collective-permute-done.11.near = bf16[512,768]{1,0:T(8,128)(2,1)} collective-permute-done((bf16[512,768]{1,0:T(8,128)(2,1)}, bf16[512,768]{1,0:T(8,128)(2,1)}, u32[]{:S(2)}, u32[]{:S(2)}) %collective-permute-start.11) | collective-permute-done | bytes 786464 | tf_op jit(solution)/shard_map/ppermute | solution.py:48
  48.6 1.6 %collective-permute-done.12.far = bf16[512,768]{1,0:T(8,128)(2,1)} collective-permute-done((bf16[512,768]{1,0:T(8,128)(2,1)}, bf16[512,768]{1,0:T(8,128)(2,1)}, u32[]{:S(2)}, u32[]{:S(2)}) %collective-permute-start.12) | collective-permute-done | bytes 786464 | tf_op jit(solution)/shard_map/ppermute | solution.py:48
  50.2 4.0 %shard_map.90 = (bf16[576,768]{1,0:T(8,128)(2,1)S(1)}, f32[16,24,256]{2,1,0:T(8,128)S(1)}) custom-call(s32[8]{0:T(128)S(1)} %stack.39.place, s32[256]{0:T(256)S(1)} %copy-done.3, bf16[576,1024]{1,0:T(8,128)(2,1)S(1)} %get-tuple-element.16.across, f32[576,768]{1,0:T(8,128)S(1)} %shard_map.89.total, bf16[512,768]{1,0:T(8,128)(2,1)} %collective-permute-done.11.near, ...), custom_call_target="tpu_custom_call" | custom-call | flops 1207959552 | bytes 6291456 | tf_op jit(solution)/shard_map/pallas_call | solution.py:264
  54.2 14.3 %all_to_all.10.parts = f32[16,24,256]{2,1,0:T(8,128)S(1)} all-to-all(f32[16,24,256]{2,1,0:T(8,128)S(1)} %get-tuple-element.21), channel_id=1, replica_groups=mesh['zg'=4,'zi'=2,'y'=4,'x'=4,'core'=2] {'y','x'}, dimensions={0} | all-to-all | bytes 786432 | tf_op jit(solution)/shard_map/all_to_all | solution.py:268
  68.7 3.0 %collective-permute-start.13 = (f32[24,256]{1,0:T(8,128)S(1)}, f32[24,256]{1,0:T(8,128)S(1)}, u32[]{:S(2)}, u32[]{:S(2)}) collective-permute-start(f32[24,256]{1,0:T(8,128)S(1)} %shard_map.91.own), channel_id=1, source_target_pairs={{0,64},{64,128},{128,192},{192,0},{1,65},{65,129},{129,193},{193,1... | collective-permute-start | bytes 73736 | tf_op jit(solution)/shard_map/ppermute | solution.py:272
  71.7 2.2 %collective-permute-start.14 = (f32[24,256]{1,0:T(8,128)S(1)}, f32[24,256]{1,0:T(8,128)S(1)}, u32[]{:S(2)}, u32[]{:S(2)}) collective-permute-start(f32[24,256]{1,0:T(8,128)S(1)} %shard_map.91.own), channel_id=1, source_target_pairs={{0,192},{64,0},{128,64},{192,128},{1,193},{65,1},{129,65},{193,129... | collective-permute-start | bytes 73736 | tf_op jit(solution)/shard_map/ppermute | solution.py:272
  74.0 4.4 %collective-permute-start.15 = (f32[24,256]{1,0:T(8,128)S(1)}, f32[24,256]{1,0:T(8,128)S(1)}, u32[]{:S(2)}, u32[]{:S(2)}) collective-permute-start(f32[24,256]{1,0:T(8,128)S(1)} %shard_map.91.own), channel_id=1, source_target_pairs={{0,128},{64,192},{128,0},{192,64},{1,129},{65,193},{129,1},{193,65... | collective-permute-start | bytes 73736 | tf_op jit(solution)/shard_map/ppermute | solution.py:272
  78.4 2.2 %collective-permute-done.15.across = f32[24,256]{1,0:T(8,128)S(1)} collective-permute-done((f32[24,256]{1,0:T(8,128)S(1)}, f32[24,256]{1,0:T(8,128)S(1)}, u32[]{:S(2)}, u32[]{:S(2)}) %collective-permute-start.15) | collective-permute-done | bytes 24608 | tf_op jit(solution)/shard_map/ppermute | solution.py:272
  81.3 9.6 %all_to_all.11.shared = bf16[16,32,128]{2,1,0:T(8,128)(2,1)S(1)} all-to-all(bf16[16,32,128]{2,1,0:T(8,128)(2,1)S(1)} %broadcast_in_dim.10), channel_id=1, replica_groups=mesh['zg'=4,'zi'=2,'y'=4,'x'=4,'core'=2] {'y','x'}, dimensions={0} | all-to-all | bytes 262144 | tf_op jit(solution)/shard_map/all_to_all | solution.py:277
  90.9 1.5 %shard_map.93 = (bf16[192,512]{1,0:T(8,128)(2,1)S(1)}, bf16[192,512]{1,0:T(8,128)(2,1)S(1)}, bf16[192,512]{1,0:T(8,128)(2,1)S(1)}, bf16[192,512]{1,0:T(8,128)(2,1)S(1)}) custom-call(s32[8]{0:T(128)S(1)} %stack.39.place, s32[256]{0:T(256)S(1)} %copy-done.3, bf16[576,768]{1,0:T(8,128)(2,1)S(1)} %get-tuple-element.20.proj, ...), custom_call_target="tpu_custom_call" | custom-call | flops 536870912 | bytes 3145728 | tf_op jit(solution)/shard_map/pallas_call | solution.py:280
  93.3 7.5 %collective-permute-start.18 = (bf16[192,512]{1,0:T(8,128)(2,1)S(1)}, bf16[192,512]{1,0:T(8,128)(2,1)S(1)}, u32[]{:S(2)}, u32[]{:S(2)}) collective-permute-start(bf16[192,512]{1,0:T(8,128)(2,1)S(1)} %get-tuple-element.27), channel_id=1, source_target_pairs={{0,33},{1,32},{32,1},{33,0},{2,35},{3,34},{34,3},{35,2},{4,37},{5,... | collective-permute-start | bytes 589832 | tf_op jit(solution)/shard_map/ppermute | solution.py:284
  100.7 5.8 %collective-permute-start.17 = (bf16[192,512]{1,0:T(8,128)(2,1)S(1)}, bf16[192,512]{1,0:T(8,128)(2,1)S(1)}, u32[]{:S(2)}, u32[]{:S(2)}) collective-permute-start(bf16[192,512]{1,0:T(8,128)(2,1)S(1)} %get-tuple-element.25), channel_id=1, source_target_pairs={{0,1},{1,0},{2,3},{3,2},{4,5},{5,4},{6,7},{7,6},{8,9},{9,8},{10,11... | collective-permute-start | bytes 589832 | tf_op jit(solution)/shard_map/ppermute | solution.py:286
  106.5 1.8 %collective-permute-done.18.refs_3_ = bf16[192,512]{1,0:T(8,128)(2,1)S(1)} collective-permute-done((bf16[192,512]{1,0:T(8,128)(2,1)S(1)}, bf16[192,512]{1,0:T(8,128)(2,1)S(1)}, u32[]{:S(2)}, u32[]{:S(2)}) %collective-permute-start.18) | collective-permute-done | bytes 196640 | tf_op jit(solution)/shard_map/ppermute | solution.py:284
  108.3 1.5 %shard_map.94 = (bf16[128,2048]{1,0:T(8,128)(2,1)}, bf16[64,2048]{1,0:T(8,128)(2,1)}) custom-call(s32[8]{0:T(128)S(1)} %stack.39.place, bf16[192,512]{1,0:T(8,128)(2,1)S(1)} %get-tuple-element.22.refs_0_, bf16[192,512]{1,0:T(8,128)(2,1)S(1)} %collective-permute-done.17.refs_1_, bf16[192,512]{1,0:T(8,128)(2,1)S(1)} %collective-permute-done.16.refs_2_, ...), custom_call_target="tpu_custom_call" | custom-call | bytes 2097152 | tf_op jit(solution)/shard_map/pallas_call | solution.py:287
  (31 shorter events, 7.9 us)
Async XLA Ops:
  0.6 5.5 %copy-start = (bf16[128,4096]{1,0:T(8,128)(2,1)S(1)}, bf16[128,4096]{1,0:T(8,128)(2,1)}, u32[]{:S(2)}) copy-start(bf16[128,4096]{1,0:T(8,128)(2,1)} %own.1) | copy-start | bytes 3145732
  0.6 24.7 %collective-permute-start.1 = (bf16[128,4096]{1,0:T(8,128)(2,1)}, bf16[128,4096]{1,0:T(8,128)(2,1)S(1)}, u32[]{:S(2)}, u32[]{:S(2)}) collective-permute-start(bf16[128,4096]{1,0:T(8,128)(2,1)} %own.1), channel_id=1, source_target_pairs={{0,32},{32,0},{1,33},{33,1},{2,34},{34,2},{3,35},{35,3},{4,36},{36... | collective-permute-start | bytes 3145736 | tf_op jit(solution)/shard_map/ppermute | solution.py:252
  5.0 2.1 %collective-permute-start.2 = (bf16[128,768]{1,0:T(8,128)(2,1)S(1)}, bf16[128,768]{1,0:T(8,128)(2,1)S(1)}, u32[]{:S(2)}, u32[]{:S(2)}) collective-permute-start(bf16[128,768]{1,0:T(8,128)(2,1)S(1)} %pad_maximum_fusion.1), channel_id=1, source_target_pairs={{0,1},{1,0},{2,3},{3,2},{4,5},{5,4},{6,7},{7,6},{8,9},{9,8},{10,11... | collective-permute-start | bytes 589832 | tf_op jit(solution)/shard_map/ppermute | solution.py:61
  6.1 22.6 %collective-permute-start = (bf16[128,4096]{1,0:T(8,128)(2,1)S(1)}, bf16[128,4096]{1,0:T(8,128)(2,1)S(1)}, u32[]{:S(2)}, u32[]{:S(2)}) collective-permute-start(bf16[128,4096]{1,0:T(8,128)(2,1)S(1)} %copy-done), channel_id=1, source_target_pairs={{0,1},{1,0},{2,3},{3,2},{4,5},{5,4},{6,7},{7,6},{8,9},{9,8},{10,11... | collective-permute-start | bytes 3145736 | tf_op jit(solution)/shard_map/ppermute | solution.py:253
  7.2 8.2 %collective-permute-start.3 = (bf16[256,768]{1,0:T(8,128)(2,1)S(1)}, bf16[256,768]{1,0:T(8,128)(2,1)S(1)}, u32[]{:S(2)}, u32[]{:S(2)}) collective-permute-start(bf16[256,768]{1,0:T(8,128)(2,1)S(1)} %pad_maximum_fusion.top), channel_id=1, source_target_pairs={{0,2},{1,9},{2,4},{3,11},{4,6},{5,13},{6,0},{7,15},{8,10},{9,17},{... | collective-permute-start | bytes 1179656 | tf_op jit(solution)/shard_map/ppermute | solution.py:48
  8.6 10.5 %collective-permute-start.5 = (bf16[256,768]{1,0:T(8,128)(2,1)S(1)}, bf16[256,768]{1,0:T(8,128)(2,1)S(1)}, u32[]{:S(2)}, u32[]{:S(2)}) collective-permute-start(bf16[256,768]{1,0:T(8,128)(2,1)S(1)} %pad_maximum_fusion.top), channel_id=1, source_target_pairs={{0,6},{1,25},{2,0},{3,27},{4,2},{5,29},{6,4},{7,31},{8,14},{9,1},{... | collective-permute-start | bytes 1179656 | tf_op jit(solution)/shard_map/ppermute | solution.py:48
  10.1 10.8 %collective-permute-start.6 = (bf16[256,768]{1,0:T(8,128)(2,1)S(1)}, bf16[256,768]{1,0:T(8,128)(2,1)S(1)}, u32[]{:S(2)}, u32[]{:S(2)}) collective-permute-start(bf16[256,768]{1,0:T(8,128)(2,1)S(1)} %pad_maximum_fusion.top), channel_id=1, source_target_pairs={{0,4},{1,17},{2,6},{3,19},{4,0},{5,21},{6,2},{7,23},{8,12},{9,25},... | collective-permute-start | bytes 1179656 | tf_op jit(solution)/shard_map/ppermute | solution.py:48
  16.4 20.4 %copy-start.2 = (f32[4096]{0:T(1024)S(1)}, f32[4096]{0:T(1024)}, u32[]{:S(2)}) copy-start(f32[4096]{0:T(1024)} %param.9) | copy-start | bytes 49156
  16.4 13.8 %collective-permute-start.7 = (bf16[512,768]{1,0:T(8,128)(2,1)}, bf16[512,768]{1,0:T(8,128)(2,1)}, u32[]{:S(2)}, u32[]{:S(2)}) collective-permute-start(bf16[512,768]{1,0:T(8,128)(2,1)} %shard_map.86.refs_0_), channel_id=1, source_target_pairs={{0,8},{1,3},{2,10},{3,5},{4,12},{5,7},{6,14},{7,1},{8,16},{9,11},{... | collective-permute-start | bytes 2359304 | tf_op jit(solution)/shard_map/ppermute | solution.py:48
  21.8 11.6 %collective-permute-start.10 = (bf16[512,768]{1,0:T(8,128)(2,1)}, bf16[512,768]{1,0:T(8,128)(2,1)}, u32[]{:S(2)}, u32[]{:S(2)}) collective-permute-start(bf16[512,768]{1,0:T(8,128)(2,1)} %shard_map.88.refs_1_), channel_id=1, source_target_pairs={{0,24},{1,7},{2,26},{3,1},{4,28},{5,3},{6,30},{7,5},{8,0},{9,15},{... | collective-permute-start | bytes 2359304 | tf_op jit(solution)/shard_map/ppermute | solution.py:48
  25.3 11.5 %collective-permute-start.4 = (bf16[128,4096]{1,0:T(8,128)(2,1)S(1)}, bf16[128,4096]{1,0:T(8,128)(2,1)}, u32[]{:S(2)}, u32[]{:S(2)}) collective-permute-start(bf16[128,4096]{1,0:T(8,128)(2,1)S(1)} %collective-permute-done.1.z_mate), channel_id=1, source_target_pairs={{0,1},{1,0},{2,3},{3,2},{4,5},{5,4},{6,7},{7,6},{8,9},{9,8},{10,11... | collective-permute-start | bytes 3145736 | tf_op jit(solution)/shard_map/ppermute | solution.py:255
  27.5 14.0 %collective-permute-start.8 = (bf16[512,768]{1,0:T(8,128)(2,1)}, bf16[512,768]{1,0:T(8,128)(2,1)}, u32[]{:S(2)}, u32[]{:S(2)}) collective-permute-start(bf16[512,768]{1,0:T(8,128)(2,1)} %shard_map.88.refs_1_), channel_id=1, source_target_pairs={{0,8},{1,3},{2,10},{3,5},{4,12},{5,7},{6,14},{7,1},{8,16},{9,11},{... | collective-permute-start | bytes 2359304 | tf_op jit(solution)/shard_map/ppermute | solution.py:48
  28.7 13.0 %collective-permute-start.9 = (bf16[512,768]{1,0:T(8,128)(2,1)}, bf16[512,768]{1,0:T(8,128)(2,1)}, u32[]{:S(2)}, u32[]{:S(2)}) collective-permute-start(bf16[512,768]{1,0:T(8,128)(2,1)} %shard_map.86.refs_0_), channel_id=1, source_target_pairs={{0,24},{1,7},{2,26},{3,1},{4,28},{5,3},{6,30},{7,5},{8,0},{9,15},{... | collective-permute-start | bytes 2359304 | tf_op jit(solution)/shard_map/ppermute | solution.py:48
  30.2 18.4 %collective-permute-start.11 = (bf16[512,768]{1,0:T(8,128)(2,1)}, bf16[512,768]{1,0:T(8,128)(2,1)}, u32[]{:S(2)}, u32[]{:S(2)}) collective-permute-start(bf16[512,768]{1,0:T(8,128)(2,1)} %collective-permute-done.7.refs_2_), channel_id=1, source_target_pairs={{0,8},{1,3},{2,10},{3,5},{4,12},{5,7},{6,14},{7,1},{8,16},{9,11},{... | collective-permute-start | bytes 2359304 | tf_op jit(solution)/shard_map/ppermute | solution.py:48
  33.3 16.9 %collective-permute-start.12 = (bf16[512,768]{1,0:T(8,128)(2,1)}, bf16[512,768]{1,0:T(8,128)(2,1)}, u32[]{:S(2)}, u32[]{:S(2)}) collective-permute-start(bf16[512,768]{1,0:T(8,128)(2,1)} %collective-permute-done.10.refs_5_), channel_id=1, source_target_pairs={{0,24},{1,7},{2,26},{3,1},{4,28},{5,3},{6,30},{7,5},{8,0},{9,15},{... | collective-permute-start | bytes 2359304 | tf_op jit(solution)/shard_map/ppermute | solution.py:48
  36.8 1.0 copy-start.1
  41.8 8.4 %copy-start.3 = (s32[256]{0:T(256)S(1)}, s32[256]{0:T(256)}, u32[]{:S(2)}) copy-start(s32[256]{0:T(256)} %lengths.3) | copy-start | bytes 3076
  68.7 9.7 %collective-permute-start.13 = (f32[24,256]{1,0:T(8,128)S(1)}, f32[24,256]{1,0:T(8,128)S(1)}, u32[]{:S(2)}, u32[]{:S(2)}) collective-permute-start(f32[24,256]{1,0:T(8,128)S(1)} %shard_map.91.own), channel_id=1, source_target_pairs={{0,64},{64,128},{128,192},{192,0},{1,65},{65,129},{129,193},{193,1... | collective-permute-start | bytes 73736 | tf_op jit(solution)/shard_map/ppermute | solution.py:272
  71.7 6.6 %collective-permute-start.14 = (f32[24,256]{1,0:T(8,128)S(1)}, f32[24,256]{1,0:T(8,128)S(1)}, u32[]{:S(2)}, u32[]{:S(2)}) collective-permute-start(f32[24,256]{1,0:T(8,128)S(1)} %shard_map.91.own), channel_id=1, source_target_pairs={{0,192},{64,0},{128,64},{192,128},{1,193},{65,1},{129,65},{193,129... | collective-permute-start | bytes 73736 | tf_op jit(solution)/shard_map/ppermute | solution.py:272
  74.0 6.6 %collective-permute-start.15 = (f32[24,256]{1,0:T(8,128)S(1)}, f32[24,256]{1,0:T(8,128)S(1)}, u32[]{:S(2)}, u32[]{:S(2)}) collective-permute-start(f32[24,256]{1,0:T(8,128)S(1)} %shard_map.91.own), channel_id=1, source_target_pairs={{0,128},{64,192},{128,0},{192,64},{1,129},{65,193},{129,1},{193,65... | collective-permute-start | bytes 73736 | tf_op jit(solution)/shard_map/ppermute | solution.py:272
  92.4 8.4 %collective-permute-start.16 = (bf16[192,512]{1,0:T(8,128)(2,1)S(1)}, bf16[192,512]{1,0:T(8,128)(2,1)S(1)}, u32[]{:S(2)}, u32[]{:S(2)}) collective-permute-start(bf16[192,512]{1,0:T(8,128)(2,1)S(1)} %get-tuple-element.24), channel_id=1, source_target_pairs={{0,32},{32,0},{1,33},{33,1},{2,34},{34,2},{3,35},{35,3},{4,36},{36... | collective-permute-start | bytes 589832 | tf_op jit(solution)/shard_map/ppermute | solution.py:283
  93.3 15.0 %collective-permute-start.18 = (bf16[192,512]{1,0:T(8,128)(2,1)S(1)}, bf16[192,512]{1,0:T(8,128)(2,1)S(1)}, u32[]{:S(2)}, u32[]{:S(2)}) collective-permute-start(bf16[192,512]{1,0:T(8,128)(2,1)S(1)} %get-tuple-element.27), channel_id=1, source_target_pairs={{0,33},{1,32},{32,1},{33,0},{2,35},{3,34},{34,3},{35,2},{4,37},{5,... | collective-permute-start | bytes 589832 | tf_op jit(solution)/shard_map/ppermute | solution.py:284
  100.7 7.6 %collective-permute-start.17 = (bf16[192,512]{1,0:T(8,128)(2,1)S(1)}, bf16[192,512]{1,0:T(8,128)(2,1)S(1)}, u32[]{:S(2)}, u32[]{:S(2)}) collective-permute-start(bf16[192,512]{1,0:T(8,128)(2,1)S(1)} %get-tuple-element.25), channel_id=1, source_target_pairs={{0,1},{1,0},{2,3},{3,2},{4,5},{5,4},{6,7},{7,6},{8,9},{9,8},{10,11... | collective-permute-start | bytes 589832 | tf_op jit(solution)/shard_map/ppermute | solution.py:286
